TPU v7x, 32 devices: a whole 2x2x4 slice. The times are simulated.
32 devices in a mesh: sub: 4 (over y, x), blk: 8 (over z, core).
Axes of the slice: x: 2, y: 2, z: 4, core: 2. Of those that a mesh axis runs over, the one named last changes fastest.
Arguments:
- schur: bfloat16 [4, 8192, 8192], P('sub', 'blk'), as said below
- inverse_blocks: float32 [4, 64, 128, 128], P('sub', 'blk'), as said below
- loads: float32 [4, 32, 8192], P('sub', None, 'blk'), may hold values from -6 to 6
- share_list: int32 [4, 4, 4], P('sub'), may hold values from -1 to 63, as said below
- multiplicity: int32 [4, 64], P('sub', 'blk'), may hold values from 1 to 2, as said below
Outputs:
- solution: float32 [4, 32, 8192], P('sub', None, 'blk')
- misfit: float32 [32, 96], replicated
Inputs may be any that keep to these rules, and one draw needn't show every extreme that they name: share_list[i, j, s] is the local block of subdomain i that holds the s-th block it shares with subdomain j, or -1 for an empty slot; share_list[j, i, s] is the same block in the numbering of j; the used slots of a pair come first and are as many both ways; share_list[i, i, :] is -1; no block of a subdomain appears twice in its list; at most 4 blocks a pair. multiplicity[i, k] is 2 where block k of subdomain i appears in share_list[i], else 1. `schur`: each local Schur complement is a full dense matrix. `inverse_blocks`: full dense blocks.
All inputs are finite; a program needn't handle non-finite values.
Results may differ from a plain program's by a relative error of at most 0.0026.
Values may be sent and summed in bfloat16 or wider, within the bound.
No kernel may reach another device: no remote copies, remote signals or barrier semaphores. Data moves between devices by JAX's collectives and lax.ppermute only.
A program may use at most 64 MiB of HBM per device.

v0:
```python
import jax
import jax.numpy as jnp
from jax import lax
from jax.sharding import PartitionSpec as P

ITERS = 2


FULL_PRECISION = lax.Precision.HIGHEST


def body(schur, inverse_blocks, loads, share_list, multiplicity):
    matrix = schur[0]
    inverse = inverse_blocks[0]
    local_rows = matrix.shape[0]
    order_size = matrix.shape[1]
    block_size = inverse.shape[-1]
    block_count = order_size // block_size
    owned_blocks = inverse.shape[0]
    vectors = loads.shape[1]
    subdomains = lax.axis_size("sub")
    weighting = 1.0 / (order_size * subdomains)
    block_weight = 1.0 / multiplicity[0].astype(jnp.float32)
    row_weight = jnp.repeat(block_weight, block_size)
    slot_blocks = share_list[0].reshape(-1)
    selector = (slot_blocks[:, None] == jnp.arange(block_count, dtype=jnp.int32)[None, :]).astype(
        jnp.float32
    )

    def share(columns):
        count = columns.shape[0]
        blocks = columns.reshape(count, block_count, block_size)
        outgoing = jnp.einsum("mn,knd->mkd", selector, blocks, precision=FULL_PRECISION)
        outgoing = outgoing.reshape(subdomains, -1, count, block_size)
        incoming = lax.all_to_all(outgoing, "sub", split_axis=0, concat_axis=0, tiled=True).reshape(
            -1, count, block_size
        )
        summed = blocks + jnp.einsum("mn,mkd->knd", selector, incoming, precision=FULL_PRECISION)
        return summed.reshape(count, order_size)

    def to_cases(values):
        return share(lax.all_to_all(values, "blk", split_axis=0, concat_axis=1, tiled=True))

    def to_dofs(values):
        return lax.all_to_all(values, "blk", split_axis=1, concat_axis=0, tiled=True)

    def precondition(basis_rows):
        blocks = basis_rows.reshape(vectors, owned_blocks, block_size)
        local = jnp.einsum("kde,pke->pkd", inverse, blocks, precision=FULL_PRECISION)
        local = local * block_weight[None, :, None]
        return to_cases(local.reshape(vectors, local_rows))

    def products(left, right):
        local = lax.dot_general(
            left * row_weight, right, (((1,), (1,)), ((), ())), precision=FULL_PRECISION
        )
        return local * weighting

    def lower_solve(lower, values):
        return jax.scipy.linalg.solve_triangular(lower, values, lower=True)

    right_side = to_dofs(to_cases(loads[0]))
    start_gram = lax.psum(products(right_side, right_side), ("sub", "blk"))
    first = jnp.linalg.cholesky(start_gram)
    basis = [lower_solve(first, right_side)]
    hessen = jnp.zeros((ITERS * vectors, (ITERS + 1) * vectors), jnp.float32)
    for level in range(ITERS):
        rounded = to_dofs(precondition(basis[level])).astype(jnp.bfloat16)
        product = lax.dot_general(
            lax.all_gather(rounded, "blk", axis=1, tiled=True),
            matrix,
            (((1,), (1,)), ((), ())),
            preferred_element_type=jnp.float32,
        )
        image = to_dofs(to_cases(product))
        stacked = jnp.stack(basis)
        local_coef = (
            jnp.einsum("pr,lqr->lpq", image * row_weight, stacked, precision=FULL_PRECISION)
            * weighting
        )
        coefs, whole_gram = lax.psum((local_coef, products(image, image)), ("sub", "blk"))
        image = image - jnp.einsum("lpq,lqr->pr", coefs, stacked, precision=FULL_PRECISION)
        gram = whole_gram - jnp.einsum("lpq,lrq->pr", coefs, coefs, precision=FULL_PRECISION)
        lower = jnp.linalg.cholesky(gram)
        basis.append(lower_solve(lower, image))
        row_slice = slice(level * vectors, (level + 1) * vectors)
        for earlier in range(level + 1):
            hessen = hessen.at[row_slice, earlier * vectors : (earlier + 1) * vectors].set(
                coefs[earlier]
            )
        hessen = hessen.at[row_slice, (level + 1) * vectors : (level + 2) * vectors].set(lower)
    target = jnp.zeros((vectors, (ITERS + 1) * vectors), jnp.float32).at[:, :vectors].set(first)
    normal_matrix = jnp.dot(hessen, hessen.T, precision=FULL_PRECISION)
    right_part = jnp.dot(target, hessen.T, precision=FULL_PRECISION)
    factor = jnp.linalg.cholesky(normal_matrix)
    middle = jax.scipy.linalg.solve_triangular(factor, right_part.T, lower=True)
    coeff_t = jax.scipy.linalg.solve_triangular(factor, middle, lower=True, trans=1)
    combine = coeff_t.T
    misfit = target - jnp.dot(combine, hessen, precision=FULL_PRECISION)
    update = jnp.zeros((vectors, local_rows), jnp.float32)
    for level in range(ITERS):
        update = update + jnp.dot(
            combine[:, level * vectors : (level + 1) * vectors],
            basis[level],
            precision=FULL_PRECISION,
        )
    solution = to_dofs(precondition(update))
    return (solution[None], misfit)


def solution(mesh):
    placed = (
        P("sub", "blk", None),
        P("sub", "blk", None, None),
        P("sub", None, "blk"),
        P("sub", None, None),
        P("sub", "blk"),
    )
    return jax.shard_map(
        body, mesh=mesh, in_specs=placed, out_specs=(P("sub", None, "blk"), P()), check_vma=False
    )
```

profile of v0, /device:TPU:0, one launch (start us, length us, event | category | flops | bytes accessed | tf_op | source)
XLA Modules:
  0.0 392.7 jit_solution(9351103619191016386)
XLA Ops:
  0.7 1.0 all_to_all.160
  1.7 12.9 %all_to_all.219 = f32[8,4,1024]{2,1,0:T(4,128)S(1)} all-to-all(f32[8,4,1024]{2,1,0:T(4,128)S(1)} %all_to_all.160), channel_id=1, replica_groups=mesh['sub'=4,'blk'=8] {'blk'}, dimensions={0} | all-to-all | bytes 262144 | tf_op jit(solution)/shard_map/all_to_all | solution.py:42
  14.7 1.5 fusion.63
  16.2 3.7 all-to-all-start.1
  19.9 0.8 eq.69
  20.7 4.0 %all-to-all-done.1 = f32[4,4,4,128]{3,1,2,0:T(4,128)S(1)} async-done(((f32[4,4,4,128]{3,1,2,0:T(4,128)}), f32[4,4,4,128]{3,1,2,0:T(4,128)S(1)}, u32[]{:S(2)}, u32[]{:S(2)}) %all-to-all-start.1) | async-done | bytes 32800 | tf_op jit(solution)/shard_map/all_to_all | solution.py:35
  25.1 0.7 copy.61
  25.8 3.4 all-to-all-start.2
  29.8 0.7 compare_reduce_fusion.3
  30.6 5.2 %all-to-all-done.2 = f32[4,8,1024]{2,0,1:T(4,128)S(1)} async-done(((f32[4,8,1024]{2,0,1:T(4,128)}), f32[4,8,1024]{2,0,1:T(4,128)S(1)}, u32[]{:S(2)}, u32[]{:S(2)}) %all-to-all-start.2) | async-done | bytes 131104 | tf_op jit(solution)/shard_map/all_to_all | solution.py:45
  36.3 38.7 %psum.35 = f32[32,32]{0,1:T(8,128)S(1)} all-reduce(f32[32,32]{0,1:T(8,128)S(1)} %convolution_multiply_fusion.7), channel_id=1, replica_groups=mesh['sub'=4,'blk'=8] {'sub','blk'}, use_global_device_ids=true, to_apply=%region_0.0 | all-reduce | flops 1024 | bytes 8192 | tf_op jit(solution)/shard_map/psum | solution.py:63
  75.0 2.9 cholesky.94
  78.6 1.3 fusion.51
  80.0 2.4 custom-call.17
  82.8 0.9 fusion.6
  83.8 9.4 %all_to_all.220 = f32[8,4,1024]{2,1,0:T(4,128)S(1)} all-to-all(f32[8,4,1024]{2,1,0:T(4,128)S(1)} %all_to_all.168), channel_id=1, replica_groups=mesh['sub'=4,'blk'=8] {'blk'}, dimensions={0} | all-to-all | bytes 262144 | tf_op jit(solution)/shard_map/all_to_all | solution.py:42
  93.3 1.5 fusion.61
  94.8 3.7 all-to-all-start.4
  98.5 4.7 %all-to-all-done.4 = f32[4,4,4,128]{3,1,2,0:T(4,128)S(1)} async-done(((f32[4,4,4,128]{3,1,2,0:T(4,128)}), f32[4,4,4,128]{3,1,2,0:T(4,128)S(1)}, u32[]{:S(2)}, u32[]{:S(2)}) %all-to-all-start.4) | async-done | bytes 32800 | tf_op jit(solution)/shard_map/all_to_all | solution.py:35
  103.7 8.4 %all_to_all.221 = bf16[4,8,1024]{2,0,1:T(4,128)(2,1)S(1)} all-to-all(bf16[4,8,1024]{2,0,1:T(4,128)(2,1)S(1)} %copy.68), channel_id=1, replica_groups=mesh['sub'=4,'blk'=8] {'blk'}, dimensions={1} | all-to-all | bytes 131072 | tf_op jit(solution)/shard_map/all_to_all | solution.py:45
  112.1 14.8 %all_gather.6 = bf16[32,8192]{1,0:T(8,128)(2,1)S(1)} all-gather(bf16[32,1024]{1,0:T(8,128)(2,1)S(1)} %convert_element_type.30), channel_id=1, replica_groups=mesh['sub'=4,'blk'=8] {'blk'}, dimensions={1}, use_global_device_ids=true | all-gather | bytes 589824 | tf_op jit(solution)/shard_map/all_gather | solution.py:70
  127.2 10.9 %fusion.2 = f32[8,4,1024]{2,1,0:T(4,128)S(1)} fusion(bf16[8,4,8192]{2,1,0:T(4,128)(2,1)S(1)} %dot_general.100, bf16[1,1024,8192]{2,1,0:T(8,128)(2,1)} %param.20), kind=kOutput, calls=%fused_computation.2 | convolution fusion | flops 536870912 | bytes 17432576 | tf_op jit(solution)/shard_map/dot_general | solution.py:69
  138.1 9.1 %all_to_all.222 = f32[8,4,1024]{2,1,0:T(4,128)S(1)} all-to-all(f32[8,4,1024]{2,1,0:T(4,128)S(1)} %fusion.2), channel_id=1, replica_groups=mesh['sub'=4,'blk'=8] {'blk'}, dimensions={0} | all-to-all | bytes 262144 | tf_op jit(solution)/shard_map/all_to_all | solution.py:42
  147.4 0.8 fusion.59
  148.2 3.3 all-to-all-start.7
  151.5 4.7 %all-to-all-done.7 = f32[4,4,4,128]{3,1,2,0:T(4,128)S(1)} async-done(((f32[4,4,4,128]{3,1,2,0:T(4,128)}), f32[4,4,4,128]{3,1,2,0:T(4,128)S(1)}, u32[]{:S(2)}, u32[]{:S(2)}) %all-to-all-start.7) | async-done | bytes 32800 | tf_op jit(solution)/shard_map/all_to_all | solution.py:35
  156.6 0.7 copy.71
  157.3 3.4 all-to-all-start.8
  162.1 5.3 %all-to-all-done.8 = f32[4,8,1024]{2,0,1:T(4,128)S(1)} async-done(((f32[4,8,1024]{2,0,1:T(4,128)}), f32[4,8,1024]{2,0,1:T(4,128)S(1)}, u32[]{:S(2)}, u32[]{:S(2)}) %all-to-all-start.8) | async-done | bytes 131104 | tf_op jit(solution)/shard_map/all_to_all | solution.py:45
  168.0 39.0 %all-reduce.3 = (f32[32,32]{1,0:T(8,128)S(1)}, f32[32,32]{0,1:T(8,128)S(1)}) all-reduce(f32[32,32]{1,0:T(8,128)S(1)} %fusion.15, f32[32,32]{0,1:T(8,128)S(1)} %convolution_multiply_fusion.5), channel_id=1, replica_groups=mesh['sub'=4,'blk'=8] {'sub','blk'}, use_global_device_ids=true, to_apply=%region_3.0 | all-reduce | flops 2048 | bytes 16384 | tf_op jit(solution)/shard_map/psum | solution.py:81
  207.6 2.9 cholesky.105
  211.2 2.6 select_bitcast_fusion
  213.8 2.4 custom-call.18
  216.6 0.9 fusion.5
  217.6 9.4 %all_to_all.223 = f32[8,4,1024]{2,1,0:T(4,128)S(1)} all-to-all(f32[8,4,1024]{2,1,0:T(4,128)S(1)} %all_to_all.181), channel_id=1, replica_groups=mesh['sub'=4,'blk'=8] {'blk'}, dimensions={0} | all-to-all | bytes 262144 | tf_op jit(solution)/shard_map/all_to_all | solution.py:42
  227.1 0.8 fusion.57
  228.0 3.6 all-to-all-start.10
  231.6 4.7 %all-to-all-done.10 = f32[4,4,4,128]{3,1,2,0:T(4,128)S(1)} async-done(((f32[4,4,4,128]{3,1,2,0:T(4,128)}), f32[4,4,4,128]{3,1,2,0:T(4,128)S(1)}, u32[]{:S(2)}, u32[]{:S(2)}) %all-to-all-start.10) | async-done | bytes 32800 | tf_op jit(solution)/shard_map/all_to_all | solution.py:35
  236.8 8.4 %all_to_all.224 = bf16[4,8,1024]{2,0,1:T(4,128)(2,1)S(1)} all-to-all(bf16[4,8,1024]{2,0,1:T(4,128)(2,1)S(1)} %copy.80), channel_id=1, replica_groups=mesh['sub'=4,'blk'=8] {'blk'}, dimensions={1} | all-to-all | bytes 131072 | tf_op jit(solution)/shard_map/all_to_all | solution.py:45
  245.3 14.8 %all_gather.7 = bf16[32,8192]{1,0:T(8,128)(2,1)S(1)} all-gather(bf16[32,1024]{1,0:T(8,128)(2,1)S(1)} %convert_element_type.33), channel_id=1, replica_groups=mesh['sub'=4,'blk'=8] {'blk'}, dimensions={1}, use_global_device_ids=true | all-gather | bytes 589824 | tf_op jit(solution)/shard_map/all_gather | solution.py:70
  260.3 10.9 %fusion = f32[8,4,1024]{2,1,0:T(4,128)S(1)} fusion(bf16[8,4,8192]{2,1,0:T(4,128)(2,1)S(1)} %dot_general.111, bf16[1,1024,8192]{2,1,0:T(8,128)(2,1)} %param.20), kind=kOutput, calls=%fused_computation | convolution fusion | flops 536870912 | bytes 17432576 | tf_op jit(solution)/shard_map/dot_general | solution.py:69
  271.2 9.1 %all_to_all.225 = f32[8,4,1024]{2,1,0:T(4,128)S(1)} all-to-all(f32[8,4,1024]{2,1,0:T(4,128)S(1)} %fusion), channel_id=1, replica_groups=mesh['sub'=4,'blk'=8] {'blk'}, dimensions={0} | all-to-all | bytes 262144 | tf_op jit(solution)/shard_map/all_to_all | solution.py:42
  280.5 0.8 fusion.55
  281.3 3.3 all-to-all-start.13
  284.6 4.7 %all-to-all-done.13 = f32[4,4,4,128]{3,1,2,0:T(4,128)S(1)} async-done(((f32[4,4,4,128]{3,1,2,0:T(4,128)}), f32[4,4,4,128]{3,1,2,0:T(4,128)S(1)}, u32[]{:S(2)}, u32[]{:S(2)}) %all-to-all-start.13) | async-done | bytes 32800 | tf_op jit(solution)/shard_map/all_to_all | solution.py:35
  289.7 0.7 copy.83
  290.4 3.4 all-to-all-start.14
  293.8 2.2 scatter.21
  296.0 4.5 %all-to-all-done.14 = f32[4,8,1024]{2,0,1:T(4,128)S(1)} async-done(((f32[4,8,1024]{2,0,1:T(4,128)}), f32[4,8,1024]{2,0,1:T(4,128)S(1)}, u32[]{:S(2)}, u32[]{:S(2)}) %all-to-all-start.14) | async-done | bytes 131104 | tf_op jit(solution)/shard_map/all_to_all | solution.py:45
  301.6 39.2 %all-reduce.2 = (f32[2,32,32]{2,1,0:T(8,128)S(1)}, f32[32,32]{0,1:T(8,128)S(1)}) all-reduce(f32[2,32,32]{2,1,0:T(8,128)S(1)} %fusion.14, f32[32,32]{0,1:T(8,128)S(1)} %convolution_multiply_fusion.4), channel_id=1, replica_groups=mesh['sub'=4,'blk'=8] {'sub','blk'}, use_global_device_ids=true, to_apply=%region_6.0 | all-reduce | flops 3072 | bytes 24576 | tf_op jit(solution)/shard_map/psum | solution.py:81
  341.1 2.9 cholesky.116
  345.9 0.8 scatter.25
  346.7 0.8 scatter.26
  348.0 5.8 %cholesky.41 = f32[64,64]{1,0:T(8,128)S(1)} custom-call(f32[64,64]{1,0:T(8,128)S(1)} %fusion.37), custom_call_target="Cholesky" | custom-call | tf_op jit(solution)/shard_map/jit(cholesky)/cholesky | solution.py:95
  355.2 4.9 %custom-call.15 = f32[1,64,64]{1,2,0:T(8,128)S(1)} custom-call(f32[1,64,64]{2,1,0:T(8,128)S(1)} %fusion.32), custom_call_target="InvertDiagBlocksLowerTriangular" | custom-call | tf_op jit(solution)/shard_map/jit(_solve_triangular)/triangular_solve | solution.py:97
  361.0 0.9 fusion.4
  362.1 9.4 %all_to_all.226 = f32[8,4,1024]{2,1,0:T(4,128)S(1)} all-to-all(f32[8,4,1024]{2,1,0:T(4,128)S(1)} %all_to_all.194), channel_id=1, replica_groups=mesh['sub'=4,'blk'=8] {'blk'}, dimensions={0} | all-to-all | bytes 262144 | tf_op jit(solution)/shard_map/all_to_all | solution.py:42
  371.6 0.8 fusion.53
  372.4 3.6 all-to-all-start.16
  376.1 4.7 %all-to-all-done.16 = f32[4,4,4,128]{3,1,2,0:T(4,128)S(1)} async-done(((f32[4,4,4,128]{3,1,2,0:T(4,128)}), f32[4,4,4,128]{3,1,2,0:T(4,128)S(1)}, u32[]{:S(2)}, u32[]{:S(2)}) %all-to-all-start.16) | async-done | bytes 32800 | tf_op jit(solution)/shard_map/all_to_all | solution.py:35
  381.2 0.7 copy.93
  381.9 3.4 all-to-all-start.17
  385.3 0.8 convolution_subtract_fusion.1
  386.1 5.9 %all-to-all-done.17 = f32[4,8,1024]{2,0,1:T(4,128)S(1)} async-done(((f32[4,8,1024]{2,0,1:T(4,128)}), f32[4,8,1024]{2,0,1:T(4,128)S(1)}, u32[]{:S(2)}, u32[]{:S(2)}) %all-to-all-start.17) | async-done | bytes 131104 | tf_op jit(solution)/shard_map/all_to_all | solution.py:45
  (106 shorter events, 16.1 us)
Async XLA Ops:
  0.6 82.1 %copy-start = (f32[1,8,128,128]{3,2,1,0:T(8,128)S(1)}, f32[1,8,128,128]{3,2,1,0:T(8,128)}, u32[]{:S(2)}) copy-start(f32[1,8,128,128]{3,2,1,0:T(8,128)} %param.21) | copy-start | bytes 1572868
  0.6 146.7 %copy-start.1 = (s32[1,4,4]{2,1,0:T(4,128)S(1)}, s32[1,4,4]{2,1,0:T(4,128)}, u32[]{:S(2)}) copy-start(s32[1,4,4]{2,1,0:T(4,128)} %param.23) | copy-start | bytes 196
  14.7 146.7 %copy-start.2 = (s32[2]{0:T(128)S(1)}, s32[2]{0:T(128)}, u32[]{:S(2)}) copy-start(s32[2]{0:T(128)} %constant.236.clone.1) | copy-start | bytes 28
  16.2 8.5 %all-to-all-start.1 = ((f32[4,4,4,128]{3,1,2,0:T(4,128)}), f32[4,4,4,128]{3,1,2,0:T(4,128)S(1)}, u32[]{:S(2)}, u32[]{:S(2)}) async-start(f32[4,4,4,128]{3,1,2,0:T(4,128)} %fusion.63), calls=%async_computation.1 | async-start | bytes 65536 | tf_op jit(solution)/shard_map/all_to_all | solution.py:35
  25.8 10.1 %all-to-all-start.2 = ((f32[4,8,1024]{2,0,1:T(4,128)}), f32[4,8,1024]{2,0,1:T(4,128)S(1)}, u32[]{:S(2)}, u32[]{:S(2)}) async-start(f32[4,8,1024]{2,0,1:T(4,128)} %copy.61), calls=%async_computation.2 | async-start | bytes 262144 | tf_op jit(solution)/shard_map/all_to_all | solution.py:45
  94.8 8.4 %all-to-all-start.4 = ((f32[4,4,4,128]{3,1,2,0:T(4,128)}), f32[4,4,4,128]{3,1,2,0:T(4,128)S(1)}, u32[]{:S(2)}, u32[]{:S(2)}) async-start(f32[4,4,4,128]{3,1,2,0:T(4,128)} %fusion.61), calls=%async_computation.4 | async-start | bytes 65536 | tf_op jit(solution)/shard_map/all_to_all | solution.py:35
  148.2 8.0 %all-to-all-start.7 = ((f32[4,4,4,128]{3,1,2,0:T(4,128)}), f32[4,4,4,128]{3,1,2,0:T(4,128)S(1)}, u32[]{:S(2)}, u32[]{:S(2)}) async-start(f32[4,4,4,128]{3,1,2,0:T(4,128)} %fusion.59), calls=%async_computation.7 | async-start | bytes 65536 | tf_op jit(solution)/shard_map/all_to_all | solution.py:35
  157.3 10.1 %all-to-all-start.8 = ((f32[4,8,1024]{2,0,1:T(4,128)}), f32[4,8,1024]{2,0,1:T(4,128)S(1)}, u32[]{:S(2)}, u32[]{:S(2)}) async-start(f32[4,8,1024]{2,0,1:T(4,128)} %copy.71), calls=%async_computation.8 | async-start | bytes 262144 | tf_op jit(solution)/shard_map/all_to_all | solution.py:45
  228.0 8.4 %all-to-all-start.10 = ((f32[4,4,4,128]{3,1,2,0:T(4,128)}), f32[4,4,4,128]{3,1,2,0:T(4,128)S(1)}, u32[]{:S(2)}, u32[]{:S(2)}) async-start(f32[4,4,4,128]{3,1,2,0:T(4,128)} %fusion.57), calls=%async_computation.10 | async-start | bytes 65536 | tf_op jit(solution)/shard_map/all_to_all | solution.py:35
  281.3 8.0 %all-to-all-start.13 = ((f32[4,4,4,128]{3,1,2,0:T(4,128)}), f32[4,4,4,128]{3,1,2,0:T(4,128)S(1)}, u32[]{:S(2)}, u32[]{:S(2)}) async-start(f32[4,4,4,128]{3,1,2,0:T(4,128)} %fusion.55), calls=%async_computation.13 | async-start | bytes 65536 | tf_op jit(solution)/shard_map/all_to_all | solution.py:35
  290.4 10.1 %all-to-all-start.14 = ((f32[4,8,1024]{2,0,1:T(4,128)}), f32[4,8,1024]{2,0,1:T(4,128)S(1)}, u32[]{:S(2)}, u32[]{:S(2)}) async-start(f32[4,8,1024]{2,0,1:T(4,128)} %copy.83), calls=%async_computation.14 | async-start | bytes 262144 | tf_op jit(solution)/shard_map/all_to_all | solution.py:45
  372.4 8.4 %all-to-all-start.16 = ((f32[4,4,4,128]{3,1,2,0:T(4,128)}), f32[4,4,4,128]{3,1,2,0:T(4,128)S(1)}, u32[]{:S(2)}, u32[]{:S(2)}) async-start(f32[4,4,4,128]{3,1,2,0:T(4,128)} %fusion.53), calls=%async_computation.16 | async-start | bytes 65536 | tf_op jit(solution)/shard_map/all_to_all | solution.py:35
  381.9 10.1 %all-to-all-start.17 = ((f32[4,8,1024]{2,0,1:T(4,128)}), f32[4,8,1024]{2,0,1:T(4,128)S(1)}, u32[]{:S(2)}, u32[]{:S(2)}) async-start(f32[4,8,1024]{2,0,1:T(4,128)} %copy.93), calls=%async_computation.17 | async-start | bytes 262144 | tf_op jit(solution)/shard_map/all_to_all | solution.py:45
where the time goes:
time: 395 us; the launch traced here: 393 us
  blocking collectives  223 us (56%)
  waiting for transfers between devices  48.5 us (12%)
  matrix products  37.9 us (10%)
  starting transfers between devices  34.7 us (9%)
  other arithmetic  34.5 us (9%)
  local copies, waits for them, and re-layouts  13.1 us (3%)
    psum x2, blocking collectives, body(): lax.psum((local_coef, products(image, image)), ('sub', 'blk'))  78.2 us
    all_to_all x6, blocking collectives, to_cases(): lax.all_to_all(values, 'blk', split_axis=0, concat_axis=1, tiled=True)  59.3 us
    psum x1, blocking collectives, body(): start_gram = lax.psum(products(right_side, right_side), ('sub', 'blk'))  38.7 us
    all_gather x2, blocking collectives, body(): lax.all_gather(rounded, 'blk', axis=1, tiled=True)  29.7 us
    all_to_all x6, waiting for transfers between devices, share(): lax.all_to_all(outgoing, 'sub', split_axis=0, concat_axis=0, tiled=True)  27.5 us
    dot_general x2, matrix products, body(): lax.dot_general(lax.all_gather(rounded, 'blk', axis=1, tiled=True), matri...  21.8 us
    all_to_all x6, starting transfers between devices, share(): lax.all_to_all(outgoing, 'sub', split_axis=0, concat_axis=0, tiled=True)  21.2 us
    all_to_all x4, waiting for transfers between devices, to_dofs(): lax.all_to_all(values, 'blk', split_axis=1, concat_axis=0, tiled=True)  21 us
  transfers between devices with their start and end apart: 10, of which 10 were waited for; matrix products, arithmetic and copies ran while one was open for 2% of the time, Pallas kernels for 0%

commit v1 on v0

v1 whole, which is shorter than its diff:
```python
import functools

import jax
import jax.numpy as jnp
from jax import lax
from jax.experimental import pallas as pl
from jax.experimental.pallas import tpu as pltpu
from jax.sharding import PartitionSpec as P

F32 = jnp.float32
BF16 = jnp.bfloat16
HIGH = lax.Precision.HIGHEST
VM = pl.BlockSpec(memory_space=pltpu.VMEM)
SM = pl.BlockSpec(memory_space=pltpu.SMEM)


def nn(a, b):
    return lax.dot_general(a, b, (((1,), (0,)), ((), ())), precision=HIGH, preferred_element_type=F32)


def nt(a, b):
    return lax.dot_general(a, b, (((1,), (1,)), ((), ())), precision=HIGH, preferred_element_type=F32)


def nt16(a, b):
    return lax.dot_general(a, b, (((1,), (1,)), ((), ())), preferred_element_type=F32)


def pair_sum(values):
    while len(values) > 1:
        values = [values[i] + values[i + 1] for i in range(0, len(values), 2)]
    return values[0]


def factor(mats):
    size = mats[0].shape[0]
    rows = lax.broadcasted_iota(jnp.int32, (size, size), 0)
    cols = lax.broadcasted_iota(jnp.int32, (size, size), 1)
    eye = (rows == cols).astype(F32)
    work = [jnp.concatenate([m, eye], axis=1) for m in mats]
    kept = [[] for _ in mats]
    for j in range(size):
        for n in range(len(mats)):
            m = work[n]
            row = m[j : j + 1, :] * lax.rsqrt(m[j : j + 1, j : j + 1])
            col = m[:, j : j + 1] * lax.rsqrt(m[j : j + 1, j : j + 1])
            kept[n].append(row)
            work[n] = m - col * row
    out = []
    for n in range(len(mats)):
        full = jnp.concatenate(kept[n], axis=0)
        out.append((jnp.where(cols >= rows, full[:, :size], 0.0), full[:, size:]))
    return out


def call(kernel, outs, args, specs, scratch=(), vmem=16, name=None):
    return pl.pallas_call(
        kernel,
        out_shape=outs,
        in_specs=specs,
        out_specs=jax.tree.map(lambda _: VM, outs),
        scratch_shapes=list(scratch),
        compiler_params=pltpu.CompilerParams(vmem_limit_bytes=vmem << 20),
        name=name,
    )(*args)


def xor(size, m):
    return [(i, i ^ m) for i in range(size)]


def body(schur, inverse_blocks, loads, share_list, multiplicity):
    matrix = schur[0]
    inverse = inverse_blocks[0]
    local_rows, order = matrix.shape
    owned, block = inverse.shape[0], inverse.shape[-1]
    cases = loads.shape[1]
    share = share_list[0]
    subs, slots = share.shape
    parts = lax.axis_size("blk")
    weighting = 1.0 / (order * subs)
    weight = 1.0 / multiplicity[0].astype(F32)
    peers = list(range(1, subs))
    cube = (owned, cases, block)

    def sds(shape, dtype=F32):
        return jax.ShapeDtypeStruct(shape, dtype)

    def permute(v, axis, m):
        return lax.ppermute(v, axis, xor(lax.axis_size(axis), m))

    def gather(v):
        same = [v] + [permute(v, "blk", 2 * m) for m in range(1, parts // 2)]
        both = []
        for piece in same:
            both += [piece, permute(piece, "blk", 1)]
        return jnp.concatenate(both, axis=0)

    def sum_blk(v):
        total = pair_sum([v] + [permute(v, "blk", 2 * m) for m in range(1, parts // 2)])
        return total + permute(total, "blk", 1)

    def to_subs(vs):
        return [permute(v, "sub", m) for m, v in zip(peers, vs)]

    def place(k, me):
        return ((k // owned) ^ me) * owned + k % owned

    def select(pieces):
        dtype = pieces.dtype

        def kernel(share_ref, p_ref, *outs):
            me, mine = lax.axis_index("blk"), lax.axis_index("sub")
            for m, o in zip(peers, outs):
                for s in range(slots):
                    k = share_ref[mine ^ m, s]
                    value = p_ref[place(jnp.maximum(k, 0), me)]
                    o[s] = jnp.where(k >= 0, value, jnp.zeros_like(value))

        outs = tuple(sds((slots, cases, block), dtype) for _ in peers)
        return call(kernel, outs, (share, pieces), [SM, VM], name="select")

    def select_all(pieces):
        dtype = pieces.dtype

        def kernel(share_ref, p_ref, o_ref):
            me = lax.axis_index("blk")
            for j in range(subs):
                for s in range(slots):
                    k = share_ref[j, s]
                    value = p_ref[place(jnp.maximum(k, 0), me)]
                    o_ref[j * slots + s] = jnp.where(k >= 0, value, jnp.zeros_like(value))

        return call(kernel, sds((subs * slots, cases, block), dtype), (share, pieces), [SM, VM], name="select_all")

    def add_shared(share_ref, acc_ref, arrived):
        me, mine = lax.axis_index("blk"), lax.axis_index("sub")
        for m, a_ref in zip(peers, arrived):
            for s in range(slots):
                k = share_ref[mine ^ m, s]

                @pl.when(jnp.logical_and(k >= 0, k // owned == me))
                def _():
                    acc_ref[k % owned] += a_ref[s].astype(F32)

    n_in = len(peers)

    def begin(raw):
        def kernel(l_ref, b_ref, g_ref):
            value = l_ref[...]
            for k in range(owned):
                b_ref[k] = value[:, k * block : (k + 1) * block]
            g_ref[...] = nt(value, value) * weighting

        return call(kernel, (sds(cube), sds((cases, cases))), (raw,), [VM], name="begin")

    def start(own, arrived, grams):
        def kernel(share_ref, w_ref, own_ref, inv_ref, g_ref, *rest):
            ins, outs = rest[:n_in], rest[n_in:]
            b_ref, x_ref, h_ref, f_ref = outs
            ((up, inv_low),) = factor([g_ref[...]])
            f_ref[...] = up
            b_ref[...] = own_ref[...]
            add_shared(share_ref, b_ref, ins)
            for k in range(owned):
                value = nn(inv_low, b_ref[k])
                b_ref[k] = value
                value = nt(value, inv_ref[k]) * w_ref[k]
                x_ref[k] = value
                h_ref[k] = value.astype(BF16)

        outs = (sds(cube), sds(cube), sds(cube, BF16), sds((cases, cases)))
        return call(kernel, outs, (share, weight, own, inverse, grams, *arrived), [SM, SM] + [VM] * (3 + n_in), name="start")

    def middle(own, arrived):
        def kernel(share_ref, w_ref, own_ref, inv_ref, *rest):
            ins, outs = rest[:n_in], rest[n_in:]
            k_ref, x_ref, h_ref = outs
            k_ref[...] = own_ref[...]
            add_shared(share_ref, k_ref, ins)
            for k in range(owned):
                value = nt(k_ref[k], inv_ref[k]) * w_ref[k]
                x_ref[k] = value
                h_ref[k] = value.astype(BF16)

        outs = (sds(cube), sds(cube), sds(cube, BF16))
        return call(kernel, outs, (share, weight, own, inverse, *arrived), [SM, SM] + [VM] * (2 + n_in), name="middle")

    def multiply(pieces):
        def kernel(m_ref, p_ref, y_ref):
            me = lax.axis_index("blk")
            total = jnp.zeros((cases, local_rows), F32)
            for q in range(parts):
                z = jnp.concatenate([p_ref[q * owned + i] for i in range(owned)], axis=1)
                at = pl.multiple_of((q ^ me) * local_rows, local_rows)
                total = total + nt16(z, m_ref[:, pl.ds(at, local_rows)])
            y_ref[...] = total

        return call(kernel, sds((cases, local_rows)), (matrix, pieces), [VM, VM], vmem=6, name="multiply")

    def multiply_shared(part, arrived):
        def kernel(share_ref, m_ref, part_ref, *rest):
            ins, (y_ref, h_ref) = rest[:n_in], rest[n_in:]
            mine = lax.axis_index("sub")
            total = part_ref[...]
            for m, a_ref in zip(peers, ins):
                z = jnp.concatenate([a_ref[s] for s in range(slots)], axis=1)
                cols = []
                for s in range(slots):
                    at = pl.multiple_of(jnp.maximum(share_ref[mine ^ m, s], 0) * block, block)
                    cols.append(m_ref[:, pl.ds(at, block)])
                total = total + nt16(z, jnp.concatenate(cols, axis=1))
            for k in range(owned):
                value = total[:, k * block : (k + 1) * block]
                y_ref[k] = value
                h_ref[k] = value.astype(BF16)

        outs = (sds(cube), sds(cube, BF16))
        return call(
            kernel, outs, (share, matrix, part, *arrived), [SM] + [VM] * (2 + n_in), vmem=6, name="multiply_shared"
        )

    def apply(half):
        pieces = gather(half)
        arrived = to_subs(select(pieces))
        image, image_half = multiply_shared(multiply(pieces), arrived)
        return arrived, image, image_half

    def inner(b, k1, y1):
        def kernel(w_ref, b_ref, k_ref, y_ref, g_ref):
            wide = lambda ref: jnp.concatenate([ref[k] for k in range(owned)], axis=1)
            weighted = lambda ref: jnp.concatenate([ref[k] * w_ref[k] for k in range(owned)], axis=1)
            bb, kk, yy = wide(b_ref), wide(k_ref), wide(y_ref)
            left = jnp.concatenate([weighted(b_ref), weighted(k_ref), yy], axis=0)
            right = jnp.concatenate([bb, kk, yy], axis=0)
            g_ref[...] = nt(left, right) * weighting

        return call(kernel, sds((3 * cases, 3 * cases)), (weight, b, k1, y1), [SM] + [VM] * 3, name="inner")

    def finish(gram, mine_slots, their_slots, upper, x0, in0, x1, in1):
        def kernel(share_ref, g_ref, s_ref, f_ref, x0_ref, x1_ref, *rest):
            theirs, in0_refs, in1_refs = rest[:n_in], rest[n_in : 2 * n_in], rest[2 * n_in : 3 * n_in]
            sol_ref, mis_ref, all_ref, z0_ref, z1_ref = rest[3 * n_in :]
            mine = lax.axis_index("sub")
            z0_ref[...] = x0_ref[...]
            add_shared(share_ref, z0_ref, in0_refs)
            z1_ref[...] = x1_ref[...]
            add_shared(share_ref, z1_ref, in1_refs)
            all_ref[mine] = s_ref[...]
            for m, t_ref in zip(peers, theirs):
                all_ref[mine ^ m] = t_ref[...]
            cross = jnp.zeros((cases, cases), F32)
            for i in range(subs):
                for j in range(i + 1, subs):
                    left = jnp.concatenate([all_ref[i, j * slots + s] for s in range(slots)], axis=1)
                    right = jnp.concatenate([all_ref[j, i * slots + s] for s in range(slots)], axis=1)
                    cross = cross + nt16(left, right) + nt16(right, left)
            n = cases
            g = lambda r, c: g_ref[r * n : (r + 1) * n, c * n : (c + 1) * n]
            g00, g10, g11, g20, g21 = g(0, 0), g(1, 0), g(1, 1), g(2, 0), g(2, 1)
            g22 = g(2, 2) + cross * weighting
            (u00, i00), (_, j1) = factor([g00, g11])
            l10 = nt(g10, i00)
            l20 = nt(g20, i00)
            k21 = nt(g21, j1)
            ((u11, i11),) = factor([g11 - nt(l10, l10)])
            l21 = nt(g21 - nt(l20, l10), i11)
            (u22, _), (_, j2) = factor([g22 - nt(l20, l20) - nt(l21, l21), g22 - nt(k21, k21)])
            tn = lambda a, b: lax.dot_general(a, b, (((0,), (1,)), ((), ())), precision=HIGH, preferred_element_type=F32)
            r1 = tn(g10, j1)
            r2 = nt(tn(g20, jnp.eye(n, dtype=F32)) - nt(r1, k21), j2)
            c1 = nn(r2, j2)
            c0 = nn(r1 - nn(c1, k21), j1)
            up = f_ref[...]
            down = lambda v: lax.dot_general(up, v, (((0,), (0,)), ((), ())), precision=HIGH, preferred_element_type=F32)
            tt = lambda u: u.T
            m0 = tt(u00) - nn(c0, l10) - nn(c1, l20)
            m1 = -nt(c0, u11) - nn(c1, l21)
            m2 = -nt(c1, u22)
            mis_ref[...] = down(jnp.concatenate([m0, m1, m2], axis=1))
            c0, c1 = down(c0), down(c1)
            for k in range(owned):
                sol_ref[:, k * block : (k + 1) * block] = nn(c0, z0_ref[k]) + nn(c1, z1_ref[k])

        outs = (sds((cases, local_rows)), sds((cases, 3 * cases)))
        return call(
            kernel,
            outs,
            (share, gram, mine_slots, upper, x0, x1, *their_slots, *in0, *in1),
            [SM] + [VM] * (5 + 3 * n_in),
            scratch=[pltpu.VMEM((subs, subs * slots, cases, block), BF16), pltpu.VMEM(cube, F32), pltpu.VMEM(cube, F32)],
            name="finish",
        )

    own, gram0 = begin(loads[0])
    gram0 = sum_blk(gram0)
    gram0 = pair_sum([gram0] + [permute(gram0, "sub", m) for m in peers])
    b, x0, half, upper = start(own, to_subs(select(gather(own))), gram0)
    in0, y0, half = apply(half)
    k1, x1, half = middle(y0, to_subs(select(gather(half))))
    in1, y1, half = apply(half)
    gram = sum_blk(inner(b, k1, y1))
    gram = pair_sum([gram] + [permute(gram, "sub", m) for m in peers])
    mine_slots = select_all(gather(half))
    solution, misfit = finish(
        gram, mine_slots, to_subs([mine_slots] * n_in), upper, x0, in0, x1, in1
    )
    return (solution[None], misfit)


def solution(mesh):
    placed = (
        P("sub", "blk", None),
        P("sub", "blk", None, None),
        P("sub", None, "blk"),
        P("sub", None, None),
        P("sub", "blk"),
    )
    return jax.shard_map(
        body, mesh=mesh, in_specs=placed, out_specs=(P("sub", None, "blk"), P()), check_vma=False
    )
```

time: 395 us -> 153 us (0.39)
  blocking collectives: 223 us -> 0 us
  matrix products: 37.9 us -> 0 us
  Pallas kernels: 0 us -> 36.4 us
  other arithmetic: 34.5 us -> 0.71 us
  starting transfers between devices: 34.7 us -> 62.9 us
  waiting for transfers between devices: 48.5 us -> 41.6 us
    psum x3 -> x0, blocking collectives: 117 us -> none  [the longest x2 78.2 us: body(): lax.psum((local_coef, products(image, image)), ('sub', 'blk'))]
    all_to_all x8 -> x0, blocking collectives: 76.2 us -> none  [the longest x6 59.3 us: to_cases(): lax.all_to_all(values, 'blk', split_axis=0, concat_axis=1, tiled=True)]
    ppermute x0 -> x64, starting transfers between devices: none -> 62.9 us  [permute(): return lax.ppermute(v, axis, xor(lax.axis_size(axis), m))]
    all_to_all x10 -> x0, waiting for transfers between devices: 48.5 us -> none  [the longest x6 27.5 us: share(): lax.all_to_all(outgoing, 'sub', split_axis=0, concat_axis=0, tiled=True)]
    ppermute x0 -> x64, waiting for transfers between devices: none -> 41.6 us  [permute(): return lax.ppermute(v, axis, xor(lax.axis_size(axis), m))]
    dot_general x30 -> x0, matrix products: 36.9 us -> none  [the longest x2 21.8 us: body(): lax.dot_general(lax.all_gather(rounded, 'blk', axis=1, tiled=True), matri...]
    pallas_call x0 -> x14, Pallas kernels: none -> 36.4 us  [call(): pl.pallas_call(kernel, out_shape=outs, in_specs=specs, out_specs=jax.tree...]
    all_to_all x10 -> x0, starting transfers between devices: 34.7 us -> none  [the longest x6 21.2 us: share(): lax.all_to_all(outgoing, 'sub', split_axis=0, concat_axis=0, tiled=True)]
  transfers between devices with their start and end apart: 10 -> 64, of which waited for: 10 -> 27; matrix products, arithmetic and copies ran while one was open for 2% -> 1% of each run, Pallas kernels for 0% -> 7%
where the time goes in v1:
time: 153 us; the launch traced here: 152 us
  starting transfers between devices  62.9 us (41%)
  waiting for transfers between devices  41.6 us (27%)
  Pallas kernels  36.4 us (24%)
  local copies, waits for them, and re-layouts  9.57 us (6%)
    ppermute x64, starting transfers between devices, permute(): return lax.ppermute(v, axis, xor(lax.axis_size(axis), m))  62.9 us
    ppermute x64, waiting for transfers between devices, permute(): return lax.ppermute(v, axis, xor(lax.axis_size(axis), m))  41.6 us
    pallas_call x14, Pallas kernels, call(): pl.pallas_call(kernel, out_shape=outs, in_specs=specs, out_specs=jax.tree...  36.4 us
    unnamed x49, local copies, waits for them, and re-layouts  9.5 us
  transfers between devices with their start and end apart: 64, of which 27 were waited for; matrix products, arithmetic and copies ran while one was open for 1% of the time, Pallas kernels for 7%

profile of v1, /device:TPU:0, one launch (start us, length us, event | category | flops | bytes accessed | tf_op | source)
XLA Modules:
  0.0 152.4 jit_solution(13095515482717431483)
XLA Ops:
  0.7 0.9 copy-done.6
  1.8 3.1 %collective-permute-start = (f32[32,32]{1,0:T(8,128)S(1)}, f32[32,32]{1,0:T(8,128)S(1)}, u32[]{:S(2)}, u32[]{:S(2)}) collective-permute-start(f32[32,32]{1,0:T(8,128)S(1)} %get-tuple-element.30), channel_id=1, source_target_pairs={{0,2},{1,3},{2,0},{3,1},{4,6},{5,7},{6,4},{7,5},{8,10},{9,11},{10,... | collective-permute-start | bytes 12296 | tf_op jit(solution)/shard_map/ppermute | solution.py:90
  4.9 2.6 %collective-permute-start.1 = (f32[32,32]{1,0:T(8,128)S(1)}, f32[32,32]{1,0:T(8,128)S(1)}, u32[]{:S(2)}, u32[]{:S(2)}) collective-permute-start(f32[32,32]{1,0:T(8,128)S(1)} %get-tuple-element.30), channel_id=1, source_target_pairs={{0,4},{1,5},{2,6},{3,7},{4,0},{5,1},{6,2},{7,3},{8,12},{9,13},{10,... | collective-permute-start | bytes 12296 | tf_op jit(solution)/shard_map/ppermute | solution.py:90
  7.5 0.9 collective-permute-start.8
  8.4 0.7 divide_bitcast_fusion.w_ref
  9.1 3.5 %collective-permute-start.10 = (f32[8,32,128]{2,1,0:T(8,128)S(1)}, f32[8,32,128]{2,1,0:T(8,128)S(1)}, u32[]{:S(2)}, u32[]{:S(2)}) collective-permute-start(f32[8,32,128]{2,1,0:T(8,128)S(1)} %get-tuple-element.29.own_ref), channel_id=1, source_target_pairs={{0,4},{1,5},{2,6},{3,7},{4,0},{5,1},{6,2},{7,3},{8,12},{9,13},{10,... | collective-permute-start | bytes 393224 | tf_op jit(solution)/shard_map/ppermute | solution.py:90
  13.3 1.2 collective-permute-done.3
  14.5 1.5 collective-permute-start.4
  16.0 1.5 collective-permute-start.5
  17.5 5.0 %collective-permute-done.10 = f32[8,32,128]{2,1,0:T(8,128)S(1)} collective-permute-done((f32[8,32,128]{2,1,0:T(8,128)S(1)}, f32[8,32,128]{2,1,0:T(8,128)S(1)}, u32[]{:S(2)}, u32[]{:S(2)}) %collective-permute-start.10) | collective-permute-done | bytes 131104 | tf_op jit(solution)/shard_map/ppermute | solution.py:90
  22.6 2.4 %collective-permute-start.6 = (f32[32,32]{1,0:T(8,128)S(1)}, f32[32,32]{1,0:T(8,128)S(1)}, u32[]{:S(2)}, u32[]{:S(2)}) collective-permute-start(f32[32,32]{1,0:T(8,128)S(1)} %add.45), channel_id=1, source_target_pairs={{0,24},{8,16},{16,8},{24,0},{1,25},{9,17},{17,9},{25,1},{2,26},{10... | collective-permute-start | bytes 12296 | tf_op jit(solution)/shard_map/ppermute | solution.py:90
  25.6 0.8 collective-permute-done.11
  26.6 0.7 copy-done.4
  29.0 2.4 %collective-permute-start.16 = (f32[4,32,128]{2,1,0:T(8,128)S(1)}, f32[4,32,128]{2,1,0:T(8,128)S(1)}, u32[]{:S(2)}, u32[]{:S(2)}) collective-permute-start(f32[4,32,128]{2,1,0:T(8,128)S(1)} %get-tuple-element.33), channel_id=1, source_target_pairs={{0,24},{8,16},{16,8},{24,0},{1,25},{9,17},{17,9},{25,1},{2,26},{10... | collective-permute-start | bytes 196616 | tf_op jit(solution)/shard_map/ppermute | solution.py:90
  31.5 0.8 collective-permute-done.14.rest_0_
  32.3 1.2 collective-permute-done.15.rest_1_
  33.5 0.7 collective-permute-done.16.rest_2_
  34.2 1.0 copy-done.2
  35.2 4.8 %start.1 = (f32[8,32,128]{2,1,0:T(8,128)S(1)}, f32[8,32,128]{2,1,0:T(8,128)S(1)}, bf16[8,32,128]{2,1,0:T(8,128)(2,1)S(1)}, f32[32,32]{1,0:T(8,128)S(1)}) custom-call(s32[4,4]{1,0:T(4,128)S(1)} %bitcast.14, f32[8]{0:T(128)S(1)} %divide_bitcast_fusion.w_ref, f32[8,32,128]{2,1,0:T(8,128)S(1)} %get-tuple-element.29.own_ref, f32[8,128,128]{2,1,0:T(8,128)S(1)} %bitcast.11, ...), custom_call_target="tpu_custom_call" | custom-call | tf_op jit(solution)/shard_map/start/pallas_call | solution.py:57
  40.1 2.6 %collective-permute-start.18 = (bf16[8,32,128]{2,1,0:T(8,128)(2,1)S(1)}, bf16[8,32,128]{2,1,0:T(8,128)(2,1)S(1)}, u32[]{:S(2)}, u32[]{:S(2)}) collective-permute-start(bf16[8,32,128]{2,1,0:T(8,128)(2,1)S(1)} %get-tuple-element.35), channel_id=1, source_target_pairs={{0,2},{1,3},{2,0},{3,1},{4,6},{5,7},{6,4},{7,5},{8,10},{9,11},{10,... | collective-permute-start | bytes 196616 | tf_op jit(solution)/shard_map/ppermute | solution.py:90
  42.7 0.9 collective-permute-start.20
  43.6 1.5 %collective-permute-start.22 = (bf16[8,32,128]{2,1,0:T(8,128)(2,1)S(1)}, bf16[8,32,128]{2,1,0:T(8,128)(2,1)S(1)}, u32[]{:S(2)}, u32[]{:S(2)}) collective-permute-start(bf16[8,32,128]{2,1,0:T(8,128)(2,1)S(1)} %get-tuple-element.35), channel_id=1, source_target_pairs={{0,6},{1,7},{2,4},{3,5},{4,2},{5,3},{6,0},{7,1},{8,14},{9,15},{10,... | collective-permute-start | bytes 196616 | tf_op jit(solution)/shard_map/ppermute | solution.py:90
  45.4 5.7 %collective-permute-done.20 = bf16[8,32,128]{2,1,0:T(8,128)(2,1)S(1)} collective-permute-done((bf16[8,32,128]{2,1,0:T(8,128)(2,1)S(1)}, bf16[8,32,128]{2,1,0:T(8,128)(2,1)S(1)}, u32[]{:S(2)}, u32[]{:S(2)}) %collective-permute-start.20) | collective-permute-done | bytes 65568 | tf_op jit(solution)/shard_map/ppermute | solution.py:90
  51.7 0.7 collective-permute-done.21
  53.7 0.7 collective-permute-start.25
  54.3 2.4 %collective-permute-start.26 = (bf16[4,32,128]{2,1,0:T(8,128)(2,1)S(1)}, bf16[4,32,128]{2,1,0:T(8,128)(2,1)S(1)}, u32[]{:S(2)}, u32[]{:S(2)}) collective-permute-start(bf16[4,32,128]{2,1,0:T(8,128)(2,1)S(1)} %get-tuple-element.38), channel_id=1, source_target_pairs={{0,24},{8,16},{16,8},{24,0},{1,25},{9,17},{17,9},{25,1},{2,26},{10... | collective-permute-start | bytes 98312 | tf_op jit(solution)/shard_map/ppermute | solution.py:90
  56.8 5.8 %copy-done = bf16[1,1024,8192]{2,1,0:T(8,128)(2,1)S(1)} copy-done((bf16[1,1024,8192]{2,1,0:T(8,128)(2,1)S(1)}, bf16[1,1024,8192]{2,1,0:T(8,128)(2,1)}, u32[]{:S(2)}) %copy-start) | copy-done | bytes 16777240
  62.5 5.0 %multiply.2.part_ref = f32[32,1024]{1,0:T(8,128)S(1)} custom-call(bf16[1024,8192]{1,0:T(8,128)(2,1)S(1)} %bitcast.7, bf16[64,32,128]{2,1,0:T(8,128)(2,1)S(1)} %constant_dynamic-update-slice_fusion.8.p_ref), custom_call_target="tpu_custom_call" | custom-call | tf_op jit(solution)/shard_map/multiply/pallas_call | solution.py:57
  67.6 0.7 copy-done.1
  68.3 1.7 %multiply_shared.2 = (f32[8,32,128]{2,1,0:T(8,128)S(1)}, bf16[8,32,128]{2,1,0:T(8,128)(2,1)S(1)}) custom-call(s32[4,4]{1,0:T(4,128)S(1)} %bitcast.16, bf16[1024,8192]{1,0:T(8,128)(2,1)S(1)} %bitcast.8, f32[32,1024]{1,0:T(8,128)S(1)} %multiply.2.part_ref, bf16[4,32,128]{2,1,0:T(8,128)(2,1)S(1)} %collective-permute-done.24.rest_0_.rest_3_, ...), custom_call_target="tpu_custom_call" | custom-call | tf_op jit(solution)/shard_map/multiply_shared/pallas_call | solution.py:57
  70.0 1.3 collective-permute-start.28
  71.3 1.3 collective-permute-start.30
  72.7 1.8 %collective-permute-start.32 = (bf16[8,32,128]{2,1,0:T(8,128)(2,1)S(1)}, bf16[8,32,128]{2,1,0:T(8,128)(2,1)S(1)}, u32[]{:S(2)}, u32[]{:S(2)}) collective-permute-start(bf16[8,32,128]{2,1,0:T(8,128)(2,1)S(1)} %get-tuple-element.40), channel_id=1, source_target_pairs={{0,6},{1,7},{2,4},{3,5},{4,2},{5,3},{6,0},{7,1},{8,14},{9,15},{10,... | collective-permute-start | bytes 196616 | tf_op jit(solution)/shard_map/ppermute | solution.py:90
  74.6 5.2 %collective-permute-done.30 = bf16[8,32,128]{2,1,0:T(8,128)(2,1)S(1)} collective-permute-done((bf16[8,32,128]{2,1,0:T(8,128)(2,1)S(1)}, bf16[8,32,128]{2,1,0:T(8,128)(2,1)S(1)}, u32[]{:S(2)}, u32[]{:S(2)}) %collective-permute-start.30) | collective-permute-done | bytes 65568 | tf_op jit(solution)/shard_map/ppermute | solution.py:90
  80.4 0.7 collective-permute-done.31
  82.4 0.7 collective-permute-start.35
  83.1 2.3 %collective-permute-start.36 = (bf16[4,32,128]{2,1,0:T(8,128)(2,1)S(1)}, bf16[4,32,128]{2,1,0:T(8,128)(2,1)S(1)}, u32[]{:S(2)}, u32[]{:S(2)}) collective-permute-start(bf16[4,32,128]{2,1,0:T(8,128)(2,1)S(1)} %get-tuple-element.43), channel_id=1, source_target_pairs={{0,24},{8,16},{16,8},{24,0},{1,25},{9,17},{17,9},{25,1},{2,26},{10... | collective-permute-start | bytes 98312 | tf_op jit(solution)/shard_map/ppermute | solution.py:90
  86.3 1.6 %collective-permute-done.36.rest_2_ = bf16[4,32,128]{2,1,0:T(8,128)(2,1)S(1)} collective-permute-done((bf16[4,32,128]{2,1,0:T(8,128)(2,1)S(1)}, bf16[4,32,128]{2,1,0:T(8,128)(2,1)S(1)}, u32[]{:S(2)}, u32[]{:S(2)}) %collective-permute-start.36) | collective-permute-done | bytes 32800 | tf_op jit(solution)/shard_map/ppermute | solution.py:90
  87.9 1.9 %middle.1 = (f32[8,32,128]{2,1,0:T(8,128)S(1)}, f32[8,32,128]{2,1,0:T(8,128)S(1)}, bf16[8,32,128]{2,1,0:T(8,128)(2,1)S(1)}) custom-call(s32[4,4]{1,0:T(4,128)S(1)} %bitcast.18, f32[8]{0:T(128)S(1)} %divide_bitcast_fusion.w_ref, f32[8,32,128]{2,1,0:T(8,128)S(1)} %get-tuple-element.39.own_ref, f32[8,128,128]{2,1,0:T(8,128)S(1)} %bitcast.12, ...), custom_call_target="tpu_custom_call" | custom-call | tf_op jit(solution)/shard_map/middle/pallas_call | solution.py:57
  89.8 1.3 collective-permute-start.38
  91.1 1.4 collective-permute-start.40
  92.5 1.7 %collective-permute-start.42 = (bf16[8,32,128]{2,1,0:T(8,128)(2,1)S(1)}, bf16[8,32,128]{2,1,0:T(8,128)(2,1)S(1)}, u32[]{:S(2)}, u32[]{:S(2)}) collective-permute-start(bf16[8,32,128]{2,1,0:T(8,128)(2,1)S(1)} %get-tuple-element.45), channel_id=1, source_target_pairs={{0,6},{1,7},{2,4},{3,5},{4,2},{5,3},{6,0},{7,1},{8,14},{9,15},{10,... | collective-permute-start | bytes 196616 | tf_op jit(solution)/shard_map/ppermute | solution.py:90
  94.3 5.2 %collective-permute-done.40 = bf16[8,32,128]{2,1,0:T(8,128)(2,1)S(1)} collective-permute-done((bf16[8,32,128]{2,1,0:T(8,128)(2,1)S(1)}, bf16[8,32,128]{2,1,0:T(8,128)(2,1)S(1)}, u32[]{:S(2)}, u32[]{:S(2)}) %collective-permute-start.40) | collective-permute-done | bytes 65568 | tf_op jit(solution)/shard_map/ppermute | solution.py:90
  100.1 0.7 collective-permute-done.41
  101.6 1.3 collective-permute-start.44
  102.9 1.6 %collective-permute-start.45 = (bf16[4,32,128]{2,1,0:T(8,128)(2,1)S(1)}, bf16[4,32,128]{2,1,0:T(8,128)(2,1)S(1)}, u32[]{:S(2)}, u32[]{:S(2)}) collective-permute-start(bf16[4,32,128]{2,1,0:T(8,128)(2,1)S(1)} %get-tuple-element.47), channel_id=1, source_target_pairs={{0,16},{8,24},{16,0},{24,8},{1,17},{9,25},{17,1},{25,9},{2,18},{10... | collective-permute-start | bytes 98312 | tf_op jit(solution)/shard_map/ppermute | solution.py:90
  105.2 5.0 %multiply.3.part_ref = f32[32,1024]{1,0:T(8,128)S(1)} custom-call(bf16[1024,8192]{1,0:T(8,128)(2,1)S(1)} %bitcast.9, bf16[64,32,128]{2,1,0:T(8,128)(2,1)S(1)} %constant_dynamic-update-slice_fusion.24.p_ref), custom_call_target="tpu_custom_call" | custom-call | tf_op jit(solution)/shard_map/multiply/pallas_call | solution.py:57
  110.3 1.7 %multiply_shared.3 = (f32[8,32,128]{2,1,0:T(8,128)S(1)}, bf16[8,32,128]{2,1,0:T(8,128)(2,1)S(1)}) custom-call(s32[4,4]{1,0:T(4,128)S(1)} %bitcast.20, bf16[1024,8192]{1,0:T(8,128)(2,1)S(1)} %bitcast.10, f32[32,1024]{1,0:T(8,128)S(1)} %multiply.3.part_ref, bf16[4,32,128]{2,1,0:T(8,128)(2,1)S(1)} %collective-permute-done.44.rest_0_.rest_6_, ...), custom_call_target="tpu_custom_call" | custom-call | tf_op jit(solution)/shard_map/multiply_shared/pallas_call | solution.py:57
  111.9 1.0 inner.1
  113.0 1.3 collective-permute-start.47
  114.2 1.4 collective-permute-start.48
  115.7 1.7 %collective-permute-start.49 = (f32[96,96]{1,0:T(8,128)S(1)}, f32[96,96]{1,0:T(8,128)S(1)}, u32[]{:S(2)}, u32[]{:S(2)}) collective-permute-start(f32[96,96]{1,0:T(8,128)S(1)} %inner.1), channel_id=1, source_target_pairs={{0,6},{1,7},{2,4},{3,5},{4,2},{5,3},{6,0},{7,1},{8,14},{9,15},{10,... | collective-permute-start | bytes 110600 | tf_op jit(solution)/shard_map/ppermute | solution.py:90
  117.8 2.3 %collective-permute-start.57 = (bf16[8,32,128]{2,1,0:T(8,128)(2,1)S(1)}, bf16[8,32,128]{2,1,0:T(8,128)(2,1)S(1)}, u32[]{:S(2)}, u32[]{:S(2)}) collective-permute-start(bf16[8,32,128]{2,1,0:T(8,128)(2,1)S(1)} %get-tuple-element.50), channel_id=1, source_target_pairs={{0,4},{1,5},{2,6},{3,7},{4,0},{5,1},{6,2},{7,3},{8,12},{9,13},{10,... | collective-permute-start | bytes 196616 | tf_op jit(solution)/shard_map/ppermute | solution.py:90
  120.3 2.1 %collective-permute-start.59 = (bf16[8,32,128]{2,1,0:T(8,128)(2,1)S(1)}, bf16[8,32,128]{2,1,0:T(8,128)(2,1)S(1)}, u32[]{:S(2)}, u32[]{:S(2)}) collective-permute-start(bf16[8,32,128]{2,1,0:T(8,128)(2,1)S(1)} %get-tuple-element.50), channel_id=1, source_target_pairs={{0,6},{1,7},{2,4},{3,5},{4,2},{5,3},{6,0},{7,1},{8,14},{9,15},{10,... | collective-permute-start | bytes 196616 | tf_op jit(solution)/shard_map/ppermute | solution.py:90
  122.5 1.1 collective-permute-done.55
  123.6 3.0 %collective-permute-done.57 = bf16[8,32,128]{2,1,0:T(8,128)(2,1)S(1)} collective-permute-done((bf16[8,32,128]{2,1,0:T(8,128)(2,1)S(1)}, bf16[8,32,128]{2,1,0:T(8,128)(2,1)S(1)}, u32[]{:S(2)}, u32[]{:S(2)}) %collective-permute-start.57) | collective-permute-done | bytes 65568 | tf_op jit(solution)/shard_map/ppermute | solution.py:90
  127.1 1.3 collective-permute-start.51
  128.4 1.6 %collective-permute-start.52 = (f32[96,96]{1,0:T(8,128)S(1)}, f32[96,96]{1,0:T(8,128)S(1)}, u32[]{:S(2)}, u32[]{:S(2)}) collective-permute-start(f32[96,96]{1,0:T(8,128)S(1)} %add.52), channel_id=1, source_target_pairs={{0,16},{8,24},{16,0},{24,8},{1,17},{9,25},{17,1},{25,9},{2,18},{10... | collective-permute-start | bytes 110600 | tf_op jit(solution)/shard_map/ppermute | solution.py:90
  130.7 0.7 select_all.1.s_ref
  131.4 1.3 collective-permute-start.61
  132.7 1.6 %collective-permute-start.62 = (bf16[16,32,128]{2,1,0:T(8,128)(2,1)S(1)}, bf16[16,32,128]{2,1,0:T(8,128)(2,1)S(1)}, u32[]{:S(2)}, u32[]{:S(2)}) collective-permute-start(bf16[16,32,128]{2,1,0:T(8,128)(2,1)S(1)} %select_all.1.s_ref), channel_id=1, source_target_pairs={{0,16},{8,24},{16,0},{24,8},{1,17},{9,25},{17,1},{25,9},{2,18},{10... | collective-permute-start | bytes 393224 | tf_op jit(solution)/shard_map/ppermute | solution.py:90
  135.6 2.2 %collective-permute-done.61.rest_0_ = bf16[16,32,128]{2,1,0:T(8,128)(2,1)S(1)} collective-permute-done((bf16[16,32,128]{2,1,0:T(8,128)(2,1)S(1)}, bf16[16,32,128]{2,1,0:T(8,128)(2,1)S(1)}, u32[]{:S(2)}, u32[]{:S(2)}) %collective-permute-start.61) | collective-permute-done | bytes 131104 | tf_op jit(solution)/shard_map/ppermute | solution.py:90
  137.8 2.7 %collective-permute-done.62.rest_1_ = bf16[16,32,128]{2,1,0:T(8,128)(2,1)S(1)} collective-permute-done((bf16[16,32,128]{2,1,0:T(8,128)(2,1)S(1)}, bf16[16,32,128]{2,1,0:T(8,128)(2,1)S(1)}, u32[]{:S(2)}, u32[]{:S(2)}) %collective-permute-start.62) | collective-permute-done | bytes 131104 | tf_op jit(solution)/shard_map/ppermute | solution.py:90
  140.5 11.9 %finish.1 = (f32[32,1024]{1,0:T(8,128)}, f32[32,96]{1,0:T(8,128)}) custom-call(s32[4,4]{1,0:T(4,128)S(1)} %bitcast.22, f32[96,96]{1,0:T(8,128)S(1)} %add_add_fusion.g_ref, bf16[16,32,128]{2,1,0:T(8,128)(2,1)S(1)} %select_all.1.s_ref, f32[32,32]{1,0:T(8,128)S(1)} %get-tuple-element.51.f_ref, f32[8,32,128]{2,1,0:T(8,128)S(1)} %get-tuple-element.52.x0_ref, ...), custom_call_target="tpu_custom_call" | custom-call | tf_op jit(solution)/shard_map/finish/pallas_call | solution.py:57
  (139 shorter events, 13.8 us)
Async XLA Ops:
  1.8 7.3 %collective-permute-start = (f32[32,32]{1,0:T(8,128)S(1)}, f32[32,32]{1,0:T(8,128)S(1)}, u32[]{:S(2)}, u32[]{:S(2)}) collective-permute-start(f32[32,32]{1,0:T(8,128)S(1)} %get-tuple-element.30), channel_id=1, source_target_pairs={{0,2},{1,3},{2,0},{3,1},{4,6},{5,7},{6,4},{7,5},{8,10},{9,11},{10,... | collective-permute-start | bytes 12296 | tf_op jit(solution)/shard_map/ppermute | solution.py:90
  4.9 7.7 %collective-permute-start.1 = (f32[32,32]{1,0:T(8,128)S(1)}, f32[32,32]{1,0:T(8,128)S(1)}, u32[]{:S(2)}, u32[]{:S(2)}) collective-permute-start(f32[32,32]{1,0:T(8,128)S(1)} %get-tuple-element.30), channel_id=1, source_target_pairs={{0,4},{1,5},{2,6},{3,7},{4,0},{5,1},{6,2},{7,3},{8,12},{9,13},{10,... | collective-permute-start | bytes 12296 | tf_op jit(solution)/shard_map/ppermute | solution.py:90
  7.5 5.7 %collective-permute-start.2 = (f32[32,32]{1,0:T(8,128)S(1)}, f32[32,32]{1,0:T(8,128)S(1)}, u32[]{:S(2)}, u32[]{:S(2)}) collective-permute-start(f32[32,32]{1,0:T(8,128)S(1)} %get-tuple-element.30), channel_id=1, source_target_pairs={{0,6},{1,7},{2,4},{3,5},{4,2},{5,3},{6,0},{7,1},{8,14},{9,15},{10,... | collective-permute-start | bytes 12296 | tf_op jit(solution)/shard_map/ppermute | solution.py:90
  7.5 8.5 %collective-permute-start.7 = (f32[8,32,128]{2,1,0:T(8,128)S(1)}, f32[8,32,128]{2,1,0:T(8,128)S(1)}, u32[]{:S(2)}, u32[]{:S(2)}) collective-permute-start(f32[8,32,128]{2,1,0:T(8,128)S(1)} %get-tuple-element.29.own_ref), channel_id=1, source_target_pairs={{0,1},{1,0},{2,3},{3,2},{4,5},{5,4},{6,7},{7,6},{8,9},{9,8},{10,11... | collective-permute-start | bytes 393224 | tf_op jit(solution)/shard_map/ppermute | solution.py:90
  7.5 10.0 %collective-permute-start.8 = (f32[8,32,128]{2,1,0:T(8,128)S(1)}, f32[8,32,128]{2,1,0:T(8,128)S(1)}, u32[]{:S(2)}, u32[]{:S(2)}) collective-permute-start(f32[8,32,128]{2,1,0:T(8,128)S(1)} %get-tuple-element.29.own_ref), channel_id=1, source_target_pairs={{0,2},{1,3},{2,0},{3,1},{4,6},{5,7},{6,4},{7,5},{8,10},{9,11},{10,... | collective-permute-start | bytes 393224 | tf_op jit(solution)/shard_map/ppermute | solution.py:90
  9.1 13.5 %collective-permute-start.10 = (f32[8,32,128]{2,1,0:T(8,128)S(1)}, f32[8,32,128]{2,1,0:T(8,128)S(1)}, u32[]{:S(2)}, u32[]{:S(2)}) collective-permute-start(f32[8,32,128]{2,1,0:T(8,128)S(1)} %get-tuple-element.29.own_ref), channel_id=1, source_target_pairs={{0,4},{1,5},{2,6},{3,7},{4,0},{5,1},{6,2},{7,3},{8,12},{9,13},{10,... | collective-permute-start | bytes 393224 | tf_op jit(solution)/shard_map/ppermute | solution.py:90
  12.6 12.5 %collective-permute-start.12 = (f32[8,32,128]{2,1,0:T(8,128)S(1)}, f32[8,32,128]{2,1,0:T(8,128)S(1)}, u32[]{:S(2)}, u32[]{:S(2)}) collective-permute-start(f32[8,32,128]{2,1,0:T(8,128)S(1)} %get-tuple-element.29.own_ref), channel_id=1, source_target_pairs={{0,6},{1,7},{2,4},{3,5},{4,2},{5,3},{6,0},{7,1},{8,14},{9,15},{10,... | collective-permute-start | bytes 393224 | tf_op jit(solution)/shard_map/ppermute | solution.py:90
  13.2 1.2 collective-permute-start.3
  14.5 14.6 %collective-permute-start.4 = (f32[32,32]{1,0:T(8,128)S(1)}, f32[32,32]{1,0:T(8,128)S(1)}, u32[]{:S(2)}, u32[]{:S(2)}) collective-permute-start(f32[32,32]{1,0:T(8,128)S(1)} %add.45), channel_id=1, source_target_pairs={{0,8},{8,0},{16,24},{24,16},{1,9},{9,1},{17,25},{25,17},{2,10},{10... | collective-permute-start | bytes 12296 | tf_op jit(solution)/shard_map/ppermute | solution.py:90
  16.0 15.5 %collective-permute-start.5 = (f32[32,32]{1,0:T(8,128)S(1)}, f32[32,32]{1,0:T(8,128)S(1)}, u32[]{:S(2)}, u32[]{:S(2)}) collective-permute-start(f32[32,32]{1,0:T(8,128)S(1)} %add.45), channel_id=1, source_target_pairs={{0,16},{8,24},{16,0},{24,8},{1,17},{9,25},{17,1},{25,9},{2,18},{10... | collective-permute-start | bytes 12296 | tf_op jit(solution)/shard_map/ppermute | solution.py:90
  17.5 7.5 %collective-permute-start.9 = (f32[8,32,128]{2,1,0:T(8,128)S(1)}, f32[8,32,128]{2,1,0:T(8,128)S(1)}, u32[]{:S(2)}, u32[]{:S(2)}) collective-permute-start(f32[8,32,128]{2,1,0:T(8,128)S(1)} %collective-permute-done.8), channel_id=1, source_target_pairs={{0,1},{1,0},{2,3},{3,2},{4,5},{5,4},{6,7},{7,6},{8,9},{9,8},{10,11... | collective-permute-start | bytes 393224 | tf_op jit(solution)/shard_map/ppermute | solution.py:90
  22.6 8.9 %collective-permute-start.6 = (f32[32,32]{1,0:T(8,128)S(1)}, f32[32,32]{1,0:T(8,128)S(1)}, u32[]{:S(2)}, u32[]{:S(2)}) collective-permute-start(f32[32,32]{1,0:T(8,128)S(1)} %add.45), channel_id=1, source_target_pairs={{0,24},{8,16},{16,8},{24,0},{1,25},{9,17},{17,9},{25,1},{2,26},{10... | collective-permute-start | bytes 12296 | tf_op jit(solution)/shard_map/ppermute | solution.py:90
  25.0 1.3 collective-permute-start.11
  25.0 1.5 %collective-permute-start.13 = (f32[8,32,128]{2,1,0:T(8,128)S(1)}, f32[8,32,128]{2,1,0:T(8,128)S(1)}, u32[]{:S(2)}, u32[]{:S(2)}) collective-permute-start(f32[8,32,128]{2,1,0:T(8,128)S(1)} %collective-permute-done.12), channel_id=1, source_target_pairs={{0,1},{1,0},{2,3},{3,2},{4,5},{5,4},{6,7},{7,6},{8,9},{9,8},{10,11... | collective-permute-start | bytes 393224 | tf_op jit(solution)/shard_map/ppermute | solution.py:90
  27.9 4.4 %collective-permute-start.14 = (f32[4,32,128]{2,1,0:T(8,128)S(1)}, f32[4,32,128]{2,1,0:T(8,128)S(1)}, u32[]{:S(2)}, u32[]{:S(2)}) collective-permute-start(f32[4,32,128]{2,1,0:T(8,128)S(1)} %get-tuple-element.31), channel_id=1, source_target_pairs={{0,8},{8,0},{16,24},{24,16},{1,9},{9,1},{17,25},{25,17},{2,10},{10... | collective-permute-start | bytes 196616 | tf_op jit(solution)/shard_map/ppermute | solution.py:90
  28.5 5.0 %collective-permute-start.15 = (f32[4,32,128]{2,1,0:T(8,128)S(1)}, f32[4,32,128]{2,1,0:T(8,128)S(1)}, u32[]{:S(2)}, u32[]{:S(2)}) collective-permute-start(f32[4,32,128]{2,1,0:T(8,128)S(1)} %get-tuple-element.32), channel_id=1, source_target_pairs={{0,16},{8,24},{16,0},{24,8},{1,17},{9,25},{17,1},{25,9},{2,18},{10... | collective-permute-start | bytes 196616 | tf_op jit(solution)/shard_map/ppermute | solution.py:90
  29.0 5.2 %collective-permute-start.16 = (f32[4,32,128]{2,1,0:T(8,128)S(1)}, f32[4,32,128]{2,1,0:T(8,128)S(1)}, u32[]{:S(2)}, u32[]{:S(2)}) collective-permute-start(f32[4,32,128]{2,1,0:T(8,128)S(1)} %get-tuple-element.33), channel_id=1, source_target_pairs={{0,24},{8,16},{16,8},{24,0},{1,25},{9,17},{17,9},{25,1},{2,26},{10... | collective-permute-start | bytes 196616 | tf_op jit(solution)/shard_map/ppermute | solution.py:90
  40.0 11.6 %collective-permute-start.17 = (bf16[8,32,128]{2,1,0:T(8,128)(2,1)S(1)}, bf16[8,32,128]{2,1,0:T(8,128)(2,1)S(1)}, u32[]{:S(2)}, u32[]{:S(2)}) collective-permute-start(bf16[8,32,128]{2,1,0:T(8,128)(2,1)S(1)} %get-tuple-element.35), channel_id=1, source_target_pairs={{0,1},{1,0},{2,3},{3,2},{4,5},{5,4},{6,7},{7,6},{8,9},{9,8},{10,11... | collective-permute-start | bytes 196616 | tf_op jit(solution)/shard_map/ppermute | solution.py:90
  40.1 5.2 %collective-permute-start.18 = (bf16[8,32,128]{2,1,0:T(8,128)(2,1)S(1)}, bf16[8,32,128]{2,1,0:T(8,128)(2,1)S(1)}, u32[]{:S(2)}, u32[]{:S(2)}) collective-permute-start(bf16[8,32,128]{2,1,0:T(8,128)(2,1)S(1)} %get-tuple-element.35), channel_id=1, source_target_pairs={{0,2},{1,3},{2,0},{3,1},{4,6},{5,7},{6,4},{7,5},{8,10},{9,11},{10,... | collective-permute-start | bytes 196616 | tf_op jit(solution)/shard_map/ppermute | solution.py:90
  42.7 8.4 %collective-permute-start.20 = (bf16[8,32,128]{2,1,0:T(8,128)(2,1)S(1)}, bf16[8,32,128]{2,1,0:T(8,128)(2,1)S(1)}, u32[]{:S(2)}, u32[]{:S(2)}) collective-permute-start(bf16[8,32,128]{2,1,0:T(8,128)(2,1)S(1)} %get-tuple-element.35), channel_id=1, source_target_pairs={{0,4},{1,5},{2,6},{3,7},{4,0},{5,1},{6,2},{7,3},{8,12},{9,13},{10,... | collective-permute-start | bytes 196616 | tf_op jit(solution)/shard_map/ppermute | solution.py:90
  43.6 7.5 %collective-permute-start.22 = (bf16[8,32,128]{2,1,0:T(8,128)(2,1)S(1)}, bf16[8,32,128]{2,1,0:T(8,128)(2,1)S(1)}, u32[]{:S(2)}, u32[]{:S(2)}) collective-permute-start(bf16[8,32,128]{2,1,0:T(8,128)(2,1)S(1)} %get-tuple-element.35), channel_id=1, source_target_pairs={{0,6},{1,7},{2,4},{3,5},{4,2},{5,3},{6,0},{7,1},{8,14},{9,15},{10,... | collective-permute-start | bytes 196616 | tf_op jit(solution)/shard_map/ppermute | solution.py:90
  45.4 6.3 %collective-permute-start.19 = (bf16[8,32,128]{2,1,0:T(8,128)(2,1)S(1)}, bf16[8,32,128]{2,1,0:T(8,128)(2,1)S(1)}, u32[]{:S(2)}, u32[]{:S(2)}) collective-permute-start(bf16[8,32,128]{2,1,0:T(8,128)(2,1)S(1)} %collective-permute-done.18), channel_id=1, source_target_pairs={{0,1},{1,0},{2,3},{3,2},{4,5},{5,4},{6,7},{7,6},{8,9},{9,8},{10,11... | collective-permute-start | bytes 196616 | tf_op jit(solution)/shard_map/ppermute | solution.py:90
  51.1 1.3 collective-permute-start.21
  51.1 1.4 collective-permute-start.23
  53.2 14.4 %collective-permute-start.24 = (bf16[4,32,128]{2,1,0:T(8,128)(2,1)S(1)}, bf16[4,32,128]{2,1,0:T(8,128)(2,1)S(1)}, u32[]{:S(2)}, u32[]{:S(2)}) collective-permute-start(bf16[4,32,128]{2,1,0:T(8,128)(2,1)S(1)} %get-tuple-element.36), channel_id=1, source_target_pairs={{0,8},{8,0},{16,24},{24,16},{1,9},{9,1},{17,25},{25,17},{2,10},{10... | collective-permute-start | bytes 98312 | tf_op jit(solution)/shard_map/ppermute | solution.py:90
  53.7 13.9 %collective-permute-start.25 = (bf16[4,32,128]{2,1,0:T(8,128)(2,1)S(1)}, bf16[4,32,128]{2,1,0:T(8,128)(2,1)S(1)}, u32[]{:S(2)}, u32[]{:S(2)}) collective-permute-start(bf16[4,32,128]{2,1,0:T(8,128)(2,1)S(1)} %get-tuple-element.37), channel_id=1, source_target_pairs={{0,16},{8,24},{16,0},{24,8},{1,17},{9,25},{17,1},{25,9},{2,18},{10... | collective-permute-start | bytes 98312 | tf_op jit(solution)/shard_map/ppermute | solution.py:90
  54.3 13.3 %collective-permute-start.26 = (bf16[4,32,128]{2,1,0:T(8,128)(2,1)S(1)}, bf16[4,32,128]{2,1,0:T(8,128)(2,1)S(1)}, u32[]{:S(2)}, u32[]{:S(2)}) collective-permute-start(bf16[4,32,128]{2,1,0:T(8,128)(2,1)S(1)} %get-tuple-element.38), channel_id=1, source_target_pairs={{0,24},{8,16},{16,8},{24,0},{1,25},{9,17},{17,9},{25,1},{2,26},{10... | collective-permute-start | bytes 98312 | tf_op jit(solution)/shard_map/ppermute | solution.py:90
  70.0 10.3 %collective-permute-start.27 = (bf16[8,32,128]{2,1,0:T(8,128)(2,1)S(1)}, bf16[8,32,128]{2,1,0:T(8,128)(2,1)S(1)}, u32[]{:S(2)}, u32[]{:S(2)}) collective-permute-start(bf16[8,32,128]{2,1,0:T(8,128)(2,1)S(1)} %get-tuple-element.40), channel_id=1, source_target_pairs={{0,1},{1,0},{2,3},{3,2},{4,5},{5,4},{6,7},{7,6},{8,9},{9,8},{10,11... | collective-permute-start | bytes 196616 | tf_op jit(solution)/shard_map/ppermute | solution.py:90
  70.0 4.5 %collective-permute-start.28 = (bf16[8,32,128]{2,1,0:T(8,128)(2,1)S(1)}, bf16[8,32,128]{2,1,0:T(8,128)(2,1)S(1)}, u32[]{:S(2)}, u32[]{:S(2)}) collective-permute-start(bf16[8,32,128]{2,1,0:T(8,128)(2,1)S(1)} %get-tuple-element.40), channel_id=1, source_target_pairs={{0,2},{1,3},{2,0},{3,1},{4,6},{5,7},{6,4},{7,5},{8,10},{9,11},{10,... | collective-permute-start | bytes 196616 | tf_op jit(solution)/shard_map/ppermute | solution.py:90
  71.3 8.5 %collective-permute-start.30 = (bf16[8,32,128]{2,1,0:T(8,128)(2,1)S(1)}, bf16[8,32,128]{2,1,0:T(8,128)(2,1)S(1)}, u32[]{:S(2)}, u32[]{:S(2)}) collective-permute-start(bf16[8,32,128]{2,1,0:T(8,128)(2,1)S(1)} %get-tuple-element.40), channel_id=1, source_target_pairs={{0,4},{1,5},{2,6},{3,7},{4,0},{5,1},{6,2},{7,3},{8,12},{9,13},{10,... | collective-permute-start | bytes 196616 | tf_op jit(solution)/shard_map/ppermute | solution.py:90
  72.7 7.1 %collective-permute-start.32 = (bf16[8,32,128]{2,1,0:T(8,128)(2,1)S(1)}, bf16[8,32,128]{2,1,0:T(8,128)(2,1)S(1)}, u32[]{:S(2)}, u32[]{:S(2)}) collective-permute-start(bf16[8,32,128]{2,1,0:T(8,128)(2,1)S(1)} %get-tuple-element.40), channel_id=1, source_target_pairs={{0,6},{1,7},{2,4},{3,5},{4,2},{5,3},{6,0},{7,1},{8,14},{9,15},{10,... | collective-permute-start | bytes 196616 | tf_op jit(solution)/shard_map/ppermute | solution.py:90
  74.5 5.8 %collective-permute-start.29 = (bf16[8,32,128]{2,1,0:T(8,128)(2,1)S(1)}, bf16[8,32,128]{2,1,0:T(8,128)(2,1)S(1)}, u32[]{:S(2)}, u32[]{:S(2)}) collective-permute-start(bf16[8,32,128]{2,1,0:T(8,128)(2,1)S(1)} %collective-permute-done.28), channel_id=1, source_target_pairs={{0,1},{1,0},{2,3},{3,2},{4,5},{5,4},{6,7},{7,6},{8,9},{9,8},{10,11... | collective-permute-start | bytes 196616 | tf_op jit(solution)/shard_map/ppermute | solution.py:90
  79.8 1.3 collective-permute-start.31
  79.8 1.4 collective-permute-start.33
  81.9 4.0 %collective-permute-start.34 = (bf16[4,32,128]{2,1,0:T(8,128)(2,1)S(1)}, bf16[4,32,128]{2,1,0:T(8,128)(2,1)S(1)}, u32[]{:S(2)}, u32[]{:S(2)}) collective-permute-start(bf16[4,32,128]{2,1,0:T(8,128)(2,1)S(1)} %get-tuple-element.41), channel_id=1, source_target_pairs={{0,8},{8,0},{16,24},{24,16},{1,9},{9,1},{17,25},{25,17},{2,10},{10... | collective-permute-start | bytes 98312 | tf_op jit(solution)/shard_map/ppermute | solution.py:90
  82.4 3.9 %collective-permute-start.35 = (bf16[4,32,128]{2,1,0:T(8,128)(2,1)S(1)}, bf16[4,32,128]{2,1,0:T(8,128)(2,1)S(1)}, u32[]{:S(2)}, u32[]{:S(2)}) collective-permute-start(bf16[4,32,128]{2,1,0:T(8,128)(2,1)S(1)} %get-tuple-element.42), channel_id=1, source_target_pairs={{0,16},{8,24},{16,0},{24,8},{1,17},{9,25},{17,1},{25,9},{2,18},{10... | collective-permute-start | bytes 98312 | tf_op jit(solution)/shard_map/ppermute | solution.py:90
  83.1 4.8 %collective-permute-start.36 = (bf16[4,32,128]{2,1,0:T(8,128)(2,1)S(1)}, bf16[4,32,128]{2,1,0:T(8,128)(2,1)S(1)}, u32[]{:S(2)}, u32[]{:S(2)}) collective-permute-start(bf16[4,32,128]{2,1,0:T(8,128)(2,1)S(1)} %get-tuple-element.43), channel_id=1, source_target_pairs={{0,24},{8,16},{16,8},{24,0},{1,25},{9,17},{17,9},{25,1},{2,26},{10... | collective-permute-start | bytes 98312 | tf_op jit(solution)/shard_map/ppermute | solution.py:90
  89.8 10.3 %collective-permute-start.37 = (bf16[8,32,128]{2,1,0:T(8,128)(2,1)S(1)}, bf16[8,32,128]{2,1,0:T(8,128)(2,1)S(1)}, u32[]{:S(2)}, u32[]{:S(2)}) collective-permute-start(bf16[8,32,128]{2,1,0:T(8,128)(2,1)S(1)} %get-tuple-element.45), channel_id=1, source_target_pairs={{0,1},{1,0},{2,3},{3,2},{4,5},{5,4},{6,7},{7,6},{8,9},{9,8},{10,11... | collective-permute-start | bytes 196616 | tf_op jit(solution)/shard_map/ppermute | solution.py:90
  89.8 4.5 %collective-permute-start.38 = (bf16[8,32,128]{2,1,0:T(8,128)(2,1)S(1)}, bf16[8,32,128]{2,1,0:T(8,128)(2,1)S(1)}, u32[]{:S(2)}, u32[]{:S(2)}) collective-permute-start(bf16[8,32,128]{2,1,0:T(8,128)(2,1)S(1)} %get-tuple-element.45), channel_id=1, source_target_pairs={{0,2},{1,3},{2,0},{3,1},{4,6},{5,7},{6,4},{7,5},{8,10},{9,11},{10,... | collective-permute-start | bytes 196616 | tf_op jit(solution)/shard_map/ppermute | solution.py:90
  91.1 8.5 %collective-permute-start.40 = (bf16[8,32,128]{2,1,0:T(8,128)(2,1)S(1)}, bf16[8,32,128]{2,1,0:T(8,128)(2,1)S(1)}, u32[]{:S(2)}, u32[]{:S(2)}) collective-permute-start(bf16[8,32,128]{2,1,0:T(8,128)(2,1)S(1)} %get-tuple-element.45), channel_id=1, source_target_pairs={{0,4},{1,5},{2,6},{3,7},{4,0},{5,1},{6,2},{7,3},{8,12},{9,13},{10,... | collective-permute-start | bytes 196616 | tf_op jit(solution)/shard_map/ppermute | solution.py:90
  92.5 7.0 %collective-permute-start.42 = (bf16[8,32,128]{2,1,0:T(8,128)(2,1)S(1)}, bf16[8,32,128]{2,1,0:T(8,128)(2,1)S(1)}, u32[]{:S(2)}, u32[]{:S(2)}) collective-permute-start(bf16[8,32,128]{2,1,0:T(8,128)(2,1)S(1)} %get-tuple-element.45), channel_id=1, source_target_pairs={{0,6},{1,7},{2,4},{3,5},{4,2},{5,3},{6,0},{7,1},{8,14},{9,15},{10,... | collective-permute-start | bytes 196616 | tf_op jit(solution)/shard_map/ppermute | solution.py:90
  94.3 5.8 %collective-permute-start.39 = (bf16[8,32,128]{2,1,0:T(8,128)(2,1)S(1)}, bf16[8,32,128]{2,1,0:T(8,128)(2,1)S(1)}, u32[]{:S(2)}, u32[]{:S(2)}) collective-permute-start(bf16[8,32,128]{2,1,0:T(8,128)(2,1)S(1)} %collective-permute-done.38), channel_id=1, source_target_pairs={{0,1},{1,0},{2,3},{3,2},{4,5},{5,4},{6,7},{7,6},{8,9},{9,8},{10,11... | collective-permute-start | bytes 196616 | tf_op jit(solution)/shard_map/ppermute | solution.py:90
  99.5 1.3 collective-permute-start.41
  99.6 1.4 collective-permute-start.43
  101.6 8.6 %collective-permute-start.44 = (bf16[4,32,128]{2,1,0:T(8,128)(2,1)S(1)}, bf16[4,32,128]{2,1,0:T(8,128)(2,1)S(1)}, u32[]{:S(2)}, u32[]{:S(2)}) collective-permute-start(bf16[4,32,128]{2,1,0:T(8,128)(2,1)S(1)} %get-tuple-element.46), channel_id=1, source_target_pairs={{0,8},{8,0},{16,24},{24,16},{1,9},{9,1},{17,25},{25,17},{2,10},{10... | collective-permute-start | bytes 98312 | tf_op jit(solution)/shard_map/ppermute | solution.py:90
  102.9 7.3 %collective-permute-start.45 = (bf16[4,32,128]{2,1,0:T(8,128)(2,1)S(1)}, bf16[4,32,128]{2,1,0:T(8,128)(2,1)S(1)}, u32[]{:S(2)}, u32[]{:S(2)}) collective-permute-start(bf16[4,32,128]{2,1,0:T(8,128)(2,1)S(1)} %get-tuple-element.47), channel_id=1, source_target_pairs={{0,16},{8,24},{16,0},{24,8},{1,17},{9,25},{17,1},{25,9},{2,18},{10... | collective-permute-start | bytes 98312 | tf_op jit(solution)/shard_map/ppermute | solution.py:90
  104.6 5.7 %collective-permute-start.46 = (bf16[4,32,128]{2,1,0:T(8,128)(2,1)S(1)}, bf16[4,32,128]{2,1,0:T(8,128)(2,1)S(1)}, u32[]{:S(2)}, u32[]{:S(2)}) collective-permute-start(bf16[4,32,128]{2,1,0:T(8,128)(2,1)S(1)} %get-tuple-element.48), channel_id=1, source_target_pairs={{0,24},{8,16},{16,8},{24,0},{1,25},{9,17},{17,9},{25,1},{2,26},{10... | collective-permute-start | bytes 98312 | tf_op jit(solution)/shard_map/ppermute | solution.py:90
  113.0 4.8 %collective-permute-start.47 = (f32[96,96]{1,0:T(8,128)S(1)}, f32[96,96]{1,0:T(8,128)S(1)}, u32[]{:S(2)}, u32[]{:S(2)}) collective-permute-start(f32[96,96]{1,0:T(8,128)S(1)} %inner.1), channel_id=1, source_target_pairs={{0,2},{1,3},{2,0},{3,1},{4,6},{5,7},{6,4},{7,5},{8,10},{9,11},{10,... | collective-permute-start | bytes 110600 | tf_op jit(solution)/shard_map/ppermute | solution.py:90
  114.2 6.0 %collective-permute-start.48 = (f32[96,96]{1,0:T(8,128)S(1)}, f32[96,96]{1,0:T(8,128)S(1)}, u32[]{:S(2)}, u32[]{:S(2)}) collective-permute-start(f32[96,96]{1,0:T(8,128)S(1)} %inner.1), channel_id=1, source_target_pairs={{0,4},{1,5},{2,6},{3,7},{4,0},{5,1},{6,2},{7,3},{8,12},{9,13},{10,... | collective-permute-start | bytes 110600 | tf_op jit(solution)/shard_map/ppermute | solution.py:90
  115.7 6.7 %collective-permute-start.49 = (f32[96,96]{1,0:T(8,128)S(1)}, f32[96,96]{1,0:T(8,128)S(1)}, u32[]{:S(2)}, u32[]{:S(2)}) collective-permute-start(f32[96,96]{1,0:T(8,128)S(1)} %inner.1), channel_id=1, source_target_pairs={{0,6},{1,7},{2,4},{3,5},{4,2},{5,3},{6,0},{7,1},{8,14},{9,15},{10,... | collective-permute-start | bytes 110600 | tf_op jit(solution)/shard_map/ppermute | solution.py:90
  117.4 6.1 %collective-permute-start.54 = (bf16[8,32,128]{2,1,0:T(8,128)(2,1)S(1)}, bf16[8,32,128]{2,1,0:T(8,128)(2,1)S(1)}, u32[]{:S(2)}, u32[]{:S(2)}) collective-permute-start(bf16[8,32,128]{2,1,0:T(8,128)(2,1)S(1)} %get-tuple-element.50), channel_id=1, source_target_pairs={{0,1},{1,0},{2,3},{3,2},{4,5},{5,4},{6,7},{7,6},{8,9},{9,8},{10,11... | collective-permute-start | bytes 196616 | tf_op jit(solution)/shard_map/ppermute | solution.py:90
  117.4 6.1 %collective-permute-start.55 = (bf16[8,32,128]{2,1,0:T(8,128)(2,1)S(1)}, bf16[8,32,128]{2,1,0:T(8,128)(2,1)S(1)}, u32[]{:S(2)}, u32[]{:S(2)}) collective-permute-start(bf16[8,32,128]{2,1,0:T(8,128)(2,1)S(1)} %get-tuple-element.50), channel_id=1, source_target_pairs={{0,2},{1,3},{2,0},{3,1},{4,6},{5,7},{6,4},{7,5},{8,10},{9,11},{10,... | collective-permute-start | bytes 196616 | tf_op jit(solution)/shard_map/ppermute | solution.py:90
  117.8 8.7 %collective-permute-start.57 = (bf16[8,32,128]{2,1,0:T(8,128)(2,1)S(1)}, bf16[8,32,128]{2,1,0:T(8,128)(2,1)S(1)}, u32[]{:S(2)}, u32[]{:S(2)}) collective-permute-start(bf16[8,32,128]{2,1,0:T(8,128)(2,1)S(1)} %get-tuple-element.50), channel_id=1, source_target_pairs={{0,4},{1,5},{2,6},{3,7},{4,0},{5,1},{6,2},{7,3},{8,12},{9,13},{10,... | collective-permute-start | bytes 196616 | tf_op jit(solution)/shard_map/ppermute | solution.py:90
  120.3 6.3 %collective-permute-start.59 = (bf16[8,32,128]{2,1,0:T(8,128)(2,1)S(1)}, bf16[8,32,128]{2,1,0:T(8,128)(2,1)S(1)}, u32[]{:S(2)}, u32[]{:S(2)}) collective-permute-start(bf16[8,32,128]{2,1,0:T(8,128)(2,1)S(1)} %get-tuple-element.50), channel_id=1, source_target_pairs={{0,6},{1,7},{2,4},{3,5},{4,2},{5,3},{6,0},{7,1},{8,14},{9,15},{10,... | collective-permute-start | bytes 196616 | tf_op jit(solution)/shard_map/ppermute | solution.py:90
  122.4 4.7 %collective-permute-start.50 = (f32[96,96]{1,0:T(8,128)S(1)}, f32[96,96]{1,0:T(8,128)S(1)}, u32[]{:S(2)}, u32[]{:S(2)}) collective-permute-start(f32[96,96]{1,0:T(8,128)S(1)} %add_add_fusion.1), channel_id=1, source_target_pairs={{0,1},{1,0},{2,3},{3,2},{4,5},{5,4},{6,7},{7,6},{8,9},{9,8},{10,11... | collective-permute-start | bytes 110600 | tf_op jit(solution)/shard_map/ppermute | solution.py:90
  123.5 6.5 %collective-permute-start.56 = (bf16[8,32,128]{2,1,0:T(8,128)(2,1)S(1)}, bf16[8,32,128]{2,1,0:T(8,128)(2,1)S(1)}, u32[]{:S(2)}, u32[]{:S(2)}) collective-permute-start(bf16[8,32,128]{2,1,0:T(8,128)(2,1)S(1)} %collective-permute-done.55), channel_id=1, source_target_pairs={{0,1},{1,0},{2,3},{3,2},{4,5},{5,4},{6,7},{7,6},{8,9},{9,8},{10,11... | collective-permute-start | bytes 196616 | tf_op jit(solution)/shard_map/ppermute | solution.py:90
  126.5 4.1 %collective-permute-start.58 = (bf16[8,32,128]{2,1,0:T(8,128)(2,1)S(1)}, bf16[8,32,128]{2,1,0:T(8,128)(2,1)S(1)}, u32[]{:S(2)}, u32[]{:S(2)}) collective-permute-start(bf16[8,32,128]{2,1,0:T(8,128)(2,1)S(1)} %collective-permute-done.57), channel_id=1, source_target_pairs={{0,1},{1,0},{2,3},{3,2},{4,5},{5,4},{6,7},{7,6},{8,9},{9,8},{10,11... | collective-permute-start | bytes 196616 | tf_op jit(solution)/shard_map/ppermute | solution.py:90
  126.5 4.2 %collective-permute-start.60 = (bf16[8,32,128]{2,1,0:T(8,128)(2,1)S(1)}, bf16[8,32,128]{2,1,0:T(8,128)(2,1)S(1)}, u32[]{:S(2)}, u32[]{:S(2)}) collective-permute-start(bf16[8,32,128]{2,1,0:T(8,128)(2,1)S(1)} %collective-permute-done.59), channel_id=1, source_target_pairs={{0,1},{1,0},{2,3},{3,2},{4,5},{5,4},{6,7},{7,6},{8,9},{9,8},{10,11... | collective-permute-start | bytes 196616 | tf_op jit(solution)/shard_map/ppermute | solution.py:90
  127.1 7.3 %collective-permute-start.51 = (f32[96,96]{1,0:T(8,128)S(1)}, f32[96,96]{1,0:T(8,128)S(1)}, u32[]{:S(2)}, u32[]{:S(2)}) collective-permute-start(f32[96,96]{1,0:T(8,128)S(1)} %add.52), channel_id=1, source_target_pairs={{0,8},{8,0},{16,24},{24,16},{1,9},{9,1},{17,25},{25,17},{2,10},{10... | collective-permute-start | bytes 110600 | tf_op jit(solution)/shard_map/ppermute | solution.py:90
  128.4 6.6 %collective-permute-start.52 = (f32[96,96]{1,0:T(8,128)S(1)}, f32[96,96]{1,0:T(8,128)S(1)}, u32[]{:S(2)}, u32[]{:S(2)}) collective-permute-start(f32[96,96]{1,0:T(8,128)S(1)} %add.52), channel_id=1, source_target_pairs={{0,16},{8,24},{16,0},{24,8},{1,17},{9,25},{17,1},{25,9},{2,18},{10... | collective-permute-start | bytes 110600 | tf_op jit(solution)/shard_map/ppermute | solution.py:90
  130.0 5.5 %collective-permute-start.53 = (f32[96,96]{1,0:T(8,128)S(1)}, f32[96,96]{1,0:T(8,128)S(1)}, u32[]{:S(2)}, u32[]{:S(2)}) collective-permute-start(f32[96,96]{1,0:T(8,128)S(1)} %add.52), channel_id=1, source_target_pairs={{0,24},{8,16},{16,8},{24,0},{1,25},{9,17},{17,9},{25,1},{2,26},{10... | collective-permute-start | bytes 110600 | tf_op jit(solution)/shard_map/ppermute | solution.py:90
  131.4 6.3 %collective-permute-start.61 = (bf16[16,32,128]{2,1,0:T(8,128)(2,1)S(1)}, bf16[16,32,128]{2,1,0:T(8,128)(2,1)S(1)}, u32[]{:S(2)}, u32[]{:S(2)}) collective-permute-start(bf16[16,32,128]{2,1,0:T(8,128)(2,1)S(1)} %select_all.1.s_ref), channel_id=1, source_target_pairs={{0,8},{8,0},{16,24},{24,16},{1,9},{9,1},{17,25},{25,17},{2,10},{10... | collective-permute-start | bytes 393224 | tf_op jit(solution)/shard_map/ppermute | solution.py:90
  132.7 7.8 %collective-permute-start.62 = (bf16[16,32,128]{2,1,0:T(8,128)(2,1)S(1)}, bf16[16,32,128]{2,1,0:T(8,128)(2,1)S(1)}, u32[]{:S(2)}, u32[]{:S(2)}) collective-permute-start(bf16[16,32,128]{2,1,0:T(8,128)(2,1)S(1)} %select_all.1.s_ref), channel_id=1, source_target_pairs={{0,16},{8,24},{16,0},{24,8},{1,17},{9,25},{17,1},{25,9},{2,18},{10... | collective-permute-start | bytes 393224 | tf_op jit(solution)/shard_map/ppermute | solution.py:90
  134.4 6.1 %collective-permute-start.63 = (bf16[16,32,128]{2,1,0:T(8,128)(2,1)S(1)}, bf16[16,32,128]{2,1,0:T(8,128)(2,1)S(1)}, u32[]{:S(2)}, u32[]{:S(2)}) collective-permute-start(bf16[16,32,128]{2,1,0:T(8,128)(2,1)S(1)} %select_all.1.s_ref), channel_id=1, source_target_pairs={{0,24},{8,16},{16,8},{24,0},{1,25},{9,17},{17,9},{25,1},{2,26},{10... | collective-permute-start | bytes 393224 | tf_op jit(solution)/shard_map/ppermute | solution.py:90
  (7 other events, 106.6 us)

commit v2 on v1

v2 whole, which is shorter than its diff:
```python
import functools

import jax
import jax.numpy as jnp
from jax import lax
from jax.experimental import pallas as pl
from jax.experimental.pallas import tpu as pltpu
from jax.sharding import PartitionSpec as P

F32 = jnp.float32
BF16 = jnp.bfloat16
HIGH = lax.Precision.HIGHEST
VM = pl.BlockSpec(memory_space=pltpu.VMEM)
SM = pl.BlockSpec(memory_space=pltpu.SMEM)


def nn(a, b):
    return lax.dot_general(a, b, (((1,), (0,)), ((), ())), precision=HIGH, preferred_element_type=F32)


def nt(a, b):
    return lax.dot_general(a, b, (((1,), (1,)), ((), ())), precision=HIGH, preferred_element_type=F32)


def nt16(a, b):
    return lax.dot_general(a, b, (((1,), (1,)), ((), ())), preferred_element_type=F32)


def pair_sum(values):
    while len(values) > 1:
        values = [values[i] + values[i + 1] for i in range(0, len(values), 2)]
    return values[0]


def factor(mats):
    size = mats[0].shape[0]
    rows = lax.broadcasted_iota(jnp.int32, (size, size), 0)
    cols = lax.broadcasted_iota(jnp.int32, (size, size), 1)
    eye = (rows == cols).astype(F32)
    work = [jnp.concatenate([m, eye], axis=1) for m in mats]
    kept = [[] for _ in mats]
    for j in range(size):
        for n in range(len(mats)):
            m = work[n]
            row = m[j : j + 1, :] * lax.rsqrt(m[j : j + 1, j : j + 1])
            col = m[:, j : j + 1] * lax.rsqrt(m[j : j + 1, j : j + 1])
            kept[n].append(row)
            work[n] = m - col * row
    out = []
    for n in range(len(mats)):
        full = jnp.concatenate(kept[n], axis=0)
        out.append((jnp.where(cols >= rows, full[:, :size], 0.0), full[:, size:]))
    return out


def cut3(v):
    high = v.astype(BF16)
    rest = v - high.astype(F32)
    mid = rest.astype(BF16)
    return high, mid, (rest - mid.astype(F32)).astype(BF16)


def join3(parts):
    high, mid, low = (p.astype(F32) for p in parts)
    return high + (mid + low)


def call(kernel, outs, args, specs, scratch=(), vmem=8, name=None, cost=None):
    return pl.pallas_call(
        kernel,
        out_shape=outs,
        in_specs=specs,
        out_specs=jax.tree.map(lambda _: VM, outs),
        scratch_shapes=list(scratch),
        compiler_params=pltpu.CompilerParams(vmem_limit_bytes=vmem << 20),
        cost_estimate=cost,
        name=name,
    )(*args)


def xor(size, m):
    return [(i, i ^ m) for i in range(size)]


EXTRA = 3


def body(schur, inverse_blocks, loads, share_list, multiplicity):
    inverse = inverse_blocks[0]
    local_rows, order = schur.shape[1:]
    owned, block = inverse.shape[0], inverse.shape[-1]
    cases = loads.shape[1]
    share = share_list[0]
    subs, slots = share.shape
    parts = lax.axis_size("blk")
    weighting = 1.0 / (order * subs)
    weight = 1.0 / multiplicity[0].astype(F32)
    peers = list(range(1, subs))
    n_in = len(peers)
    cube = (owned, cases, block)
    pad = block - 3 * cases

    def sds(shape, dtype=F32):
        return jax.ShapeDtypeStruct(shape, dtype)

    def permute(v, axis, m):
        return lax.ppermute(v, axis, xor(lax.axis_size(axis), m))

    def to_subs(vs):
        return [permute(v, "sub", m) for m, v in zip(peers, vs)]

    def padded(v):
        return jnp.concatenate([v, jnp.zeros((cases, block - v.shape[1]), v.dtype)], axis=1)

    def me_blk():
        return lax.axis_index("blk")

    def me_sub():
        return lax.axis_index("sub")


    def masked(share_ref, own, dtype, outs):
        for m, o_ref in zip(peers, outs):
            for s in range(slots):
                k = share_ref[me_sub() ^ m, s]
                here = jnp.logical_and(k >= 0, k // owned == me_blk())
                value = own(jnp.where(here, k % owned, 0))
                o_ref[s] = jnp.where(here, value, jnp.zeros_like(value)).astype(dtype)

    def route(outs, extra=None):
        arrived = to_subs(outs)
        dtype = arrived[0].dtype
        total = n_in * slots + (extra is not None)
        half = (total + 1) // 2

        def kernel(*refs):
            ins, (keep_ref, send_ref, all_ref) = refs[:-3], refs[-3:]
            side = me_blk() % 2
            for i in range(2 * half):
                at = all_ref.at[i // half, i % half]
                if i < n_in * slots:
                    at[...] = ins[i // slots][i % slots]
                elif i < total:
                    at[...] = pair_sum([ins[-1][...]] + [r[slots] for r in ins[:n_in]])
                else:
                    at[...] = jnp.zeros((cases, block), dtype)
            keep_ref[...] = all_ref[side]
            send_ref[...] = all_ref[1 - side]

        args = tuple(arrived) + (() if extra is None else (extra,))
        shape = (half, cases, block)
        keep, send = call(
            kernel,
            (sds(shape, dtype), sds(shape, dtype)),
            args,
            [VM] * len(args),
            scratch=[pltpu.VMEM((2,) + shape, dtype)],
            name="split",
        )
        keep = keep + permute(send, "blk", 1)
        far = [permute(keep, "blk", 2 * m) for m in reversed(range(1, parts // 2))]
        keep = pair_sum([keep] + far[::-1])
        return keep, permute(keep, "blk", 1)

    def routed(refs, all_ref):
        side = me_blk() % 2
        all_ref[side] = refs[0][...]
        all_ref[1 - side] = refs[1][...]
        half = all_ref.shape[1]
        return lambda i: all_ref[i // half, i % half]

    def add_shared(share_ref, acc_ref, arrived):
        for n, m in enumerate(peers):
            for s in range(slots):
                k = share_ref[me_sub() ^ m, s]

                @pl.when(jnp.logical_and(k >= 0, k // owned == me_blk()))
                def _():
                    acc_ref[k % owned] += arrived(n, s).astype(F32)


    def gather(v):
        far = {m: permute(v, "blk", 2 * m) for m in reversed(range(1, parts // 2))}
        far[0] = v
        both = []
        for m in range(parts // 2):
            both += [far[m], permute(far[m], "blk", 1)]
        near = max(2, parts // 2)
        rest = both[near:]
        return [jnp.concatenate(both[:near], axis=0)] + ([jnp.concatenate(rest, axis=0)] if rest else [])

    def piece_reader(p_refs, stride):
        sizes = [r.shape[0] // stride for r in p_refs]

        def read(k):
            q, r = (k // owned) ^ me_blk(), k % owned
            value = p_refs[0][jnp.minimum(q, sizes[0] - 1) * stride + r]
            if len(p_refs) > 1:
                other = p_refs[1][jnp.maximum(q - sizes[0], 0) * stride + r]
                value = jnp.where(q < sizes[0], value, other)
            return value

        return read

    def extra_sum(p_refs, stride):
        found = []
        for r in p_refs:
            for q in range(r.shape[0] // stride):
                found.append(join3([r[q * stride + owned + e] for e in range(EXTRA)]))
        return pair_sum(found)

    def select(pieces, extra, joined):
        stride = owned + (EXTRA if extra else 0)
        n_p = len(pieces)
        more = EXTRA if extra else 0

        def kernel(share_ref, *refs):
            p_refs, outs = refs[:n_p], refs[n_p:]
            read = piece_reader(p_refs, stride)
            for n, m in enumerate(peers):
                for s in range(slots):
                    k = share_ref[me_sub() ^ m, s]
                    value = read(jnp.maximum(k, 0))
                    value = jnp.where(k >= 0, value, jnp.zeros_like(value))
                    if joined:
                        outs[0][n * slots + s] = value
                    else:
                        outs[n][s] = value
            if extra:
                total = extra_sum(p_refs, stride)
                outs[-1][...] = total
                for e, part in enumerate(cut3(total)):
                    for o in outs[:-1]:
                        o[o.shape[0] - EXTRA + e] = part

        if joined:
            outs = [sds((n_in * slots + more, cases, block), BF16)]
        else:
            outs = [sds((slots + more, cases, block), BF16) for _ in peers]
        if extra:
            outs.append(sds((cases, block)))
        return call(kernel, tuple(outs), (share, *pieces), [SM] + [VM] * n_p, name="select")


    def open_(raw):
        def kernel(share_ref, l_ref, b_ref, g_ref, *outs):
            value = l_ref[...]
            for k in range(owned):
                b_ref[k] = value[:, k * block : (k + 1) * block]
            gram = padded(nt(value, value) * weighting)
            g_ref[...] = gram
            masked(share_ref, lambda k: b_ref[k], F32, outs)
            for o_ref in outs:
                o_ref[slots] = gram

        outs = (sds(cube), sds((cases, block))) + tuple(sds((slots + 1, cases, block)) for _ in peers)
        return call(kernel, outs, (share, raw), [SM, VM], name="open")

    def fetch(full, after):
        def kernel(m_ref, a_ref, o_ref, sem):
            copy = pltpu.make_async_copy(m_ref, o_ref, sem)
            copy.start()
            copy.wait()

        anywhere = pl.BlockSpec(memory_space=pl.ANY)
        cost = pl.CostEstimate(flops=0, transcendentals=0, bytes_accessed=2 * full.size * 2)
        return call(
            kernel,
            sds(full.shape, full.dtype),
            (full, after),
            [anywhere, anywhere],
            scratch=[pltpu.SemaphoreType.DMA],
            name="fetch",
            cost=cost,
        )

    def start(own, arrived):
        half = arrived[0].shape[0]

        def kernel(share_ref, w_ref, own_ref, inv_ref, a0, a1, b_ref, x_ref, h_ref, f_ref, all_ref):
            at = routed((a0, a1), all_ref)
            ((up, inv_low),) = factor([at(n_in * slots)[:, :cases]])
            f_ref[...] = up
            b_ref[...] = own_ref[...]
            add_shared(share_ref, b_ref, lambda n, s: at(n * slots + s))
            for k in range(owned):
                value = nn(inv_low, b_ref[k])
                b_ref[k] = value
                value = nt(value, inv_ref[k]) * w_ref[k]
                x_ref[k] = value
                h_ref[k] = value.astype(BF16)

        outs = (sds(cube), sds(cube), sds(cube, BF16), sds((cases, cases)))
        return call(
            kernel,
            outs,
            (share, weight, own, inverse, *arrived),
            [SM, SM] + [VM] * 4,
            scratch=[pltpu.VMEM((2, half, cases, block), F32)],
            name="start",
        )

    def middle(own, base, arrived):
        half = arrived[0].shape[0]

        def kernel(share_ref, w_ref, own_ref, base_ref, inv_ref, a0, a1, x_ref, h_ref, k_ref, all_ref):
            at = routed((a0, a1), all_ref)
            k_ref[...] = own_ref[...]
            add_shared(share_ref, k_ref, lambda n, s: at(n * slots + s))
            for k in range(owned):
                value = nt(k_ref[k], inv_ref[k]) * w_ref[k]
                x_ref[k] = value
                h_ref[k] = value.astype(BF16)
            wide = lambda ref: jnp.concatenate([ref[k] for k in range(owned)], axis=1)
            weighted = lambda ref: jnp.concatenate([ref[k] * w_ref[k] for k in range(owned)], axis=1)
            g0 = nt(weighted(base_ref), wide(base_ref))
            g1 = nt(weighted(k_ref), jnp.concatenate([wide(base_ref), wide(k_ref)], axis=0))
            gram = padded(jnp.concatenate([g0, g1], axis=1) * weighting)
            for e, part in enumerate(cut3(gram)):
                h_ref[owned + e] = part

        outs = (sds(cube), sds((owned + EXTRA, cases, block), BF16), sds(cube))
        return call(
            kernel,
            outs,
            (share, weight, own, base, inverse, *arrived),
            [SM, SM] + [VM] * 5,
            scratch=[pltpu.VMEM((2, half, cases, block), BF16)],
            name="middle",
        )

    def multiply(matrix, pieces, first, stride, before):
        count = pieces.shape[0] // stride

        def kernel(m_ref, p_ref, *rest):
            y_ref = rest[-1]
            total = rest[0][...] if len(rest) > 1 else jnp.zeros((cases, local_rows), F32)
            for q in range(count):
                z = jnp.concatenate([p_ref[q * stride + i] for i in range(owned)], axis=1)
                at = pl.multiple_of(((first + q) ^ me_blk()) * local_rows, local_rows)
                total = total + nt16(z, m_ref[:, pl.ds(at, local_rows)])
            y_ref[...] = total

        args = (matrix, pieces) + (() if before is None else (before,))
        cost = pl.CostEstimate(
            flops=2 * cases * local_rows * local_rows * count, transcendentals=0, bytes_accessed=2 * local_rows * local_rows * count
        )
        return call(kernel, sds((cases, local_rows)), args, [VM] * len(args), name="multiply", cost=cost)

    def shared_product(share_ref, m_ref, total, ins):
        for m, a_ref in zip(peers, ins):
            z = jnp.concatenate([a_ref[s] for s in range(slots)], axis=1)
            cols = []
            for s in range(slots):
                at = pl.multiple_of(jnp.maximum(share_ref[me_sub() ^ m, s], 0) * block, block)
                cols.append(m_ref[:, pl.ds(at, block)])
            total = total + nt16(z, jnp.concatenate(cols, axis=1))
        return total

    def tail_route(matrix, part, arrived):
        def kernel(share_ref, m_ref, part_ref, *rest):
            ins, y_ref, outs = rest[:n_in], rest[n_in], rest[n_in + 1 :]
            total = shared_product(share_ref, m_ref, part_ref[...], ins)
            for k in range(owned):
                y_ref[k] = total[:, k * block : (k + 1) * block]
            masked(share_ref, lambda k: y_ref[k], BF16, outs)

        outs = (sds(cube),) + tuple(sds((slots, cases, block), BF16) for _ in peers)
        return call(kernel, outs, (share, matrix, part, *arrived), [SM] + [VM] * (2 + n_in), name="tail_route")

    def tail_gram(matrix, part, arrived, b, k1):
        def kernel(share_ref, m_ref, part_ref, b_ref, k_ref, *rest):
            ins, h_ref = rest[:n_in], rest[n_in]
            total = shared_product(share_ref, m_ref, part_ref[...], ins)
            for k in range(owned):
                h_ref[k] = total[:, k * block : (k + 1) * block].astype(BF16)
            wide = lambda ref: jnp.concatenate([ref[k] for k in range(owned)], axis=1)
            gram = nt(total, jnp.concatenate([wide(b_ref), wide(k_ref), total], axis=0))
            for e, part in enumerate(cut3(padded(gram * weighting))):
                h_ref[owned + e] = part

        outs = sds((owned + EXTRA, cases, block), BF16)
        return call(
            kernel, outs, (share, matrix, part, b, k1, *arrived), [SM] + [VM] * (4 + n_in), name="tail_gram"
        )

    def gram_of(g_ref, ins):
        return pair_sum([g_ref[...]] + [join3([r[r.shape[0] - EXTRA + e] for e in range(EXTRA)]) for r in ins])

    n = cases

    def early(g01, arrived):
        def kernel(g_ref, *rest):
            ins, (u00_ref, i00_ref, l10_ref, u11_ref, i11_ref, j1_ref, r1_ref) = rest[:n_in], rest[n_in:]
            g = gram_of(g_ref, ins)
            g00, g10, g11 = g[:, :n], g[:, n : 2 * n], g[:, 2 * n : 3 * n]
            (u00, i00), (_, j1) = factor([g00, g11])
            l10 = nt(g10, i00)
            ((u11, i11),) = factor([g11 - nt(l10, l10)])
            u00_ref[...] = u00
            i00_ref[...] = i00
            l10_ref[...] = l10
            u11_ref[...] = u11
            i11_ref[...] = i11
            j1_ref[...] = j1
            r1_ref[...] = nt(g10.T, j1)

        outs = tuple(sds((n, n)) for _ in range(7))
        cost = pl.CostEstimate(flops=10**8, transcendentals=0, bytes_accessed=10**7)
        return call(kernel, outs, (g01, *arrived), [VM] * (1 + n_in), name="early", cost=cost)

    def finish(g2, mine_slots, their_slots, known, upper, x0, in0, x1, in1):
        n_known = len(known)

        def kernel(share_ref, g_ref, s_ref, f_ref, x0_ref, x1_ref, *rest):
            known_refs, rest = rest[:n_known], rest[n_known:]
            theirs, in0_refs, in1_refs = rest[:n_in], rest[n_in : 2 * n_in], rest[2 * n_in : 3 * n_in]
            sol_ref, mis_ref, all_ref, z0_ref, z1_ref = rest[3 * n_in :]
            u00, i00, l10, u11, i11, j1, r1 = (r[...] for r in known_refs)
            z0_ref[...] = x0_ref[...]
            add_shared(share_ref, z0_ref, lambda p, s: in0_refs[p][s])
            z1_ref[...] = x1_ref[...]
            add_shared(share_ref, z1_ref, lambda p, s: in1_refs[p][s])
            all_ref[me_sub()] = s_ref[...]
            for m, t_ref in zip(peers, theirs):
                all_ref[me_sub() ^ m] = t_ref[...]
            cross = jnp.zeros((n, n), F32)
            for i in range(subs):
                for j in range(i + 1, subs):
                    at = ((i ^ j) - 1) * slots
                    left = jnp.concatenate([all_ref[i, at + s] for s in range(slots)], axis=1)
                    right = jnp.concatenate([all_ref[j, at + s] for s in range(slots)], axis=1)
                    cross = cross + nt16(left, right)
            g = gram_of(g_ref, theirs)
            g20, g21 = g[:, :n], g[:, n : 2 * n]
            g22 = g[:, 2 * n : 3 * n] + (cross + cross.T) * weighting
            l20 = nt(g20, i00)
            k21 = nt(g21, j1)
            l21 = nt(g21 - nt(l20, l10), i11)
            (u22, _), (_, j2) = factor([g22 - nt(l20, l20) - nt(l21, l21), g22 - nt(k21, k21)])
            r2 = nt(g20.T - nt(r1, k21), j2)
            c1 = nn(r2, j2)
            c0 = nn(r1 - nn(c1, k21), j1)
            low = f_ref[...].T
            m0 = u00.T - nn(c0, l10) - nn(c1, l20)
            m1 = -nt(c0, u11) - nn(c1, l21)
            m2 = -nt(c1, u22)
            mixed = nn(low, jnp.concatenate([m0, m1, m2, c0, c1], axis=1))
            mis_ref[...] = mixed[:, : 3 * n]
            both = mixed[:, 3 * n :]
            for k in range(owned):
                z = jnp.concatenate([z0_ref[k], z1_ref[k]], axis=0)
                sol_ref[:, k * block : (k + 1) * block] = nn(both, z)

        outs = (sds((n, local_rows)), sds((n, 3 * n)))
        return call(
            kernel,
            outs,
            (share, g2, mine_slots, upper, x0, x1, *known, *their_slots, *in0, *in1),
            [SM] + [VM] * (5 + n_known + 3 * n_in),
            scratch=[
                pltpu.VMEM((subs,) + mine_slots.shape, BF16),
                pltpu.VMEM(cube, F32),
                pltpu.VMEM(cube, F32),
            ],
            name="finish",
        )

    def product(matrix, half, extra):
        stride = owned + (EXTRA if extra else 0)
        pieces = gather(half)
        chosen = select(pieces, extra, False)
        arrived = to_subs(chosen[:n_in])
        part, first = None, 0
        for p in pieces:
            part = multiply(matrix, p, first, stride, part)
            first += p.shape[0] // stride
        return part, arrived, chosen[-1]

    own, gram0, *outs = open_(loads[0])
    matrix = fetch(schur[0], gram0)
    b, x0, half, upper = start(own, route(outs, gram0))
    part, in0, _ = product(matrix, half, False)
    y0, *outs = tail_route(matrix, part, in0)
    x1, half, k1 = middle(y0, b, route(outs))
    part, in1, g01 = product(matrix, half, True)
    known = early(g01, in1)
    half = tail_gram(matrix, part, in1, b, k1)
    mine_slots, g2 = select(gather(half), True, True)
    solution, misfit = finish(g2, mine_slots, to_subs([mine_slots] * n_in), known, upper, x0, in0, x1, in1)
    return (solution[None], misfit)


def solution(mesh):
    placed = (
        P("sub", "blk", None),
        P("sub", "blk", None, None),
        P("sub", None, "blk"),
        P("sub", None, None),
        P("sub", "blk"),
    )
    return jax.shard_map(
        body, mesh=mesh, in_specs=placed, out_specs=(P("sub", None, "blk"), P()), check_vma=False
    )
```

time: 153 us -> 130 us (0.85)
  starting transfers between devices: 62.9 us -> 43.2 us
  local copies, waits for them, and re-layouts: 9.57 us -> 7.56 us
  Pallas kernels: 36.4 us -> 38.3 us
    ppermute x64 -> x46, starting transfers between devices: 62.9 us -> 43.2 us  [permute(): return lax.ppermute(v, axis, xor(lax.axis_size(axis), m))]
    unnamed x49 -> x24, local copies, waits for them, and re-layouts: 9.5 us -> 7.5 us
    pallas_call x14 -> x17, Pallas kernels: 36.4 us -> 38.3 us  [call(): pl.pallas_call(kernel, out_shape=outs, in_specs=specs, out_specs=jax.tree...]
    ppermute x64 -> x46, waiting for transfers between devices: 41.6 us -> 40.1 us  [permute(): return lax.ppermute(v, axis, xor(lax.axis_size(axis), m))]
  transfers between devices with their start and end apart: 64 -> 46, of which waited for: 27 -> 26; matrix products, arithmetic and copies ran while one was open for 1% -> 0% of each run, Pallas kernels for 7% -> 13%
where the time goes in v2:
time: 130 us
  starting transfers between devices  43.2 us (33%)
  waiting for transfers between devices  40.1 us (31%)
  Pallas kernels  38.3 us (29%)
  local copies, waits for them, and re-layouts  7.56 us (6%)
    ppermute x46, starting transfers between devices, permute(): return lax.ppermute(v, axis, xor(lax.axis_size(axis), m))  43.2 us
    ppermute x46, waiting for transfers between devices, permute(): return lax.ppermute(v, axis, xor(lax.axis_size(axis), m))  40.1 us
    pallas_call x17, Pallas kernels, call(): pl.pallas_call(kernel, out_shape=outs, in_specs=specs, out_specs=jax.tree...  38.3 us
    unnamed x24, local copies, waits for them, and re-layouts  7.5 us
  transfers between devices with their start and end apart: 46, of which 26 were waited for; matrix products, arithmetic and copies ran while one was open for 0% of the time, Pallas kernels for 13%

profile of v2, /device:TPU:0, one launch (start us, length us, event | category | flops | bytes accessed | tf_op | source)
XLA Modules:
  0.0 130.3 jit_solution(4909279031773239552)
XLA Ops:
  0.6 0.7 copy-done.2
  1.3 0.9 copy-done.4
  2.2 0.8 open.1
  3.0 3.0 %collective-permute-start = (f32[5,32,128]{2,1,0:T(8,128)S(1)}, f32[5,32,128]{2,1,0:T(8,128)S(1)}, u32[]{:S(2)}, u32[]{:S(2)}) collective-permute-start(f32[5,32,128]{2,1,0:T(8,128)S(1)} %get-tuple-element.42), channel_id=1, source_target_pairs={{0,8},{8,0},{16,24},{24,16},{1,9},{9,1},{17,25},{25,17},{2,10},{10... | collective-permute-start | bytes 245768 | tf_op jit(solution)/shard_map/ppermute | solution.py:107
  6.1 1.5 %collective-permute-start.1 = (f32[5,32,128]{2,1,0:T(8,128)S(1)}, f32[5,32,128]{2,1,0:T(8,128)S(1)}, u32[]{:S(2)}, u32[]{:S(2)}) collective-permute-start(f32[5,32,128]{2,1,0:T(8,128)S(1)} %get-tuple-element.43), channel_id=1, source_target_pairs={{0,16},{8,24},{16,0},{24,8},{1,17},{9,25},{17,1},{25,9},{2,18},{10... | collective-permute-start | bytes 245768 | tf_op jit(solution)/shard_map/ppermute | solution.py:107
  7.6 1.2 collective-permute-done.refs_0_
  8.8 2.6 %collective-permute-done.1.refs_1_ = f32[5,32,128]{2,1,0:T(8,128)S(1)} collective-permute-done((f32[5,32,128]{2,1,0:T(8,128)S(1)}, f32[5,32,128]{2,1,0:T(8,128)S(1)}, u32[]{:S(2)}, u32[]{:S(2)}) %collective-permute-start.1) | collective-permute-done | bytes 81952 | tf_op jit(solution)/shard_map/ppermute | solution.py:107
  11.4 1.5 %collective-permute-done.2.refs_2_ = f32[5,32,128]{2,1,0:T(8,128)S(1)} collective-permute-done((f32[5,32,128]{2,1,0:T(8,128)S(1)}, f32[5,32,128]{2,1,0:T(8,128)S(1)}, u32[]{:S(2)}, u32[]{:S(2)}) %collective-permute-start.2) | collective-permute-done | bytes 81952 | tf_op jit(solution)/shard_map/ppermute | solution.py:107
  13.1 1.3 %collective-permute-done.3 = f32[7,32,128]{2,1,0:T(8,128)S(1)} collective-permute-done((f32[7,32,128]{2,1,0:T(8,128)S(1)}, f32[7,32,128]{2,1,0:T(8,128)S(1)}, u32[]{:S(2)}, u32[]{:S(2)}) %collective-permute-start.3) | collective-permute-done | bytes 114720 | tf_op jit(solution)/shard_map/ppermute | solution.py:107
  14.4 1.6 %collective-permute-start.4 = (f32[7,32,128]{2,1,0:T(8,128)S(1)}, f32[7,32,128]{2,1,0:T(8,128)S(1)}, u32[]{:S(2)}, u32[]{:S(2)}) collective-permute-start(f32[7,32,128]{2,1,0:T(8,128)S(1)} %add.24), channel_id=1, source_target_pairs={{0,2},{1,3},{2,0},{3,1},{4,6},{5,7},{6,4},{7,5},{8,10},{9,11},{10,... | collective-permute-start | bytes 344072 | tf_op jit(solution)/shard_map/ppermute | solution.py:107
  16.0 2.6 %collective-permute-start.5 = (f32[7,32,128]{2,1,0:T(8,128)S(1)}, f32[7,32,128]{2,1,0:T(8,128)S(1)}, u32[]{:S(2)}, u32[]{:S(2)}) collective-permute-start(f32[7,32,128]{2,1,0:T(8,128)S(1)} %add.24), channel_id=1, source_target_pairs={{0,4},{1,5},{2,6},{3,7},{4,0},{5,1},{6,2},{7,3},{8,12},{9,13},{10,... | collective-permute-start | bytes 344072 | tf_op jit(solution)/shard_map/ppermute | solution.py:107
  18.8 5.8 %copy-done = bf16[1,1024,8192]{2,1,0:T(8,128)(2,1)S(1)} copy-done((bf16[1,1024,8192]{2,1,0:T(8,128)(2,1)S(1)}, bf16[1,1024,8192]{2,1,0:T(8,128)(2,1)}, u32[]{:S(2)}) %copy-start) | copy-done | bytes 16777240
  24.6 1.2 fetch.1.m_ref
  25.8 2.1 %collective-permute-done.5 = f32[7,32,128]{2,1,0:T(8,128)S(1)} collective-permute-done((f32[7,32,128]{2,1,0:T(8,128)S(1)}, f32[7,32,128]{2,1,0:T(8,128)S(1)}, u32[]{:S(2)}, u32[]{:S(2)}) %collective-permute-start.5) | collective-permute-done | bytes 114720 | tf_op jit(solution)/shard_map/ppermute | solution.py:107
  28.0 1.3 collective-permute-done.7.a1
  29.3 4.8 %start.1 = (f32[8,32,128]{2,1,0:T(8,128)S(1)}, f32[8,32,128]{2,1,0:T(8,128)S(1)}, bf16[8,32,128]{2,1,0:T(8,128)(2,1)S(1)}, f32[32,32]{1,0:T(8,128)S(1)}) custom-call(s32[4,4]{1,0:T(4,128)S(1)} %bitcast.11, f32[8]{0:T(128)S(1)} %divide_bitcast_fusion.w_ref, f32[8,32,128]{2,1,0:T(8,128)S(1)} %get-tuple-element.41.own_ref, f32[8,128,128]{2,1,0:T(8,128)S(1)} %bitcast.8, ...), custom_call_target="tpu_custom_call" | custom-call | tf_op jit(solution)/shard_map/start/pallas_call | solution.py:69
  34.3 2.0 %collective-permute-start.13 = (bf16[8,32,128]{2,1,0:T(8,128)(2,1)S(1)}, bf16[8,32,128]{2,1,0:T(8,128)(2,1)S(1)}, u32[]{:S(2)}, u32[]{:S(2)}) collective-permute-start(bf16[8,32,128]{2,1,0:T(8,128)(2,1)S(1)} %get-tuple-element.47), channel_id=1, source_target_pairs={{0,2},{1,3},{2,0},{3,1},{4,6},{5,7},{6,4},{7,5},{8,10},{9,11},{10,... | collective-permute-start | bytes 196616 | tf_op jit(solution)/shard_map/ppermute | solution.py:107
  36.4 1.0 collective-permute-start.8
  37.3 1.5 %collective-permute-start.10 = (bf16[8,32,128]{2,1,0:T(8,128)(2,1)S(1)}, bf16[8,32,128]{2,1,0:T(8,128)(2,1)S(1)}, u32[]{:S(2)}, u32[]{:S(2)}) collective-permute-start(bf16[8,32,128]{2,1,0:T(8,128)(2,1)S(1)} %get-tuple-element.47), channel_id=1, source_target_pairs={{0,6},{1,7},{2,4},{3,5},{4,2},{5,3},{6,0},{7,1},{8,14},{9,15},{10,... | collective-permute-start | bytes 196616 | tf_op jit(solution)/shard_map/ppermute | solution.py:107
  38.9 5.8 %collective-permute-done.8 = bf16[8,32,128]{2,1,0:T(8,128)(2,1)S(1)} collective-permute-done((bf16[8,32,128]{2,1,0:T(8,128)(2,1)S(1)}, bf16[8,32,128]{2,1,0:T(8,128)(2,1)S(1)}, u32[]{:S(2)}, u32[]{:S(2)}) %collective-permute-start.8) | collective-permute-done | bytes 65568 | tf_op jit(solution)/shard_map/ppermute | solution.py:107
  45.2 0.7 collective-permute-done.9
  46.1 0.7 select.3
  46.8 0.6 collective-permute-start.15
  47.4 0.7 collective-permute-start.16
  48.1 2.3 %collective-permute-start.17 = (bf16[4,32,128]{2,1,0:T(8,128)(2,1)S(1)}, bf16[4,32,128]{2,1,0:T(8,128)(2,1)S(1)}, u32[]{:S(2)}, u32[]{:S(2)}) collective-permute-start(bf16[4,32,128]{2,1,0:T(8,128)(2,1)S(1)} %get-tuple-element.50), channel_id=1, source_target_pairs={{0,24},{8,16},{16,8},{24,0},{1,25},{9,17},{17,9},{25,1},{2,26},{10... | collective-permute-start | bytes 98312 | tf_op jit(solution)/shard_map/ppermute | solution.py:107
  50.4 2.6 %multiply.4.rest_0_ = f32[32,1024]{1,0:T(8,128)S(1)} custom-call(bf16[1024,8192]{1,0:T(8,128)(2,1)S(1)} %fetch.1.m_ref, bf16[32,32,128]{2,1,0:T(8,128)(2,1)S(1)} %constant_dynamic-update-slice_fusion.4.p_ref.refs_0_), custom_call_target="tpu_custom_call" | custom-call | flops 268435456 | bytes 8388608 | tf_op jit(solution)/shard_map/multiply/pallas_call | solution.py:69
  52.9 2.6 %multiply.5.part_ref = f32[32,1024]{1,0:T(8,128)S(1)} custom-call(bf16[1024,8192]{1,0:T(8,128)(2,1)S(1)} %fetch.1.m_ref, bf16[32,32,128]{2,1,0:T(8,128)(2,1)S(1)} %constant_dynamic-update-slice_fusion.p_ref.refs_1_, f32[32,1024]{1,0:T(8,128)S(1)} %multiply.4.rest_0_), custom_call_target="tpu_custom_call" | custom-call | flops 268435456 | bytes 8388608 | tf_op jit(solution)/shard_map/multiply/pallas_call | solution.py:69
  55.6 1.7 %tail_route.1 = (f32[8,32,128]{2,1,0:T(8,128)S(1)}, bf16[4,32,128]{2,1,0:T(8,128)(2,1)S(1)}, bf16[4,32,128]{2,1,0:T(8,128)(2,1)S(1)}, bf16[4,32,128]{2,1,0:T(8,128)(2,1)S(1)}) custom-call(s32[4,4]{1,0:T(4,128)S(1)} %bitcast.13, bf16[1024,8192]{1,0:T(8,128)(2,1)S(1)} %fetch.1.m_ref, f32[32,1024]{1,0:T(8,128)S(1)} %multiply.5.part_ref, ...), custom_call_target="tpu_custom_call" | custom-call | tf_op jit(solution)/shard_map/tail_route/pallas_call | solution.py:69
  57.3 0.5 collective-permute-start.18
  57.8 0.7 collective-permute-start.19
  58.5 2.3 %collective-permute-start.20 = (bf16[4,32,128]{2,1,0:T(8,128)(2,1)S(1)}, bf16[4,32,128]{2,1,0:T(8,128)(2,1)S(1)}, u32[]{:S(2)}, u32[]{:S(2)}) collective-permute-start(bf16[4,32,128]{2,1,0:T(8,128)(2,1)S(1)} %get-tuple-element.55), channel_id=1, source_target_pairs={{0,24},{8,16},{16,8},{24,0},{1,25},{9,17},{17,9},{25,1},{2,26},{10... | collective-permute-start | bytes 98312 | tf_op jit(solution)/shard_map/ppermute | solution.py:107
  60.8 0.7 collective-permute-done.18.refs_0_
  61.9 1.5 %collective-permute-done.20.refs_2_ = bf16[4,32,128]{2,1,0:T(8,128)(2,1)S(1)} collective-permute-done((bf16[4,32,128]{2,1,0:T(8,128)(2,1)S(1)}, bf16[4,32,128]{2,1,0:T(8,128)(2,1)S(1)}, u32[]{:S(2)}, u32[]{:S(2)}) %collective-permute-start.20) | collective-permute-done | bytes 32800 | tf_op jit(solution)/shard_map/ppermute | solution.py:107
  63.4 1.2 collective-permute-done.21
  64.7 1.4 %collective-permute-start.22 = (bf16[6,32,128]{2,1,0:T(8,128)(2,1)S(1)}, bf16[6,32,128]{2,1,0:T(8,128)(2,1)S(1)}, u32[]{:S(2)}, u32[]{:S(2)}) collective-permute-start(bf16[6,32,128]{2,1,0:T(8,128)(2,1)S(1)} %add.28), channel_id=1, source_target_pairs={{0,2},{1,3},{2,0},{3,1},{4,6},{5,7},{6,4},{7,5},{8,10},{9,11},{10,... | collective-permute-start | bytes 147464 | tf_op jit(solution)/shard_map/ppermute | solution.py:107
  66.1 1.4 %collective-permute-start.23 = (bf16[6,32,128]{2,1,0:T(8,128)(2,1)S(1)}, bf16[6,32,128]{2,1,0:T(8,128)(2,1)S(1)}, u32[]{:S(2)}, u32[]{:S(2)}) collective-permute-start(bf16[6,32,128]{2,1,0:T(8,128)(2,1)S(1)} %add.28), channel_id=1, source_target_pairs={{0,4},{1,5},{2,6},{3,7},{4,0},{5,1},{6,2},{7,3},{8,12},{9,13},{10,... | collective-permute-start | bytes 147464 | tf_op jit(solution)/shard_map/ppermute | solution.py:107
  67.5 1.6 %collective-permute-start.24 = (bf16[6,32,128]{2,1,0:T(8,128)(2,1)S(1)}, bf16[6,32,128]{2,1,0:T(8,128)(2,1)S(1)}, u32[]{:S(2)}, u32[]{:S(2)}) collective-permute-start(bf16[6,32,128]{2,1,0:T(8,128)(2,1)S(1)} %add.28), channel_id=1, source_target_pairs={{0,6},{1,7},{2,4},{3,5},{4,2},{5,3},{6,0},{7,1},{8,14},{9,15},{10,... | collective-permute-start | bytes 147464 | tf_op jit(solution)/shard_map/ppermute | solution.py:107
  69.1 3.5 %collective-permute-done.23 = bf16[6,32,128]{2,1,0:T(8,128)(2,1)S(1)} collective-permute-done((bf16[6,32,128]{2,1,0:T(8,128)(2,1)S(1)}, bf16[6,32,128]{2,1,0:T(8,128)(2,1)S(1)}, u32[]{:S(2)}, u32[]{:S(2)}) %collective-permute-start.23) | collective-permute-done | bytes 49184 | tf_op jit(solution)/shard_map/ppermute | solution.py:107
  72.6 0.9 collective-permute-done.24
  73.6 1.2 collective-permute-done.25.a1
  74.8 2.3 %middle.1 = (f32[8,32,128]{2,1,0:T(8,128)S(1)}, bf16[11,32,128]{2,1,0:T(8,128)(2,1)S(1)}, f32[8,32,128]{2,1,0:T(8,128)S(1)}) custom-call(s32[4,4]{1,0:T(4,128)S(1)} %bitcast.14, f32[8]{0:T(128)S(1)} %divide_bitcast_fusion.w_ref, f32[8,32,128]{2,1,0:T(8,128)S(1)} %get-tuple-element.51.own_ref, f32[8,32,128]{2,1,0:T(8,128)S(1)} %get-tuple-element.52.base_ref.b_ref, ...), custom_call_target="tpu_custom_call" | custom-call | tf_op jit(solution)/shard_map/middle/pallas_call | solution.py:69
  77.3 0.8 collective-permute-start.31
  78.1 1.7 %collective-permute-start.26 = (bf16[11,32,128]{2,1,0:T(8,128)(2,1)S(1)}, bf16[11,32,128]{2,1,0:T(8,128)(2,1)S(1)}, u32[]{:S(2)}, u32[]{:S(2)}) collective-permute-start(bf16[11,32,128]{2,1,0:T(8,128)(2,1)S(1)} %get-tuple-element.58), channel_id=1, source_target_pairs={{0,4},{1,5},{2,6},{3,7},{4,0},{5,1},{6,2},{7,3},{8,12},{9,13},{10,... | collective-permute-start | bytes 270344 | tf_op jit(solution)/shard_map/ppermute | solution.py:107
  79.8 1.9 %collective-permute-start.28 = (bf16[11,32,128]{2,1,0:T(8,128)(2,1)S(1)}, bf16[11,32,128]{2,1,0:T(8,128)(2,1)S(1)}, u32[]{:S(2)}, u32[]{:S(2)}) collective-permute-start(bf16[11,32,128]{2,1,0:T(8,128)(2,1)S(1)} %get-tuple-element.58), channel_id=1, source_target_pairs={{0,6},{1,7},{2,4},{3,5},{4,2},{5,3},{6,0},{7,1},{8,14},{9,15},{10,... | collective-permute-start | bytes 270344 | tf_op jit(solution)/shard_map/ppermute | solution.py:107
  81.7 1.7 %collective-permute-done.31 = bf16[11,32,128]{2,1,0:T(8,128)(2,1)S(1)} collective-permute-done((bf16[11,32,128]{2,1,0:T(8,128)(2,1)S(1)}, bf16[11,32,128]{2,1,0:T(8,128)(2,1)S(1)}, u32[]{:S(2)}, u32[]{:S(2)}) %collective-permute-start.31) | collective-permute-done | bytes 90144 | tf_op jit(solution)/shard_map/ppermute | solution.py:107
  83.3 5.0 %collective-permute-done.26 = bf16[11,32,128]{2,1,0:T(8,128)(2,1)S(1)} collective-permute-done((bf16[11,32,128]{2,1,0:T(8,128)(2,1)S(1)}, bf16[11,32,128]{2,1,0:T(8,128)(2,1)S(1)}, u32[]{:S(2)}, u32[]{:S(2)}) %collective-permute-start.26) | collective-permute-done | bytes 90144 | tf_op jit(solution)/shard_map/ppermute | solution.py:107
  88.3 0.5 collective-permute-start.29
  88.9 0.7 collective-permute-done.27
  89.8 0.7 select.4
  90.5 1.4 %collective-permute-start.33 = (bf16[7,32,128]{2,1,0:T(8,128)(2,1)S(1)}, bf16[7,32,128]{2,1,0:T(8,128)(2,1)S(1)}, u32[]{:S(2)}, u32[]{:S(2)}) collective-permute-start(bf16[7,32,128]{2,1,0:T(8,128)(2,1)S(1)} %get-tuple-element.60), channel_id=1, source_target_pairs={{0,8},{8,0},{16,24},{24,16},{1,9},{9,1},{17,25},{25,17},{2,10},{10... | collective-permute-start | bytes 172040 | tf_op jit(solution)/shard_map/ppermute | solution.py:107
  91.9 1.5 %collective-permute-start.34 = (bf16[7,32,128]{2,1,0:T(8,128)(2,1)S(1)}, bf16[7,32,128]{2,1,0:T(8,128)(2,1)S(1)}, u32[]{:S(2)}, u32[]{:S(2)}) collective-permute-start(bf16[7,32,128]{2,1,0:T(8,128)(2,1)S(1)} %get-tuple-element.61), channel_id=1, source_target_pairs={{0,16},{8,24},{16,0},{24,8},{1,17},{9,25},{17,1},{25,9},{2,18},{10... | collective-permute-start | bytes 172040 | tf_op jit(solution)/shard_map/ppermute | solution.py:107
  93.3 0.7 collective-permute-start.35
  94.0 2.6 %multiply.6.rest_0_ = f32[32,1024]{1,0:T(8,128)S(1)} custom-call(bf16[1024,8192]{1,0:T(8,128)(2,1)S(1)} %fetch.1.m_ref, bf16[44,32,128]{2,1,0:T(8,128)(2,1)S(1)} %constant_dynamic-update-slice_fusion.12.p_ref.refs_0_), custom_call_target="tpu_custom_call" | custom-call | flops 268435456 | bytes 8388608 | tf_op jit(solution)/shard_map/multiply/pallas_call | solution.py:69
  96.6 2.6 %multiply.7.part_ref = f32[32,1024]{1,0:T(8,128)S(1)} custom-call(bf16[1024,8192]{1,0:T(8,128)(2,1)S(1)} %fetch.1.m_ref, bf16[44,32,128]{2,1,0:T(8,128)(2,1)S(1)} %constant_dynamic-update-slice_fusion.8.p_ref.refs_1_, f32[32,1024]{1,0:T(8,128)S(1)} %multiply.6.rest_0_), custom_call_target="tpu_custom_call" | custom-call | flops 268435456 | bytes 8388608 | tf_op jit(solution)/shard_map/multiply/pallas_call | solution.py:69
  99.2 2.3 %tail_gram.1 = bf16[11,32,128]{2,1,0:T(8,128)(2,1)S(1)} custom-call(s32[4,4]{1,0:T(4,128)S(1)} %bitcast.16, bf16[1024,8192]{1,0:T(8,128)(2,1)S(1)} %fetch.1.m_ref, f32[32,1024]{1,0:T(8,128)S(1)} %multiply.7.part_ref, f32[8,32,128]{2,1,0:T(8,128)S(1)} %get-tuple-element.52.base_ref.b_ref, f32[8,32,128]{2,1,0:T(8,128)S(1)} %get-tuple-element.59.k_ref, ...), custom_call_target="tpu_custom_call" | custom-call | tf_op jit(solution)/shard_map/tail_gram/pallas_call | solution.py:69
  101.6 2.3 %collective-permute-start.39 = (bf16[11,32,128]{2,1,0:T(8,128)(2,1)S(1)}, bf16[11,32,128]{2,1,0:T(8,128)(2,1)S(1)}, u32[]{:S(2)}, u32[]{:S(2)}) collective-permute-start(bf16[11,32,128]{2,1,0:T(8,128)(2,1)S(1)} %tail_gram.1), channel_id=1, source_target_pairs={{0,4},{1,5},{2,6},{3,7},{4,0},{5,1},{6,2},{7,3},{8,12},{9,13},{10,... | collective-permute-start | bytes 270344 | tf_op jit(solution)/shard_map/ppermute | solution.py:107
  103.9 1.6 %collective-permute-start.41 = (bf16[11,32,128]{2,1,0:T(8,128)(2,1)S(1)}, bf16[11,32,128]{2,1,0:T(8,128)(2,1)S(1)}, u32[]{:S(2)}, u32[]{:S(2)}) collective-permute-start(bf16[11,32,128]{2,1,0:T(8,128)(2,1)S(1)} %tail_gram.1), channel_id=1, source_target_pairs={{0,6},{1,7},{2,4},{3,5},{4,2},{5,3},{6,0},{7,1},{8,14},{9,15},{10,... | collective-permute-start | bytes 270344 | tf_op jit(solution)/shard_map/ppermute | solution.py:107
  105.5 5.8 %collective-permute-done.39 = bf16[11,32,128]{2,1,0:T(8,128)(2,1)S(1)} collective-permute-done((bf16[11,32,128]{2,1,0:T(8,128)(2,1)S(1)}, bf16[11,32,128]{2,1,0:T(8,128)(2,1)S(1)}, u32[]{:S(2)}, u32[]{:S(2)}) %collective-permute-start.39) | collective-permute-done | bytes 90144 | tf_op jit(solution)/shard_map/ppermute | solution.py:107
  113.2 0.7 select.5
  113.9 1.4 %collective-permute-start.43 = (bf16[15,32,128]{2,1,0:T(8,128)(2,1)S(1)}, bf16[15,32,128]{2,1,0:T(8,128)(2,1)S(1)}, u32[]{:S(2)}, u32[]{:S(2)}) collective-permute-start(bf16[15,32,128]{2,1,0:T(8,128)(2,1)S(1)} %get-tuple-element.64.s_ref), channel_id=1, source_target_pairs={{0,8},{8,0},{16,24},{24,16},{1,9},{9,1},{17,25},{25,17},{2,10},{10... | collective-permute-start | bytes 368648 | tf_op jit(solution)/shard_map/ppermute | solution.py:107
  115.3 1.5 %collective-permute-start.44 = (bf16[15,32,128]{2,1,0:T(8,128)(2,1)S(1)}, bf16[15,32,128]{2,1,0:T(8,128)(2,1)S(1)}, u32[]{:S(2)}, u32[]{:S(2)}) collective-permute-start(bf16[15,32,128]{2,1,0:T(8,128)(2,1)S(1)} %get-tuple-element.64.s_ref), channel_id=1, source_target_pairs={{0,16},{8,24},{16,0},{24,8},{1,17},{9,25},{17,1},{25,9},{2,18},{10... | collective-permute-start | bytes 368648 | tf_op jit(solution)/shard_map/ppermute | solution.py:107
  116.8 0.7 collective-permute-start.45
  117.5 5.8 %early.1 = (f32[32,32]{1,0:T(8,128)S(1)}, f32[32,32]{1,0:T(8,128)S(1)}, f32[32,32]{1,0:T(8,128)S(1)}, f32[32,32]{1,0:T(8,128)S(1)}, f32[32,32]{1,0:T(8,128)S(1)}...) custom-call(f32[32,128]{1,0:T(8,128)S(1)} %get-tuple-element.68.g_ref, ...), custom_call_target="tpu_custom_call" | custom-call | flops 100000000 | bytes 10000000 | tf_op jit(solution)/shard_map/early/pallas_call | solution.py:69
  123.3 6.9 %finish.1 = (f32[32,1024]{1,0:T(8,128)}, f32[32,96]{1,0:T(8,128)}) custom-call(s32[4,4]{1,0:T(4,128)S(1)} %bitcast.18, f32[32,128]{1,0:T(8,128)S(1)} %get-tuple-element.63.g_ref, bf16[15,32,128]{2,1,0:T(8,128)(2,1)S(1)} %get-tuple-element.64.s_ref, f32[32,32]{1,0:T(8,128)S(1)} %get-tuple-element.65.f_ref, f32[8,32,128]{2,1,0:T(8,128)S(1)} %get-tuple-element.66.x0_ref, ...), custom_call_target="tpu_custom_call" | custom-call | tf_op jit(solution)/shard_map/finish/pallas_call | solution.py:69
  (80 shorter events, 4.5 us)
Async XLA Ops:
  0.6 0.7 copy-start.2
  1.3 0.9 copy-start.4
  3.0 5.7 %collective-permute-start = (f32[5,32,128]{2,1,0:T(8,128)S(1)}, f32[5,32,128]{2,1,0:T(8,128)S(1)}, u32[]{:S(2)}, u32[]{:S(2)}) collective-permute-start(f32[5,32,128]{2,1,0:T(8,128)S(1)} %get-tuple-element.42), channel_id=1, source_target_pairs={{0,8},{8,0},{16,24},{24,16},{1,9},{9,1},{17,25},{25,17},{2,10},{10... | collective-permute-start | bytes 245768 | tf_op jit(solution)/shard_map/ppermute | solution.py:107
  6.1 5.3 %collective-permute-start.1 = (f32[5,32,128]{2,1,0:T(8,128)S(1)}, f32[5,32,128]{2,1,0:T(8,128)S(1)}, u32[]{:S(2)}, u32[]{:S(2)}) collective-permute-start(f32[5,32,128]{2,1,0:T(8,128)S(1)} %get-tuple-element.43), channel_id=1, source_target_pairs={{0,16},{8,24},{16,0},{24,8},{1,17},{9,25},{17,1},{25,9},{2,18},{10... | collective-permute-start | bytes 245768 | tf_op jit(solution)/shard_map/ppermute | solution.py:107
  7.6 5.3 %collective-permute-start.2 = (f32[5,32,128]{2,1,0:T(8,128)S(1)}, f32[5,32,128]{2,1,0:T(8,128)S(1)}, u32[]{:S(2)}, u32[]{:S(2)}) collective-permute-start(f32[5,32,128]{2,1,0:T(8,128)S(1)} %get-tuple-element.44), channel_id=1, source_target_pairs={{0,24},{8,16},{16,8},{24,0},{1,25},{9,17},{17,9},{25,1},{2,26},{10... | collective-permute-start | bytes 245768 | tf_op jit(solution)/shard_map/ppermute | solution.py:107
  13.0 1.4 %collective-permute-start.3 = (f32[7,32,128]{2,1,0:T(8,128)S(1)}, f32[7,32,128]{2,1,0:T(8,128)S(1)}, u32[]{:S(2)}, u32[]{:S(2)}) collective-permute-start(f32[7,32,128]{2,1,0:T(8,128)S(1)} %get-tuple-element.46), channel_id=1, source_target_pairs={{0,1},{1,0},{2,3},{3,2},{4,5},{5,4},{6,7},{7,6},{8,9},{9,8},{10,11... | collective-permute-start | bytes 344072 | tf_op jit(solution)/shard_map/ppermute | solution.py:107
  14.4 11.4 %collective-permute-start.4 = (f32[7,32,128]{2,1,0:T(8,128)S(1)}, f32[7,32,128]{2,1,0:T(8,128)S(1)}, u32[]{:S(2)}, u32[]{:S(2)}) collective-permute-start(f32[7,32,128]{2,1,0:T(8,128)S(1)} %add.24), channel_id=1, source_target_pairs={{0,2},{1,3},{2,0},{3,1},{4,6},{5,7},{6,4},{7,5},{8,10},{9,11},{10,... | collective-permute-start | bytes 344072 | tf_op jit(solution)/shard_map/ppermute | solution.py:107
  16.0 11.8 %collective-permute-start.5 = (f32[7,32,128]{2,1,0:T(8,128)S(1)}, f32[7,32,128]{2,1,0:T(8,128)S(1)}, u32[]{:S(2)}, u32[]{:S(2)}) collective-permute-start(f32[7,32,128]{2,1,0:T(8,128)S(1)} %add.24), channel_id=1, source_target_pairs={{0,4},{1,5},{2,6},{3,7},{4,0},{5,1},{6,2},{7,3},{8,12},{9,13},{10,... | collective-permute-start | bytes 344072 | tf_op jit(solution)/shard_map/ppermute | solution.py:107
  18.6 9.2 %collective-permute-start.6 = (f32[7,32,128]{2,1,0:T(8,128)S(1)}, f32[7,32,128]{2,1,0:T(8,128)S(1)}, u32[]{:S(2)}, u32[]{:S(2)}) collective-permute-start(f32[7,32,128]{2,1,0:T(8,128)S(1)} %add.24), channel_id=1, source_target_pairs={{0,6},{1,7},{2,4},{3,5},{4,2},{5,3},{6,0},{7,1},{8,14},{9,15},{10,... | collective-permute-start | bytes 344072 | tf_op jit(solution)/shard_map/ppermute | solution.py:107
  18.8 5.8 %copy-start = (bf16[1,1024,8192]{2,1,0:T(8,128)(2,1)S(1)}, bf16[1,1024,8192]{2,1,0:T(8,128)(2,1)}, u32[]{:S(2)}) copy-start(bf16[1,1024,8192]{2,1,0:T(8,128)(2,1)} %param.5) | copy-start | bytes 50331652
  24.6 3.4 %copy-start.5 = (s32[1,8]{1,0:T(1,128)S(1)}, s32[1,8]{1,0:T(1,128)}, u32[]{:S(2)}) copy-start(s32[1,8]{1,0:T(1,128)} %param.9) | copy-start | bytes 100
  24.6 4.7 %copy-start.1 = (f32[1,8,128,128]{3,2,1,0:T(8,128)S(1)}, f32[1,8,128,128]{3,2,1,0:T(8,128)}, u32[]{:S(2)}) copy-start(f32[1,8,128,128]{3,2,1,0:T(8,128)} %param.6) | copy-start | bytes 1572868
  24.6 4.7 %copy-start.3 = (s32[1,4,4]{2,1,0:T(4,128)S(1)}, s32[1,4,4]{2,1,0:T(4,128)}, u32[]{:S(2)}) copy-start(s32[1,4,4]{2,1,0:T(4,128)} %param.8) | copy-start | bytes 196
  27.9 1.4 %collective-permute-start.7 = (f32[7,32,128]{2,1,0:T(8,128)S(1)}, f32[7,32,128]{2,1,0:T(8,128)S(1)}, u32[]{:S(2)}, u32[]{:S(2)}) collective-permute-start(f32[7,32,128]{2,1,0:T(8,128)S(1)} %add_add_fusion.a0), channel_id=1, source_target_pairs={{0,1},{1,0},{2,3},{3,2},{4,5},{5,4},{6,7},{7,6},{8,9},{9,8},{10,11... | collective-permute-start | bytes 344072 | tf_op jit(solution)/shard_map/ppermute | solution.py:107
  34.1 11.1 %collective-permute-start.12 = (bf16[8,32,128]{2,1,0:T(8,128)(2,1)S(1)}, bf16[8,32,128]{2,1,0:T(8,128)(2,1)S(1)}, u32[]{:S(2)}, u32[]{:S(2)}) collective-permute-start(bf16[8,32,128]{2,1,0:T(8,128)(2,1)S(1)} %get-tuple-element.47), channel_id=1, source_target_pairs={{0,1},{1,0},{2,3},{3,2},{4,5},{5,4},{6,7},{7,6},{8,9},{9,8},{10,11... | collective-permute-start | bytes 196616 | tf_op jit(solution)/shard_map/ppermute | solution.py:107
  34.3 4.6 %collective-permute-start.13 = (bf16[8,32,128]{2,1,0:T(8,128)(2,1)S(1)}, bf16[8,32,128]{2,1,0:T(8,128)(2,1)S(1)}, u32[]{:S(2)}, u32[]{:S(2)}) collective-permute-start(bf16[8,32,128]{2,1,0:T(8,128)(2,1)S(1)} %get-tuple-element.47), channel_id=1, source_target_pairs={{0,2},{1,3},{2,0},{3,1},{4,6},{5,7},{6,4},{7,5},{8,10},{9,11},{10,... | collective-permute-start | bytes 196616 | tf_op jit(solution)/shard_map/ppermute | solution.py:107
  36.4 8.3 %collective-permute-start.8 = (bf16[8,32,128]{2,1,0:T(8,128)(2,1)S(1)}, bf16[8,32,128]{2,1,0:T(8,128)(2,1)S(1)}, u32[]{:S(2)}, u32[]{:S(2)}) collective-permute-start(bf16[8,32,128]{2,1,0:T(8,128)(2,1)S(1)} %get-tuple-element.47), channel_id=1, source_target_pairs={{0,4},{1,5},{2,6},{3,7},{4,0},{5,1},{6,2},{7,3},{8,12},{9,13},{10,... | collective-permute-start | bytes 196616 | tf_op jit(solution)/shard_map/ppermute | solution.py:107
  37.3 7.3 %collective-permute-start.10 = (bf16[8,32,128]{2,1,0:T(8,128)(2,1)S(1)}, bf16[8,32,128]{2,1,0:T(8,128)(2,1)S(1)}, u32[]{:S(2)}, u32[]{:S(2)}) collective-permute-start(bf16[8,32,128]{2,1,0:T(8,128)(2,1)S(1)} %get-tuple-element.47), channel_id=1, source_target_pairs={{0,6},{1,7},{2,4},{3,5},{4,2},{5,3},{6,0},{7,1},{8,14},{9,15},{10,... | collective-permute-start | bytes 196616 | tf_op jit(solution)/shard_map/ppermute | solution.py:107
  38.9 7.1 %collective-permute-start.14 = (bf16[8,32,128]{2,1,0:T(8,128)(2,1)S(1)}, bf16[8,32,128]{2,1,0:T(8,128)(2,1)S(1)}, u32[]{:S(2)}, u32[]{:S(2)}) collective-permute-start(bf16[8,32,128]{2,1,0:T(8,128)(2,1)S(1)} %collective-permute-done.13), channel_id=1, source_target_pairs={{0,1},{1,0},{2,3},{3,2},{4,5},{5,4},{6,7},{7,6},{8,9},{9,8},{10,11... | collective-permute-start | bytes 196616 | tf_op jit(solution)/shard_map/ppermute | solution.py:107
  44.7 1.3 collective-permute-start.9
  44.7 1.4 %collective-permute-start.11 = (bf16[8,32,128]{2,1,0:T(8,128)(2,1)S(1)}, bf16[8,32,128]{2,1,0:T(8,128)(2,1)S(1)}, u32[]{:S(2)}, u32[]{:S(2)}) collective-permute-start(bf16[8,32,128]{2,1,0:T(8,128)(2,1)S(1)} %collective-permute-done.10), channel_id=1, source_target_pairs={{0,1},{1,0},{2,3},{3,2},{4,5},{5,4},{6,7},{7,6},{8,9},{9,8},{10,11... | collective-permute-start | bytes 196616 | tf_op jit(solution)/shard_map/ppermute | solution.py:107
  46.8 8.7 %collective-permute-start.15 = (bf16[4,32,128]{2,1,0:T(8,128)(2,1)S(1)}, bf16[4,32,128]{2,1,0:T(8,128)(2,1)S(1)}, u32[]{:S(2)}, u32[]{:S(2)}) collective-permute-start(bf16[4,32,128]{2,1,0:T(8,128)(2,1)S(1)} %get-tuple-element.48), channel_id=1, source_target_pairs={{0,8},{8,0},{16,24},{24,16},{1,9},{9,1},{17,25},{25,17},{2,10},{10... | collective-permute-start | bytes 98312 | tf_op jit(solution)/shard_map/ppermute | solution.py:107
  47.4 8.2 %collective-permute-start.16 = (bf16[4,32,128]{2,1,0:T(8,128)(2,1)S(1)}, bf16[4,32,128]{2,1,0:T(8,128)(2,1)S(1)}, u32[]{:S(2)}, u32[]{:S(2)}) collective-permute-start(bf16[4,32,128]{2,1,0:T(8,128)(2,1)S(1)} %get-tuple-element.49), channel_id=1, source_target_pairs={{0,16},{8,24},{16,0},{24,8},{1,17},{9,25},{17,1},{25,9},{2,18},{10... | collective-permute-start | bytes 98312 | tf_op jit(solution)/shard_map/ppermute | solution.py:107
  48.1 7.5 %collective-permute-start.17 = (bf16[4,32,128]{2,1,0:T(8,128)(2,1)S(1)}, bf16[4,32,128]{2,1,0:T(8,128)(2,1)S(1)}, u32[]{:S(2)}, u32[]{:S(2)}) collective-permute-start(bf16[4,32,128]{2,1,0:T(8,128)(2,1)S(1)} %get-tuple-element.50), channel_id=1, source_target_pairs={{0,24},{8,16},{16,8},{24,0},{1,25},{9,17},{17,9},{25,1},{2,26},{10... | collective-permute-start | bytes 98312 | tf_op jit(solution)/shard_map/ppermute | solution.py:107
  57.3 4.3 %collective-permute-start.18 = (bf16[4,32,128]{2,1,0:T(8,128)(2,1)S(1)}, bf16[4,32,128]{2,1,0:T(8,128)(2,1)S(1)}, u32[]{:S(2)}, u32[]{:S(2)}) collective-permute-start(bf16[4,32,128]{2,1,0:T(8,128)(2,1)S(1)} %get-tuple-element.53), channel_id=1, source_target_pairs={{0,8},{8,0},{16,24},{24,16},{1,9},{9,1},{17,25},{25,17},{2,10},{10... | collective-permute-start | bytes 98312 | tf_op jit(solution)/shard_map/ppermute | solution.py:107
  57.8 4.1 %collective-permute-start.19 = (bf16[4,32,128]{2,1,0:T(8,128)(2,1)S(1)}, bf16[4,32,128]{2,1,0:T(8,128)(2,1)S(1)}, u32[]{:S(2)}, u32[]{:S(2)}) collective-permute-start(bf16[4,32,128]{2,1,0:T(8,128)(2,1)S(1)} %get-tuple-element.54), channel_id=1, source_target_pairs={{0,16},{8,24},{16,0},{24,8},{1,17},{9,25},{17,1},{25,9},{2,18},{10... | collective-permute-start | bytes 98312 | tf_op jit(solution)/shard_map/ppermute | solution.py:107
  58.5 4.8 %collective-permute-start.20 = (bf16[4,32,128]{2,1,0:T(8,128)(2,1)S(1)}, bf16[4,32,128]{2,1,0:T(8,128)(2,1)S(1)}, u32[]{:S(2)}, u32[]{:S(2)}) collective-permute-start(bf16[4,32,128]{2,1,0:T(8,128)(2,1)S(1)} %get-tuple-element.55), channel_id=1, source_target_pairs={{0,24},{8,16},{16,8},{24,0},{1,25},{9,17},{17,9},{25,1},{2,26},{10... | collective-permute-start | bytes 98312 | tf_op jit(solution)/shard_map/ppermute | solution.py:107
  63.4 1.3 collective-permute-start.21
  64.7 4.5 %collective-permute-start.22 = (bf16[6,32,128]{2,1,0:T(8,128)(2,1)S(1)}, bf16[6,32,128]{2,1,0:T(8,128)(2,1)S(1)}, u32[]{:S(2)}, u32[]{:S(2)}) collective-permute-start(bf16[6,32,128]{2,1,0:T(8,128)(2,1)S(1)} %add.28), channel_id=1, source_target_pairs={{0,2},{1,3},{2,0},{3,1},{4,6},{5,7},{6,4},{7,5},{8,10},{9,11},{10,... | collective-permute-start | bytes 147464 | tf_op jit(solution)/shard_map/ppermute | solution.py:107
  66.1 6.5 %collective-permute-start.23 = (bf16[6,32,128]{2,1,0:T(8,128)(2,1)S(1)}, bf16[6,32,128]{2,1,0:T(8,128)(2,1)S(1)}, u32[]{:S(2)}, u32[]{:S(2)}) collective-permute-start(bf16[6,32,128]{2,1,0:T(8,128)(2,1)S(1)} %add.28), channel_id=1, source_target_pairs={{0,4},{1,5},{2,6},{3,7},{4,0},{5,1},{6,2},{7,3},{8,12},{9,13},{10,... | collective-permute-start | bytes 147464 | tf_op jit(solution)/shard_map/ppermute | solution.py:107
  67.5 6.0 %collective-permute-start.24 = (bf16[6,32,128]{2,1,0:T(8,128)(2,1)S(1)}, bf16[6,32,128]{2,1,0:T(8,128)(2,1)S(1)}, u32[]{:S(2)}, u32[]{:S(2)}) collective-permute-start(bf16[6,32,128]{2,1,0:T(8,128)(2,1)S(1)} %add.28), channel_id=1, source_target_pairs={{0,6},{1,7},{2,4},{3,5},{4,2},{5,3},{6,0},{7,1},{8,14},{9,15},{10,... | collective-permute-start | bytes 147464 | tf_op jit(solution)/shard_map/ppermute | solution.py:107
  73.5 1.3 collective-permute-start.25
  77.1 11.8 %collective-permute-start.30 = (bf16[11,32,128]{2,1,0:T(8,128)(2,1)S(1)}, bf16[11,32,128]{2,1,0:T(8,128)(2,1)S(1)}, u32[]{:S(2)}, u32[]{:S(2)}) collective-permute-start(bf16[11,32,128]{2,1,0:T(8,128)(2,1)S(1)} %get-tuple-element.58), channel_id=1, source_target_pairs={{0,1},{1,0},{2,3},{3,2},{4,5},{5,4},{6,7},{7,6},{8,9},{9,8},{10,11... | collective-permute-start | bytes 270344 | tf_op jit(solution)/shard_map/ppermute | solution.py:107
  77.3 6.1 %collective-permute-start.31 = (bf16[11,32,128]{2,1,0:T(8,128)(2,1)S(1)}, bf16[11,32,128]{2,1,0:T(8,128)(2,1)S(1)}, u32[]{:S(2)}, u32[]{:S(2)}) collective-permute-start(bf16[11,32,128]{2,1,0:T(8,128)(2,1)S(1)} %get-tuple-element.58), channel_id=1, source_target_pairs={{0,2},{1,3},{2,0},{3,1},{4,6},{5,7},{6,4},{7,5},{8,10},{9,11},{10,... | collective-permute-start | bytes 270344 | tf_op jit(solution)/shard_map/ppermute | solution.py:107
  78.1 10.2 %collective-permute-start.26 = (bf16[11,32,128]{2,1,0:T(8,128)(2,1)S(1)}, bf16[11,32,128]{2,1,0:T(8,128)(2,1)S(1)}, u32[]{:S(2)}, u32[]{:S(2)}) collective-permute-start(bf16[11,32,128]{2,1,0:T(8,128)(2,1)S(1)} %get-tuple-element.58), channel_id=1, source_target_pairs={{0,4},{1,5},{2,6},{3,7},{4,0},{5,1},{6,2},{7,3},{8,12},{9,13},{10,... | collective-permute-start | bytes 270344 | tf_op jit(solution)/shard_map/ppermute | solution.py:107
  79.8 8.5 %collective-permute-start.28 = (bf16[11,32,128]{2,1,0:T(8,128)(2,1)S(1)}, bf16[11,32,128]{2,1,0:T(8,128)(2,1)S(1)}, u32[]{:S(2)}, u32[]{:S(2)}) collective-permute-start(bf16[11,32,128]{2,1,0:T(8,128)(2,1)S(1)} %get-tuple-element.58), channel_id=1, source_target_pairs={{0,6},{1,7},{2,4},{3,5},{4,2},{5,3},{6,0},{7,1},{8,14},{9,15},{10,... | collective-permute-start | bytes 270344 | tf_op jit(solution)/shard_map/ppermute | solution.py:107
  83.3 6.3 %collective-permute-start.32 = (bf16[11,32,128]{2,1,0:T(8,128)(2,1)S(1)}, bf16[11,32,128]{2,1,0:T(8,128)(2,1)S(1)}, u32[]{:S(2)}, u32[]{:S(2)}) collective-permute-start(bf16[11,32,128]{2,1,0:T(8,128)(2,1)S(1)} %collective-permute-done.31), channel_id=1, source_target_pairs={{0,1},{1,0},{2,3},{3,2},{4,5},{5,4},{6,7},{7,6},{8,9},{9,8},{10,11... | collective-permute-start | bytes 270344 | tf_op jit(solution)/shard_map/ppermute | solution.py:107
  88.3 1.3 collective-permute-start.27
  88.3 1.4 %collective-permute-start.29 = (bf16[11,32,128]{2,1,0:T(8,128)(2,1)S(1)}, bf16[11,32,128]{2,1,0:T(8,128)(2,1)S(1)}, u32[]{:S(2)}, u32[]{:S(2)}) collective-permute-start(bf16[11,32,128]{2,1,0:T(8,128)(2,1)S(1)} %collective-permute-done.28), channel_id=1, source_target_pairs={{0,1},{1,0},{2,3},{3,2},{4,5},{5,4},{6,7},{7,6},{8,9},{9,8},{10,11... | collective-permute-start | bytes 270344 | tf_op jit(solution)/shard_map/ppermute | solution.py:107
  90.5 8.7 %collective-permute-start.33 = (bf16[7,32,128]{2,1,0:T(8,128)(2,1)S(1)}, bf16[7,32,128]{2,1,0:T(8,128)(2,1)S(1)}, u32[]{:S(2)}, u32[]{:S(2)}) collective-permute-start(bf16[7,32,128]{2,1,0:T(8,128)(2,1)S(1)} %get-tuple-element.60), channel_id=1, source_target_pairs={{0,8},{8,0},{16,24},{24,16},{1,9},{9,1},{17,25},{25,17},{2,10},{10... | collective-permute-start | bytes 172040 | tf_op jit(solution)/shard_map/ppermute | solution.py:107
  91.9 7.3 %collective-permute-start.34 = (bf16[7,32,128]{2,1,0:T(8,128)(2,1)S(1)}, bf16[7,32,128]{2,1,0:T(8,128)(2,1)S(1)}, u32[]{:S(2)}, u32[]{:S(2)}) collective-permute-start(bf16[7,32,128]{2,1,0:T(8,128)(2,1)S(1)} %get-tuple-element.61), channel_id=1, source_target_pairs={{0,16},{8,24},{16,0},{24,8},{1,17},{9,25},{17,1},{25,9},{2,18},{10... | collective-permute-start | bytes 172040 | tf_op jit(solution)/shard_map/ppermute | solution.py:107
  93.3 5.9 %collective-permute-start.35 = (bf16[7,32,128]{2,1,0:T(8,128)(2,1)S(1)}, bf16[7,32,128]{2,1,0:T(8,128)(2,1)S(1)}, u32[]{:S(2)}, u32[]{:S(2)}) collective-permute-start(bf16[7,32,128]{2,1,0:T(8,128)(2,1)S(1)} %get-tuple-element.62), channel_id=1, source_target_pairs={{0,24},{8,16},{16,8},{24,0},{1,25},{9,17},{17,9},{25,1},{2,26},{10... | collective-permute-start | bytes 172040 | tf_op jit(solution)/shard_map/ppermute | solution.py:107
  101.6 9.7 %collective-permute-start.39 = (bf16[11,32,128]{2,1,0:T(8,128)(2,1)S(1)}, bf16[11,32,128]{2,1,0:T(8,128)(2,1)S(1)}, u32[]{:S(2)}, u32[]{:S(2)}) collective-permute-start(bf16[11,32,128]{2,1,0:T(8,128)(2,1)S(1)} %tail_gram.1), channel_id=1, source_target_pairs={{0,4},{1,5},{2,6},{3,7},{4,0},{5,1},{6,2},{7,3},{8,12},{9,13},{10,... | collective-permute-start | bytes 270344 | tf_op jit(solution)/shard_map/ppermute | solution.py:107
  103.9 7.3 %collective-permute-start.41 = (bf16[11,32,128]{2,1,0:T(8,128)(2,1)S(1)}, bf16[11,32,128]{2,1,0:T(8,128)(2,1)S(1)}, u32[]{:S(2)}, u32[]{:S(2)}) collective-permute-start(bf16[11,32,128]{2,1,0:T(8,128)(2,1)S(1)} %tail_gram.1), channel_id=1, source_target_pairs={{0,6},{1,7},{2,4},{3,5},{4,2},{5,3},{6,0},{7,1},{8,14},{9,15},{10,... | collective-permute-start | bytes 270344 | tf_op jit(solution)/shard_map/ppermute | solution.py:107
  105.4 6.3 %collective-permute-start.37 = (bf16[11,32,128]{2,1,0:T(8,128)(2,1)S(1)}, bf16[11,32,128]{2,1,0:T(8,128)(2,1)S(1)}, u32[]{:S(2)}, u32[]{:S(2)}) collective-permute-start(bf16[11,32,128]{2,1,0:T(8,128)(2,1)S(1)} %tail_gram.1), channel_id=1, source_target_pairs={{0,2},{1,3},{2,0},{3,1},{4,6},{5,7},{6,4},{7,5},{8,10},{9,11},{10,... | collective-permute-start | bytes 270344 | tf_op jit(solution)/shard_map/ppermute | solution.py:107
  111.2 1.3 collective-permute-start.40
  111.2 1.4 %collective-permute-start.42 = (bf16[11,32,128]{2,1,0:T(8,128)(2,1)S(1)}, bf16[11,32,128]{2,1,0:T(8,128)(2,1)S(1)}, u32[]{:S(2)}, u32[]{:S(2)}) collective-permute-start(bf16[11,32,128]{2,1,0:T(8,128)(2,1)S(1)} %collective-permute-done.41), channel_id=1, source_target_pairs={{0,1},{1,0},{2,3},{3,2},{4,5},{5,4},{6,7},{7,6},{8,9},{9,8},{10,11... | collective-permute-start | bytes 270344 | tf_op jit(solution)/shard_map/ppermute | solution.py:107
  111.7 1.3 collective-permute-start.36
  111.7 1.4 %collective-permute-start.38 = (bf16[11,32,128]{2,1,0:T(8,128)(2,1)S(1)}, bf16[11,32,128]{2,1,0:T(8,128)(2,1)S(1)}, u32[]{:S(2)}, u32[]{:S(2)}) collective-permute-start(bf16[11,32,128]{2,1,0:T(8,128)(2,1)S(1)} %collective-permute-done.37), channel_id=1, source_target_pairs={{0,1},{1,0},{2,3},{3,2},{4,5},{5,4},{6,7},{7,6},{8,9},{9,8},{10,11... | collective-permute-start | bytes 270344 | tf_op jit(solution)/shard_map/ppermute | solution.py:107
  113.9 9.4 %collective-permute-start.43 = (bf16[15,32,128]{2,1,0:T(8,128)(2,1)S(1)}, bf16[15,32,128]{2,1,0:T(8,128)(2,1)S(1)}, u32[]{:S(2)}, u32[]{:S(2)}) collective-permute-start(bf16[15,32,128]{2,1,0:T(8,128)(2,1)S(1)} %get-tuple-element.64.s_ref), channel_id=1, source_target_pairs={{0,8},{8,0},{16,24},{24,16},{1,9},{9,1},{17,25},{25,17},{2,10},{10... | collective-permute-start | bytes 368648 | tf_op jit(solution)/shard_map/ppermute | solution.py:107
  115.3 8.0 %collective-permute-start.44 = (bf16[15,32,128]{2,1,0:T(8,128)(2,1)S(1)}, bf16[15,32,128]{2,1,0:T(8,128)(2,1)S(1)}, u32[]{:S(2)}, u32[]{:S(2)}) collective-permute-start(bf16[15,32,128]{2,1,0:T(8,128)(2,1)S(1)} %get-tuple-element.64.s_ref), channel_id=1, source_target_pairs={{0,16},{8,24},{16,0},{24,8},{1,17},{9,25},{17,1},{25,9},{2,18},{10... | collective-permute-start | bytes 368648 | tf_op jit(solution)/shard_map/ppermute | solution.py:107
  116.8 6.5 %collective-permute-start.45 = (bf16[15,32,128]{2,1,0:T(8,128)(2,1)S(1)}, bf16[15,32,128]{2,1,0:T(8,128)(2,1)S(1)}, u32[]{:S(2)}, u32[]{:S(2)}) collective-permute-start(bf16[15,32,128]{2,1,0:T(8,128)(2,1)S(1)} %get-tuple-element.64.s_ref), channel_id=1, source_target_pairs={{0,24},{8,16},{16,8},{24,0},{1,25},{9,17},{17,9},{25,1},{2,26},{10... | collective-permute-start | bytes 368648 | tf_op jit(solution)/shard_map/ppermute | solution.py:107

commit v3 on v0

v3 whole, which is shorter than its diff:
```python
import functools

import jax
import jax.numpy as jnp
from jax import lax
from jax.experimental import pallas as pl
from jax.experimental.pallas import tpu as pltpu
from jax.sharding import PartitionSpec as P

F32 = jnp.float32
BF16 = jnp.bfloat16
HIGH = lax.Precision.HIGHEST
VM = pl.BlockSpec(memory_space=pltpu.VMEM)
SM = pl.BlockSpec(memory_space=pltpu.SMEM)


def nn(a, b):
    return lax.dot_general(a, b, (((1,), (0,)), ((), ())), precision=HIGH, preferred_element_type=F32)


def nt(a, b):
    return lax.dot_general(a, b, (((1,), (1,)), ((), ())), precision=HIGH, preferred_element_type=F32)


def nt16(a, b):
    return lax.dot_general(a, b, (((1,), (1,)), ((), ())), preferred_element_type=F32)


def pair_sum(values):
    while len(values) > 1:
        values = [values[i] + values[i + 1] for i in range(0, len(values), 2)]
    return values[0]


def factor(mats):
    size = mats[0].shape[0]
    rows = lax.broadcasted_iota(jnp.int32, (size, size), 0)
    cols = lax.broadcasted_iota(jnp.int32, (size, size), 1)
    eye = (rows == cols).astype(F32)
    work = [jnp.concatenate([m, eye], axis=1) for m in mats]
    kept = [[] for _ in mats]
    for j in range(size):
        for n in range(len(mats)):
            m = work[n]
            row = m[j : j + 1, :] * lax.rsqrt(m[j : j + 1, j : j + 1])
            col = m[:, j : j + 1] * lax.rsqrt(m[j : j + 1, j : j + 1])
            kept[n].append(row)
            work[n] = m - col * row
    out = []
    for n in range(len(mats)):
        full = jnp.concatenate(kept[n], axis=0)
        out.append((jnp.where(cols >= rows, full[:, :size], 0.0), full[:, size:]))
    return out


def cut3(v):
    high = v.astype(BF16)
    rest = v - high.astype(F32)
    mid = rest.astype(BF16)
    return high, mid, (rest - mid.astype(F32)).astype(BF16)


def join3(parts):
    high, mid, low = (p.astype(F32) for p in parts)
    return high + (mid + low)


def call(kernel, outs, args, specs, scratch=(), vmem=8, name=None, cost=None):
    return pl.pallas_call(
        kernel,
        out_shape=outs,
        in_specs=specs,
        out_specs=jax.tree.map(lambda _: VM, outs),
        scratch_shapes=list(scratch),
        compiler_params=pltpu.CompilerParams(vmem_limit_bytes=vmem << 20),
        cost_estimate=cost,
        name=name,
    )(*args)


def xor(size, m):
    return [(i, i ^ m) for i in range(size)]


EXTRA = 3
CHUNKS = 1


def body(schur, inverse_blocks, loads, share_list, multiplicity):
    inverse = inverse_blocks[0]
    local_rows, order = schur.shape[1:]
    owned, block = inverse.shape[0], inverse.shape[-1]
    cases = loads.shape[1]
    share = share_list[0]
    subs, slots = share.shape
    parts = lax.axis_size("blk")
    zs = parts // 2
    weighting = 1.0 / (order * subs)
    weight = 1.0 / multiplicity[0].astype(F32)
    blocks = order // block
    plain = 1 - jnp.any(
        share.reshape(-1)[:, None] == jnp.arange(blocks, dtype=jnp.int32)[None, :], axis=0
    ).astype(jnp.int32)
    peers = list(range(1, subs))
    n_in = len(peers)
    n_slots = n_in * slots
    cube = (owned, cases, block)
    unit = (block // 2, block)
    per = -(-2 * n_slots // parts)
    n = cases

    def sds(shape, dtype=F32):
        return jax.ShapeDtypeStruct(shape, dtype)

    def permute(v, axis, m):
        return lax.ppermute(v, axis, xor(lax.axis_size(axis), m))

    def to_subs(vs):
        return [permute(v, "sub", m) for m, v in zip(peers, vs)]

    def padded(v):
        if v.shape[1] == block:
            return v
        return jnp.concatenate([v, jnp.zeros((v.shape[0], block - v.shape[1]), v.dtype)], axis=1)

    def me_blk():
        return lax.axis_index("blk")

    def me_sub():
        return lax.axis_index("sub")

    def wide(ref):
        return jnp.concatenate([ref[k] for k in range(owned)], axis=1)

    def weighted(ref, w_ref):
        return jnp.concatenate([ref[k] * w_ref[k] for k in range(owned)], axis=1)

    def far_and_self(v):
        far = {m: permute(v, "blk", 2 * m) for m in reversed(range(1, zs))}
        far[0] = v
        return [far[m] for m in range(zs)]


    def slot_inverse(after):
        def masked(share_ref, w_ref, inv_ref, m, s):
            k = share_ref[me_sub() ^ m, s]
            here = jnp.logical_and(k >= 0, k // owned == me_blk())
            at = jnp.where(here, k % owned, 0)
            return jnp.where(here, inv_ref[at] * w_ref[at], 0.0)

        def lend(share_ref, w_ref, inv_ref, after_ref, *outs):
            for m, o_ref in zip(peers, outs):
                for s in range(slots):
                    o_ref[s] = masked(share_ref, w_ref, inv_ref, m, s).astype(BF16)

        outs = tuple(sds((slots, block, block), BF16) for _ in peers)
        lent = call(lend, outs, (share, weight, inverse, after), [SM, SM, VM, pl.BlockSpec(memory_space=pl.ANY)], name="lend")
        arrived = to_subs(lent)

        def deal(share_ref, w_ref, inv_ref, *refs):
            ins, (keep_ref, send_ref, all_ref) = refs[:n_in], refs[n_in:]
            me = me_blk()
            for i in range(n_slots):
                m, s = peers[i // slots], i % slots
                value = masked(share_ref, w_ref, inv_ref, m, s) + ins[i // slots][s].astype(F32)
                for h in range(2):
                    u = 2 * i + h
                    all_ref[u // per, u % per] = value[h * unit[0] : (h + 1) * unit[0]]
            for u in range(2 * n_slots, parts * per):
                all_ref[u // per, u % per] = jnp.zeros(unit, F32)
            for q in range(zs):
                keep_ref[q] = all_ref[me ^ (2 * q)].astype(BF16)
                send_ref[q] = all_ref[me ^ (2 * q + 1)].astype(BF16)

        shape = (zs, per) + unit
        keep, send = call(
            deal,
            (sds(shape, BF16), sds(shape, BF16)),
            (share, weight, inverse, *arrived),
            [SM, SM] + [VM] * (1 + n_in),
            scratch=[pltpu.VMEM((parts, per) + unit, F32)],
            vmem=16,
            name="deal",
        )
        keep = keep + permute(send, "blk", 1)
        far = [permute(keep[m], "blk", 2 * m) for m in reversed(range(1, zs))]
        mine = pair_sum([v.astype(F32) for v in [keep[0]] + far[::-1]]).astype(BF16)
        same = jnp.stack(far_and_self(mine))
        return (same, permute(same, "blk", 1)), lent[0], keep, mine

    def slot_reader(same_ref, other_ref):
        def unit_at(u):
            q = (u // per) ^ me_blk()
            value, other = same_ref[q // 2, u % per], other_ref[q // 2, u % per]
            return jnp.where(q % 2 == 0, value, other)

        return lambda i: jnp.concatenate([unit_at(2 * i), unit_at(2 * i + 1)], axis=0)


    def gather(v, work, gate=()):
        pieces = far_and_self(v)
        near, far = pieces[:2], pieces[2:]
        near = jnp.concatenate([w for p in near for w in (p, permute(p, "blk", 1))], axis=0)
        done = work(near)
        if not far:
            return [near], done
        far, _, done = lax.optimization_barrier((far, gate, done))
        far = jnp.concatenate([w for p in far for w in (p, permute(p, "blk", 1))], axis=0)
        return [near, far], done

    def piece_reader(p_refs, stride):
        sizes = [r.shape[0] // stride for r in p_refs]

        def read(k):
            q, r = (k // owned) ^ me_blk(), k % owned
            value = p_refs[0][jnp.minimum(q, sizes[0] - 1) * stride + r]
            if len(p_refs) > 1:
                other = p_refs[1][jnp.maximum(q - sizes[0], 0) * stride + r]
                value = jnp.where(q < sizes[0], value, other)
            return value

        return read

    def extra_sum(p_refs, stride):
        found = []
        for r in p_refs:
            for q in range(r.shape[0] // stride):
                found.append(join3([r[q * stride + owned + e] for e in range(EXTRA)]))
        return pair_sum(found)

    def select_first(pieces, after):
        stride, n_p = owned + 1, len(pieces)

        def kernel(share_ref, after_ref, *refs):
            p_refs, outs = refs[:n_p], refs[n_p:]
            read = piece_reader(p_refs, stride)
            for i in range(n_slots):
                k = share_ref[me_sub() ^ peers[i // slots], i % slots]
                value = read(jnp.maximum(k, 0))
                outs[i // slots][i % slots] = jnp.where(k >= 0, value, jnp.zeros_like(value))
            total = pair_sum([r[q * stride + owned] for r in p_refs for q in range(r.shape[0] // stride)])
            for o_ref in outs:
                o_ref[slots] = total

        outs = tuple(sds((slots + 1, cases, block)) for _ in peers)
        anywhere = pl.BlockSpec(memory_space=pl.ANY)
        return call(kernel, outs, (share, after, *pieces), [SM, anywhere] + [VM] * n_p, name="select_first")

    def select(pieces, extra, after):
        stride = owned + (EXTRA if extra else 0)
        n_p = len(pieces)
        more = EXTRA if extra else 0

        def kernel(share_ref, after_ref, *refs):
            p_refs, outs = refs[:n_p], refs[n_p:]
            read = piece_reader(p_refs, stride)
            for i in range(n_slots):
                k = share_ref[me_sub() ^ peers[i // slots], i % slots]
                value = read(jnp.maximum(k, 0))
                value = jnp.where(k >= 0, value, jnp.zeros_like(value))
                if extra:
                    outs[0][i] = value
                else:
                    outs[i // slots][i % slots] = value
            if extra:
                total = extra_sum(p_refs, stride)
                outs[-1][...] = total
                for e, part in enumerate(cut3(total)):
                    outs[0][n_slots + e] = part

        if extra:
            outs = (sds((n_slots + more, cases, block), BF16), sds((cases, block)))
        else:
            outs = tuple(sds((slots, cases, block), BF16) for _ in peers)
        anywhere = pl.BlockSpec(memory_space=pl.ANY)
        return call(kernel, outs, (share, after, *pieces), [SM, anywhere] + [VM] * n_p, name="select")


    def mix(plain_ref, inv_ref, v_ref, x_ref, h_ref):
        for k in range(owned):
            value = v_ref[k]
            x = nt(value, inv_ref[k])
            x_ref[k] = x
            h_ref[k] = jnp.where(plain_ref[me_blk() * owned + k] > 0, x, value).astype(h_ref.dtype)

    def open_(raw):
        def kernel(plain_ref, l_ref, inv_ref, v_ref, x_ref, h_ref):
            value = l_ref[...]
            for k in range(owned):
                v_ref[k] = value[:, k * block : (k + 1) * block]
            mix(plain_ref, inv_ref, v_ref, x_ref, h_ref)
            h_ref[owned] = padded(nt(value, value) * weighting)

        outs = (sds(cube), sds(cube), sds((owned + 1, cases, block)))
        return call(kernel, outs, (plain, raw, inverse), [SM, VM, VM], name="open")

    def touch(full, after):
        def kernel(m_ref, a_ref, o_ref):
            o_ref[...] = m_ref[:8, :block].astype(F32)

        anywhere = pl.BlockSpec(memory_space=pl.ANY)
        return call(kernel, sds((8, block)), (full, after), [VM, anywhere], name="touch")

    def multiply(matrix, pieces, first, stride, before):
        count = pieces.shape[0] // stride
        wide_type = pieces.dtype == F32
        rows = local_rows // CHUNKS

        def kernel(plain_ref, p_ref, *rest):
            m_refs, y_ref = rest[:CHUNKS], rest[-1]
            totals = [
                rest[CHUNKS][:, c * rows : (c + 1) * rows] if before is not None else jnp.zeros((n, rows), F32)
                for c in range(CHUNKS)
            ]
            for q in range(count):
                owner = (first + q) ^ me_blk()
                z = []
                for i in range(owned):
                    value = p_ref[q * stride + i]
                    z.append(jnp.where(plain_ref[owner * owned + i] > 0, value, jnp.zeros_like(value)))
                z = jnp.concatenate(z, axis=1)
                if wide_type:
                    high = z.astype(BF16)
                    z = jnp.concatenate([high, (z - high.astype(F32)).astype(BF16)], axis=0)
                at = pl.multiple_of(owner * local_rows, local_rows)
                for c in range(CHUNKS):
                    found = nt16(z, m_refs[c][:, pl.ds(at, local_rows)])
                    totals[c] = totals[c] + (found[:n] + found[n:] if wide_type else found)
            for c in range(CHUNKS):
                y_ref[:, c * rows : (c + 1) * rows] = totals[c]

        args = (plain, pieces, *matrix) + (() if before is None else (before,))
        cost = pl.CostEstimate(
            flops=2 * n * local_rows * local_rows * count,
            transcendentals=0,
            bytes_accessed=2 * local_rows * local_rows * count,
        )
        return call(kernel, sds((n, local_rows)), args, [SM] + [VM] * (len(args) - 1), name="multiply", cost=cost)

    def shared_part(share_ref, m_refs, total, mine, theirs, inv_at, v_ref, x_ref, u_ref, z_ref):
        u_ref[...] = v_ref[...]
        z_ref[...] = x_ref[...]
        totals = [total[:, c * (local_rows // CHUNKS) : (c + 1) * (local_rows // CHUNKS)] for c in range(CHUNKS)]
        for p, m in enumerate(peers):
            zz, where_ = [], []
            for s in range(slots):
                k = share_ref[me_sub() ^ m, s]
                far = theirs(p, s)
                near = mine(p, s)
                if far.dtype == F32:
                    both = near + far
                    near = both.astype(BF16)
                    lower = (both - near.astype(F32)).astype(BF16)
                else:
                    lower = far
                both = nt16(jnp.concatenate([near, lower], axis=0), inv_at(p * slots + s))
                both = both[:n] + both[n:]
                high = both.astype(BF16)
                if far.dtype == F32:
                    high = jnp.concatenate([high, (both - high.astype(F32)).astype(BF16)], axis=0)
                zz.append(high)
                where_.append(pl.multiple_of(jnp.maximum(k, 0) * block, block))

                @pl.when(jnp.logical_and(k >= 0, k // owned == me_blk()))
                def _():
                    u_ref[k % owned] += far.astype(F32)
                    z_ref[k % owned] = both

            zz = jnp.concatenate(zz, axis=1)
            for c in range(CHUNKS):
                cols = jnp.concatenate([m_refs[c][:, pl.ds(at, block)] for at in where_], axis=1)
                found = nt16(zz, cols)
                totals[c] = totals[c] + (found[:n] + found[n:] if found.shape[0] > n else found)
        return jnp.concatenate(totals, axis=1)

    def tail_first(matrix, part, mine, theirs, slot_inv, v, x):
        def kernel(share_ref, plain_ref, w_ref, part_ref, inv_ref, s0, s1, v_ref, x_ref, *rest):
            m_refs, rest = rest[:CHUNKS], rest[CHUNKS:]
            mine_refs, their_refs, (y_ref, h_ref, x1_ref, u_ref, z_ref, f_ref, i_ref) = (
                rest[:n_in],
                rest[n_in : 2 * n_in],
                rest[2 * n_in :],
            )
            total = shared_part(
                share_ref,
                m_refs,
                part_ref[...],
                lambda p, s: mine_refs[p][s],
                lambda p, s: their_refs[p][s],
                slot_reader(s0, s1),
                v_ref,
                x_ref,
                u_ref,
                z_ref,
            )
            grams = [mine_refs[0][slots]] + [r[slots] for r in their_refs]
            ((up, inv_low),) = factor([pair_sum(grams)[:, :n]])
            f_ref[...] = up
            i_ref[...] = inv_low
            total = nn(inv_low, jnp.concatenate([total, wide(u_ref)], axis=1))
            total, base = total[:, :local_rows], total[:, local_rows:]
            for k in range(owned):
                y_ref[k] = total[:, k * block : (k + 1) * block]
                u_ref[k] = base[:, k * block : (k + 1) * block]
            mix(plain_ref, inv_ref, y_ref, x1_ref, h_ref)
            g0 = nt(weighted(u_ref, w_ref), base)
            g1 = nt(total, jnp.concatenate([base, total], axis=0))
            gram = padded(jnp.concatenate([g0, g1], axis=1) * weighting)
            for e, part in enumerate(cut3(gram)):
                h_ref[owned + e] = part

        outs = (sds(cube), sds((owned + EXTRA, cases, block), BF16)) + (sds(cube),) * 3 + (sds((n, n)),) * 2
        args = (share, plain, weight, part, inverse, *slot_inv, v, x, *matrix, *mine, *theirs)
        return call(kernel, outs, args, [SM] * 3 + [VM] * (len(args) - 3), vmem=16, name="tail_first")

    def tail_second(matrix, part, mine, theirs, slot_inv, v, x, base):
        def kernel(share_ref, part_ref, b_ref, s0, s1, v_ref, x_ref, mine_ref, *rest):
            m_refs, rest = rest[:CHUNKS], rest[CHUNKS:]
            their_refs, (h_ref, z_ref, u_ref) = rest[:n_in], rest[n_in:]
            total = shared_part(
                share_ref,
                m_refs,
                part_ref[...],
                lambda p, s: mine_ref[p * slots + s],
                lambda p, s: their_refs[p][p * slots + s],
                slot_reader(s0, s1),
                v_ref,
                x_ref,
                u_ref,
                z_ref,
            )
            for k in range(owned):
                h_ref[k] = total[:, k * block : (k + 1) * block].astype(BF16)
            gram = nt(total, jnp.concatenate([wide(b_ref), wide(u_ref), total], axis=0))
            for e, part in enumerate(cut3(padded(gram * weighting))):
                h_ref[owned + e] = part

        outs = (sds((owned + EXTRA, cases, block), BF16), sds(cube))
        args = (share, part, base, *slot_inv, v, x, mine, *matrix, *theirs)
        return call(
            kernel, outs, args, [SM] + [VM] * (len(args) - 1), scratch=[pltpu.VMEM(cube, F32)], vmem=16, name="tail_second"
        )

    def gram_and_cross(g_ref, s_ref, theirs, all_ref):
        gram = pair_sum([g_ref[...]] + [join3([r[n_slots + e] for e in range(EXTRA)]) for r in theirs])
        all_ref[me_sub()] = s_ref[...]
        for m, t_ref in zip(peers, theirs):
            all_ref[me_sub() ^ m] = t_ref[...]
        cross = jnp.zeros((n, n), F32)
        for i in range(subs):
            for j in range(i + 1, subs):
                at = ((i ^ j) - 1) * slots
                left = jnp.concatenate([all_ref[i, at + s] for s in range(slots)], axis=1)
                right = jnp.concatenate([all_ref[j, at + s] for s in range(slots)], axis=1)
                cross = cross + nt16(left, right)
        return gram, (cross + cross.T) * weighting

    def early(g01, mine, theirs):
        def kernel(g_ref, s_ref, *rest):
            ins, (u00_ref, i00_ref, l10_ref, u11_ref, i11_ref, j1_ref, r1_ref, all_ref) = rest[:n_in], rest[n_in:]
            g, cross = gram_and_cross(g_ref, s_ref, ins, all_ref)
            g00, g10, g11 = g[:, :n], g[:, n : 2 * n], g[:, 2 * n : 3 * n] + cross
            (u00, i00), (_, j1) = factor([g00, g11])
            l10 = nt(g10, i00)
            ((u11, i11),) = factor([g11 - nt(l10, l10)])
            u00_ref[...] = u00
            i00_ref[...] = i00
            l10_ref[...] = l10
            u11_ref[...] = u11
            i11_ref[...] = i11
            j1_ref[...] = j1
            r1_ref[...] = nt(g10.T, j1)

        outs = tuple(sds((n, n)) for _ in range(7))
        cost = pl.CostEstimate(flops=10**8, transcendentals=0, bytes_accessed=10**7)
        return call(
            kernel,
            outs,
            (g01, mine, *theirs),
            [VM] * (2 + n_in),
            scratch=[pltpu.VMEM((subs,) + mine.shape, BF16)],
            vmem=24,
            name="early",
            cost=cost,
        )

    def finish(g2, mine, theirs, known, upper, inv_low, z0, z1):
        n_known = len(known)

        def kernel(g_ref, s_ref, f_ref, t_ref, z0_ref, z1_ref, *rest):
            known_refs, rest = rest[:n_known], rest[n_known:]
            ins, (sol_ref, mis_ref, all_ref) = rest[:n_in], rest[n_in:]
            u00, i00, l10, u11, i11, j1, r1 = (r[...] for r in known_refs)
            g, cross = gram_and_cross(g_ref, s_ref, ins, all_ref)
            g20, g21, g22 = g[:, :n], g[:, n : 2 * n], g[:, 2 * n : 3 * n] + cross
            l20 = nt(g20, i00)
            k21 = nt(g21, j1)
            l21 = nt(g21 - nt(l20, l10), i11)
            (u22, _), (_, j2) = factor([g22 - nt(l20, l20) - nt(l21, l21), g22 - nt(k21, k21)])
            r2 = nt(g20.T - nt(r1, k21), j2)
            c1 = nn(r2, j2)
            c0 = nn(r1 - nn(c1, k21), j1)
            low = f_ref[...].T
            m0 = u00.T - nn(c0, l10) - nn(c1, l20)
            m1 = -nt(c0, u11) - nn(c1, l21)
            m2 = -nt(c1, u22)
            mixed = nn(low, jnp.concatenate([m0, m1, m2, nn(c0, t_ref[...]), c1], axis=1))
            mis_ref[...] = mixed[:, : 3 * n]
            both = mixed[:, 3 * n :]
            for k in range(owned):
                z = jnp.concatenate([z0_ref[k], z1_ref[k]], axis=0)
                sol_ref[:, k * block : (k + 1) * block] = nn(both, z)

        outs = (sds((n, local_rows)), sds((n, 3 * n)))
        return call(
            kernel,
            outs,
            (g2, mine, upper, inv_low, z0, z1, *known, *theirs),
            [VM] * (6 + n_known + n_in),
            scratch=[pltpu.VMEM((subs,) + mine.shape, BF16)],
            vmem=24,
            name="finish",
        )

    def rest_of(matrix, pieces, stride, part):
        first = pieces[0].shape[0] // stride
        for p in pieces[1:]:
            part = multiply(matrix, p, first, stride, part)
        return part

    v0, x0, half = open_(loads[0])
    slot_inv, lent, gate, late = slot_inverse(v0)
    matrix, touched = lax.optimization_barrier((schur[0], touch(schur[0], lent)))
    matrix = [matrix]
    pieces, part = gather(half, lambda p: multiply(matrix, p, 0, owned + 1, None), gate)
    mine = select_first(pieces, late)
    theirs = to_subs(mine)
    part = rest_of(matrix, pieces, owned + 1, part)
    v1, half, x1, b, z0, upper, inv_low = tail_first(matrix, part, mine, theirs, slot_inv, v0, x0)

    pieces, part = gather(half, lambda p: multiply(matrix, p, 0, owned + EXTRA, None))
    mine, g01 = select(pieces, True, part)
    theirs = to_subs([mine] * n_in)
    part = rest_of(matrix, pieces, owned + EXTRA, part)
    half, z1 = tail_second(matrix, part, mine, theirs, slot_inv, v1, x1, b)

    pieces, known = gather(half, lambda p: early(g01, mine, theirs))
    mine, g2 = select(pieces, True, known[0])
    solution, misfit = finish(g2, mine, to_subs([mine] * n_in), known, upper, inv_low, z0, z1)
    return (solution[None], misfit)


def solution(mesh):
    placed = (
        P("sub", "blk", None),
        P("sub", "blk", None, None),
        P("sub", None, "blk"),
        P("sub", None, None),
        P("sub", "blk"),
    )
    return jax.shard_map(
        body, mesh=mesh, in_specs=placed, out_specs=(P("sub", None, "blk"), P()), check_vma=False
    )
```

time: 395 us -> 120 us (0.30)
  blocking collectives: 223 us -> 0 us
  Pallas kernels: 0 us -> 41.5 us
  matrix products: 37.9 us -> 0 us
  other arithmetic: 34.5 us -> 0.97 us
  waiting for transfers between devices: 48.5 us -> 21.9 us
  starting transfers between devices: 34.7 us -> 42.3 us
    psum x3 -> x0, blocking collectives: 117 us -> none  [the longest x2 78.2 us: body(): lax.psum((local_coef, products(image, image)), ('sub', 'blk'))]
    all_to_all x8 -> x0, blocking collectives: 76.2 us -> none  [the longest x6 59.3 us: to_cases(): lax.all_to_all(values, 'blk', split_axis=0, concat_axis=1, tiled=True)]
    all_to_all x10 -> x0, waiting for transfers between devices: 48.5 us -> none  [the longest x6 27.5 us: share(): lax.all_to_all(outgoing, 'sub', split_axis=0, concat_axis=0, tiled=True)]
    ppermute x0 -> x41, starting transfers between devices: none -> 42.3 us  [permute(): return lax.ppermute(v, axis, xor(lax.axis_size(axis), m))]
    pallas_call x0 -> x14, Pallas kernels: none -> 41.5 us  [call(): pl.pallas_call(kernel, out_shape=outs, in_specs=specs, out_specs=jax.tree...]
    dot_general x30 -> x0, matrix products: 36.9 us -> none  [the longest x2 21.8 us: body(): lax.dot_general(lax.all_gather(rounded, 'blk', axis=1, tiled=True), matri...]
    all_to_all x10 -> x0, starting transfers between devices: 34.7 us -> none  [the longest x6 21.2 us: share(): lax.all_to_all(outgoing, 'sub', split_axis=0, concat_axis=0, tiled=True)]
    another operation x21 -> x1, other arithmetic: 33.1 us -> 0.03 us  [slot_inverse(): same = jnp.stack(far_and_self(mine))]
  transfers between devices with their start and end apart: 10 -> 41, of which waited for: 10 -> 19; matrix products, arithmetic and copies ran while one was open for 2% -> 1% of each run, Pallas kernels for 0% -> 17%
where the time goes in v3:
time: 120 us
  starting transfers between devices  42.3 us (35%)
  Pallas kernels  41.5 us (35%)
  waiting for transfers between devices  21.9 us (18%)
  local copies, waits for them, and re-layouts  12.2 us (10%)
    ppermute x41, starting transfers between devices, permute(): return lax.ppermute(v, axis, xor(lax.axis_size(axis), m))  42.3 us
    pallas_call x14, Pallas kernels, call(): pl.pallas_call(kernel, out_shape=outs, in_specs=specs, out_specs=jax.tree...  41.5 us
    ppermute x41, waiting for transfers between devices, permute(): return lax.ppermute(v, axis, xor(lax.axis_size(axis), m))  21.9 us
    unnamed x32, local copies, waits for them, and re-layouts  11.3 us
  transfers between devices with their start and end apart: 41, of which 19 were waited for; matrix products, arithmetic and copies ran while one was open for 1% of the time, Pallas kernels for 17%

profile of v3, /device:TPU:0, one launch (start us, length us, event | category | flops | bytes accessed | tf_op | source)
XLA Modules:
  0.0 119.8 jit_solution(145991431148017000)
XLA Ops:
  0.6 0.8 eq.15
  1.6 1.0 copy-done.2
  2.6 0.9 copy-done.9
  3.5 1.6 %open.1 = (f32[8,32,128]{2,1,0:T(8,128)S(1)}, f32[8,32,128]{2,1,0:T(8,128)S(1)}, f32[9,32,128]{2,1,0:T(8,128)S(1)}) custom-call(s32[64]{0:T(128)S(1)} %convert_subtract_fusion.plain_ref, f32[32,1024]{1,0:T(8,128)S(1)} %bitcast.40, f32[8,128,128]{2,1,0:T(8,128)S(1)} %bitcast.28), custom_call_target="tpu_custom_call" | custom-call | tf_op jit(solution)/shard_map/open/pallas_call | solution.py:69
  5.1 0.5 collective-permute-start.6
  5.6 2.6 %collective-permute-start.7 = (f32[9,32,128]{2,1,0:T(8,128)S(1)}, f32[9,32,128]{2,1,0:T(8,128)S(1)}, u32[]{:S(2)}, u32[]{:S(2)}) collective-permute-start(f32[9,32,128]{2,1,0:T(8,128)S(1)} %get-tuple-element.50), channel_id=1, source_target_pairs={{0,2},{1,3},{2,0},{3,1},{4,6},{5,7},{6,4},{7,5},{8,10},{9,11},{10,... | collective-permute-start | bytes 442376 | tf_op jit(solution)/shard_map/ppermute | solution.py:116
  8.2 0.7 divide_bitcast_fusion.w_ref
  8.9 1.0 copy-done.3
  9.9 0.7 copy-done.6
  10.6 0.7 lend.1
  11.3 1.6 %collective-permute-start.2 = (bf16[4,128,128]{2,1,0:T(8,128)(2,1)S(1)}, bf16[4,128,128]{2,1,0:T(8,128)(2,1)S(1)}, u32[]{:S(2)}, u32[]{:S(2)}) collective-permute-start(bf16[4,128,128]{2,1,0:T(8,128)(2,1)S(1)} %get-tuple-element.52), channel_id=1, source_target_pairs={{0,8},{8,0},{16,24},{24,16},{1,9},{9,1},{17,25},{25,17},{2,10},{10... | collective-permute-start | bytes 393224 | tf_op jit(solution)/shard_map/ppermute | solution.py:116
  12.9 1.5 %collective-permute-start.3 = (bf16[4,128,128]{2,1,0:T(8,128)(2,1)S(1)}, bf16[4,128,128]{2,1,0:T(8,128)(2,1)S(1)}, u32[]{:S(2)}, u32[]{:S(2)}) collective-permute-start(bf16[4,128,128]{2,1,0:T(8,128)(2,1)S(1)} %get-tuple-element.53), channel_id=1, source_target_pairs={{0,16},{8,24},{16,0},{24,8},{1,17},{9,25},{17,1},{25,9},{2,18},{10... | collective-permute-start | bytes 393224 | tf_op jit(solution)/shard_map/ppermute | solution.py:116
  14.9 2.5 %collective-permute-done.2.refs_0_ = bf16[4,128,128]{2,1,0:T(8,128)(2,1)S(1)} collective-permute-done((bf16[4,128,128]{2,1,0:T(8,128)(2,1)S(1)}, bf16[4,128,128]{2,1,0:T(8,128)(2,1)S(1)}, u32[]{:S(2)}, u32[]{:S(2)}) %collective-permute-start.2) | collective-permute-done | bytes 131104 | tf_op jit(solution)/shard_map/ppermute | solution.py:116
  17.3 2.6 %collective-permute-start = (f32[9,32,128]{2,1,0:T(8,128)S(1)}, f32[9,32,128]{2,1,0:T(8,128)S(1)}, u32[]{:S(2)}, u32[]{:S(2)}) collective-permute-start(f32[9,32,128]{2,1,0:T(8,128)S(1)} %get-tuple-element.50), channel_id=1, source_target_pairs={{0,4},{1,5},{2,6},{3,7},{4,0},{5,1},{6,2},{7,3},{8,12},{9,13},{10,... | collective-permute-start | bytes 442376 | tf_op jit(solution)/shard_map/ppermute | solution.py:116
  19.9 1.0 collective-permute-done.3.refs_1_
  21.0 2.5 %collective-permute-start.1 = (f32[9,32,128]{2,1,0:T(8,128)S(1)}, f32[9,32,128]{2,1,0:T(8,128)S(1)}, u32[]{:S(2)}, u32[]{:S(2)}) collective-permute-start(f32[9,32,128]{2,1,0:T(8,128)S(1)} %get-tuple-element.50), channel_id=1, source_target_pairs={{0,6},{1,7},{2,4},{3,5},{4,2},{5,3},{6,0},{7,1},{8,14},{9,15},{10,... | collective-permute-start | bytes 442376 | tf_op jit(solution)/shard_map/ppermute | solution.py:116
  23.4 1.0 copy-done.4
  24.5 0.7 copy-done.7
  25.2 0.7 deal.1
  26.0 0.5 collective-permute-start.8
  26.5 0.9 collective-permute-done.5
  27.5 0.7 collective-permute-start.11
  28.2 1.2 %collective-permute-start.12 = (bf16[3,64,128]{2,1,0:T(8,128)(2,1)S(1)}, bf16[3,64,128]{2,1,0:T(8,128)(2,1)S(1)}, u32[]{:S(2)}, u32[]{:S(2)}) collective-permute-start(bf16[3,64,128]{2,1,0:T(8,128)(2,1)S(1)} %get-tuple-element.100), channel_id=1, source_target_pairs={{0,4},{1,5},{2,6},{3,7},{4,0},{5,1},{6,2},{7,3},{8,12},{9,13},{10,... | collective-permute-start | bytes 147464 | tf_op jit(solution)/shard_map/ppermute | solution.py:116
  29.5 2.5 %collective-permute-start.13 = (bf16[3,64,128]{2,1,0:T(8,128)(2,1)S(1)}, bf16[3,64,128]{2,1,0:T(8,128)(2,1)S(1)}, u32[]{:S(2)}, u32[]{:S(2)}) collective-permute-start(bf16[3,64,128]{2,1,0:T(8,128)(2,1)S(1)} %get-tuple-element.99), channel_id=1, source_target_pairs={{0,6},{1,7},{2,4},{3,5},{4,2},{5,3},{6,0},{7,1},{8,14},{9,15},{10,... | collective-permute-start | bytes 147464 | tf_op jit(solution)/shard_map/ppermute | solution.py:116
  32.0 5.8 %copy-done = bf16[1,1024,8192]{2,1,0:T(8,128)(2,1)S(1)} copy-done((bf16[1,1024,8192]{2,1,0:T(8,128)(2,1)S(1)}, bf16[1,1024,8192]{2,1,0:T(8,128)(2,1)}, u32[]{:S(2)}) %copy-start) | copy-done | bytes 16777240
  37.7 3.2 %multiply.4.rest_1_ = f32[32,1024]{1,0:T(8,128)S(1)} custom-call(s32[64]{0:T(128)S(1)} %convert_subtract_fusion.plain_ref, f32[36,32,128]{2,1,0:T(8,128)S(1)} %constant_dynamic-update-slice_fusion.p_ref.refs_0_, bf16[1024,8192]{1,0:T(8,128)(2,1)S(1)} %bitcast.22), custom_call_target="tpu_custom_call" | custom-call | flops 268435456 | bytes 8388608 | tf_op jit(solution)/shard_map/multiply/pallas_call | solution.py:69
  41.2 1.9 %collective-permute-start.15 = (bf16[3,64,128]{2,1,0:T(8,128)(2,1)S(1)}, bf16[3,64,128]{2,1,0:T(8,128)(2,1)S(1)}, u32[]{:S(2)}, u32[]{:S(2)}) collective-permute-start(bf16[3,64,128]{2,1,0:T(8,128)(2,1)S(1)} %fusion.1.after_ref), channel_id=1, source_target_pairs={{0,4},{1,5},{2,6},{3,7},{4,0},{5,1},{6,2},{7,3},{8,12},{9,13},{10,... | collective-permute-start | bytes 147464 | tf_op jit(solution)/shard_map/ppermute | solution.py:116
  43.1 2.5 %collective-permute-start.16 = (bf16[3,64,128]{2,1,0:T(8,128)(2,1)S(1)}, bf16[3,64,128]{2,1,0:T(8,128)(2,1)S(1)}, u32[]{:S(2)}, u32[]{:S(2)}) collective-permute-start(bf16[3,64,128]{2,1,0:T(8,128)(2,1)S(1)} %fusion.1.after_ref), channel_id=1, source_target_pairs={{0,6},{1,7},{2,4},{3,5},{4,2},{5,3},{6,0},{7,1},{8,14},{9,15},{10,... | collective-permute-start | bytes 147464 | tf_op jit(solution)/shard_map/ppermute | solution.py:116
  45.7 2.7 %collective-permute-done.15 = bf16[3,64,128]{2,1,0:T(8,128)(2,1)S(1)} collective-permute-done((bf16[3,64,128]{2,1,0:T(8,128)(2,1)S(1)}, bf16[3,64,128]{2,1,0:T(8,128)(2,1)S(1)}, u32[]{:S(2)}, u32[]{:S(2)}) %collective-permute-start.15) | collective-permute-done | bytes 49184 | tf_op jit(solution)/shard_map/ppermute | solution.py:116
  48.4 0.6 collective-permute-done.16
  49.2 0.7 select_first.1
  49.9 0.9 collective-permute-start.18
  50.8 1.6 %collective-permute-start.19 = (f32[5,32,128]{2,1,0:T(8,128)S(1)}, f32[5,32,128]{2,1,0:T(8,128)S(1)}, u32[]{:S(2)}, u32[]{:S(2)}) collective-permute-start(f32[5,32,128]{2,1,0:T(8,128)S(1)} %get-tuple-element.62.rest_2_), channel_id=1, source_target_pairs={{0,16},{8,24},{16,0},{24,8},{1,17},{9,25},{17,1},{25,9},{2,18},{10... | collective-permute-start | bytes 245768 | tf_op jit(solution)/shard_map/ppermute | solution.py:116
  52.5 1.0 collective-permute-start.20
  53.5 3.2 %multiply.5.part_ref = f32[32,1024]{1,0:T(8,128)S(1)} custom-call(s32[64]{0:T(128)S(1)} %convert_subtract_fusion.plain_ref, f32[36,32,128]{2,1,0:T(8,128)S(1)} %constant_dynamic-update-slice_fusion.4.p_ref.refs_1_, bf16[1024,8192]{1,0:T(8,128)(2,1)S(1)} %bitcast.23, f32[32,1024]{1,0:T(8,128)S(1)} %multiply.4.rest_1_), custom_call_target="tpu_custom_call" | custom-call | flops 268435456 | bytes 8388608 | tf_op jit(solution)/shard_map/multiply/pallas_call | solution.py:69
  56.7 1.1 collective-permute-done.20.rest_6_
  57.8 7.7 %tail_first.1 = (f32[8,32,128]{2,1,0:T(8,128)S(1)}, bf16[11,32,128]{2,1,0:T(8,128)(2,1)S(1)}, f32[8,32,128]{2,1,0:T(8,128)S(1)}, f32[8,32,128]{2,1,0:T(8,128)S(1...) custom-call(s32[4,4]{1,0:T(4,128)S(1)} %bitcast.36, ...), custom_call_target="tpu_custom_call" | custom-call | tf_op jit(solution)/shard_map/tail_first/pallas_call | solution.py:69
  65.6 0.8 collective-permute-start.24
  66.4 2.0 %collective-permute-start.21 = (bf16[11,32,128]{2,1,0:T(8,128)(2,1)S(1)}, bf16[11,32,128]{2,1,0:T(8,128)(2,1)S(1)}, u32[]{:S(2)}, u32[]{:S(2)}) collective-permute-start(bf16[11,32,128]{2,1,0:T(8,128)(2,1)S(1)} %get-tuple-element.64), channel_id=1, source_target_pairs={{0,4},{1,5},{2,6},{3,7},{4,0},{5,1},{6,2},{7,3},{8,12},{9,13},{10,... | collective-permute-start | bytes 270344 | tf_op jit(solution)/shard_map/ppermute | solution.py:116
  68.4 1.6 %collective-permute-start.22 = (bf16[11,32,128]{2,1,0:T(8,128)(2,1)S(1)}, bf16[11,32,128]{2,1,0:T(8,128)(2,1)S(1)}, u32[]{:S(2)}, u32[]{:S(2)}) collective-permute-start(bf16[11,32,128]{2,1,0:T(8,128)(2,1)S(1)} %get-tuple-element.64), channel_id=1, source_target_pairs={{0,6},{1,7},{2,4},{3,5},{4,2},{5,3},{6,0},{7,1},{8,14},{9,15},{10,... | collective-permute-start | bytes 270344 | tf_op jit(solution)/shard_map/ppermute | solution.py:116
  70.0 1.7 %collective-permute-done.24 = bf16[11,32,128]{2,1,0:T(8,128)(2,1)S(1)} collective-permute-done((bf16[11,32,128]{2,1,0:T(8,128)(2,1)S(1)}, bf16[11,32,128]{2,1,0:T(8,128)(2,1)S(1)}, u32[]{:S(2)}, u32[]{:S(2)}) %collective-permute-start.24) | collective-permute-done | bytes 90144 | tf_op jit(solution)/shard_map/ppermute | solution.py:116
  71.7 1.2 %collective-permute-done.25 = bf16[11,32,128]{2,1,0:T(8,128)(2,1)S(1)} collective-permute-done((bf16[11,32,128]{2,1,0:T(8,128)(2,1)S(1)}, bf16[11,32,128]{2,1,0:T(8,128)(2,1)S(1)}, u32[]{:S(2)}, u32[]{:S(2)}) %collective-permute-start.25) | collective-permute-done | bytes 90144 | tf_op jit(solution)/shard_map/ppermute | solution.py:116
  73.0 3.1 %multiply.6.rest_1_.after_ref = f32[32,1024]{1,0:T(8,128)S(1)} custom-call(s32[64]{0:T(128)S(1)} %convert_subtract_fusion.plain_ref, bf16[44,32,128]{2,1,0:T(8,128)(2,1)S(1)} %constant_dynamic-update-slice_fusion.8.p_ref.refs_0_, bf16[1024,8192]{1,0:T(8,128)(2,1)S(1)} %bitcast.25), custom_call_target="tpu_custom_call" | custom-call | flops 268435456 | bytes 8388608 | tf_op jit(solution)/shard_map/multiply/pallas_call | solution.py:69
  76.1 0.5 collective-permute-done.21
  76.6 0.5 collective-permute-start.27
  77.1 0.8 collective-permute-done.26
  78.0 0.7 select.2
  78.8 1.4 %collective-permute-start.28 = (bf16[15,32,128]{2,1,0:T(8,128)(2,1)S(1)}, bf16[15,32,128]{2,1,0:T(8,128)(2,1)S(1)}, u32[]{:S(2)}, u32[]{:S(2)}) collective-permute-start(bf16[15,32,128]{2,1,0:T(8,128)(2,1)S(1)} %get-tuple-element.71.mine_ref.s_ref), channel_id=1, source_target_pairs={{0,8},{8,0},{16,24},{24,16},{1,9},{9,1},{17,25},{25,17},{2,10},{10... | collective-permute-start | bytes 368648 | tf_op jit(solution)/shard_map/ppermute | solution.py:116
  80.2 1.0 collective-permute-start.29
  81.1 1.2 collective-permute-start.30
  82.3 3.1 %multiply.7.part_ref = f32[32,1024]{1,0:T(8,128)S(1)} custom-call(s32[64]{0:T(128)S(1)} %convert_subtract_fusion.plain_ref, bf16[44,32,128]{2,1,0:T(8,128)(2,1)S(1)} %constant_dynamic-update-slice_fusion.12.p_ref.refs_1_, bf16[1024,8192]{1,0:T(8,128)(2,1)S(1)} %bitcast.26, f32[32,1024]{1,0:T(8,128)S(1)} %multiply.6.rest_1_.after_ref), custom_call_target="tpu_custom_call" | custom-call | flops 268435456 | bytes 8388608 | tf_op jit(solution)/shard_map/multiply/pallas_call | solution.py:69
  85.4 2.7 %collective-permute-done.29.rest_2_.rest_1_ = bf16[15,32,128]{2,1,0:T(8,128)(2,1)S(1)} collective-permute-done((bf16[15,32,128]{2,1,0:T(8,128)(2,1)S(1)}, bf16[15,32,128]{2,1,0:T(8,128)(2,1)S(1)}, u32[]{:S(2)}, u32[]{:S(2)}) %collective-permute-start.29) | collective-permute-done | bytes 122912 | tf_op jit(solution)/shard_map/ppermute | solution.py:116
  88.1 4.2 %tail_second.1 = (bf16[11,32,128]{2,1,0:T(8,128)(2,1)S(1)}, f32[8,32,128]{2,1,0:T(8,128)S(1)}) custom-call(s32[4,4]{1,0:T(4,128)S(1)} %bitcast.38, f32[32,1024]{1,0:T(8,128)S(1)} %multiply.7.part_ref, f32[8,32,128]{2,1,0:T(8,128)S(1)} %get-tuple-element.68.b_ref, bf16[4,3,64,128]{3,2,1,0:T(8,128)(2,1)S(1)} %pad_maximum_fusion.2.s0, ...), custom_call_target="tpu_custom_call" | custom-call | tf_op jit(solution)/shard_map/tail_second/pallas_call | solution.py:69
  92.3 2.1 %collective-permute-start.31 = (bf16[11,32,128]{2,1,0:T(8,128)(2,1)S(1)}, bf16[11,32,128]{2,1,0:T(8,128)(2,1)S(1)}, u32[]{:S(2)}, u32[]{:S(2)}) collective-permute-start(bf16[11,32,128]{2,1,0:T(8,128)(2,1)S(1)} %get-tuple-element.72), channel_id=1, source_target_pairs={{0,4},{1,5},{2,6},{3,7},{4,0},{5,1},{6,2},{7,3},{8,12},{9,13},{10,... | collective-permute-start | bytes 270344 | tf_op jit(solution)/shard_map/ppermute | solution.py:116
  94.4 2.0 %collective-permute-start.32 = (bf16[11,32,128]{2,1,0:T(8,128)(2,1)S(1)}, bf16[11,32,128]{2,1,0:T(8,128)(2,1)S(1)}, u32[]{:S(2)}, u32[]{:S(2)}) collective-permute-start(bf16[11,32,128]{2,1,0:T(8,128)(2,1)S(1)} %get-tuple-element.72), channel_id=1, source_target_pairs={{0,6},{1,7},{2,4},{3,5},{4,2},{5,3},{6,0},{7,1},{8,14},{9,15},{10,... | collective-permute-start | bytes 270344 | tf_op jit(solution)/shard_map/ppermute | solution.py:116
  96.4 5.8 %early.1 = (f32[32,32]{1,0:T(8,128)S(1)}, f32[32,32]{1,0:T(8,128)S(1)}, f32[32,32]{1,0:T(8,128)S(1)}, f32[32,32]{1,0:T(8,128)S(1)}, f32[32,32]{1,0:T(8,128)S(1)}...) custom-call(f32[32,128]{1,0:T(8,128)S(1)} %get-tuple-element.73.g_ref, ...), custom_call_target="tpu_custom_call" | custom-call | flops 100000000 | bytes 10000000 | tf_op jit(solution)/shard_map/early/pallas_call | solution.py:69
  102.3 0.5 collective-permute-start.37
  104.3 0.7 select.3
  105.0 0.8 collective-permute-start.38
  105.8 1.0 collective-permute-start.39
  106.8 1.8 %collective-permute-start.40 = (bf16[15,32,128]{2,1,0:T(8,128)(2,1)S(1)}, bf16[15,32,128]{2,1,0:T(8,128)(2,1)S(1)}, u32[]{:S(2)}, u32[]{:S(2)}) collective-permute-start(bf16[15,32,128]{2,1,0:T(8,128)(2,1)S(1)} %get-tuple-element.85.s_ref), channel_id=1, source_target_pairs={{0,24},{8,16},{16,8},{24,0},{1,25},{9,17},{17,9},{25,1},{2,26},{10... | collective-permute-start | bytes 368648 | tf_op jit(solution)/shard_map/ppermute | solution.py:116
  108.6 2.7 %collective-permute-done.38.rest_7_ = bf16[15,32,128]{2,1,0:T(8,128)(2,1)S(1)} collective-permute-done((bf16[15,32,128]{2,1,0:T(8,128)(2,1)S(1)}, bf16[15,32,128]{2,1,0:T(8,128)(2,1)S(1)}, u32[]{:S(2)}, u32[]{:S(2)}) %collective-permute-start.38) | collective-permute-done | bytes 122912 | tf_op jit(solution)/shard_map/ppermute | solution.py:116
  111.7 2.0 %collective-permute-done.40.rest_9_ = bf16[15,32,128]{2,1,0:T(8,128)(2,1)S(1)} collective-permute-done((bf16[15,32,128]{2,1,0:T(8,128)(2,1)S(1)}, bf16[15,32,128]{2,1,0:T(8,128)(2,1)S(1)}, u32[]{:S(2)}, u32[]{:S(2)}) %collective-permute-start.40) | collective-permute-done | bytes 122912 | tf_op jit(solution)/shard_map/ppermute | solution.py:116
  113.7 6.1 %finish.1 = (f32[32,1024]{1,0:T(8,128)}, f32[32,96]{1,0:T(8,128)}) custom-call(f32[32,128]{1,0:T(8,128)S(1)} %get-tuple-element.84.g_ref, bf16[15,32,128]{2,1,0:T(8,128)(2,1)S(1)} %get-tuple-element.85.s_ref, f32[32,32]{1,0:T(8,128)S(1)} %get-tuple-element.86.f_ref, f32[32,32]{1,0:T(8,128)S(1)} %get-tuple-element.87.t_ref, ...), custom_call_target="tpu_custom_call" | custom-call | tf_op jit(solution)/shard_map/finish/pallas_call | solution.py:69
  (78 shorter events, 3.5 us)
Async XLA Ops:
  0.6 48.6 %copy-start.8 = (s32[1,4,4]{2,1,0:T(4,128)S(1)}, s32[1,4,4]{2,1,0:T(4,128)}, u32[]{:S(2)}) copy-start(s32[1,4,4]{2,1,0:T(4,128)} %param.8) | copy-start | bytes 196
  1.6 1.0 copy-start.2
  2.6 0.9 copy-start.9
  5.1 21.4 %collective-permute-start.6 = (f32[9,32,128]{2,1,0:T(8,128)S(1)}, f32[9,32,128]{2,1,0:T(8,128)S(1)}, u32[]{:S(2)}, u32[]{:S(2)}) collective-permute-start(f32[9,32,128]{2,1,0:T(8,128)S(1)} %get-tuple-element.50), channel_id=1, source_target_pairs={{0,1},{1,0},{2,3},{3,2},{4,5},{5,4},{6,7},{7,6},{8,9},{9,8},{10,11... | collective-permute-start | bytes 442376 | tf_op jit(solution)/shard_map/ppermute | solution.py:116
  5.6 20.4 %collective-permute-start.7 = (f32[9,32,128]{2,1,0:T(8,128)S(1)}, f32[9,32,128]{2,1,0:T(8,128)S(1)}, u32[]{:S(2)}, u32[]{:S(2)}) collective-permute-start(f32[9,32,128]{2,1,0:T(8,128)S(1)} %get-tuple-element.50), channel_id=1, source_target_pairs={{0,2},{1,3},{2,0},{3,1},{4,6},{5,7},{6,4},{7,5},{8,10},{9,11},{10,... | collective-permute-start | bytes 442376 | tf_op jit(solution)/shard_map/ppermute | solution.py:116
  8.9 1.0 copy-start.3
  9.9 0.7 copy-start.6
  11.3 6.0 %collective-permute-start.2 = (bf16[4,128,128]{2,1,0:T(8,128)(2,1)S(1)}, bf16[4,128,128]{2,1,0:T(8,128)(2,1)S(1)}, u32[]{:S(2)}, u32[]{:S(2)}) collective-permute-start(bf16[4,128,128]{2,1,0:T(8,128)(2,1)S(1)} %get-tuple-element.52), channel_id=1, source_target_pairs={{0,8},{8,0},{16,24},{24,16},{1,9},{9,1},{17,25},{25,17},{2,10},{10... | collective-permute-start | bytes 393224 | tf_op jit(solution)/shard_map/ppermute | solution.py:116
  12.9 8.1 %collective-permute-start.3 = (bf16[4,128,128]{2,1,0:T(8,128)(2,1)S(1)}, bf16[4,128,128]{2,1,0:T(8,128)(2,1)S(1)}, u32[]{:S(2)}, u32[]{:S(2)}) collective-permute-start(bf16[4,128,128]{2,1,0:T(8,128)(2,1)S(1)} %get-tuple-element.53), channel_id=1, source_target_pairs={{0,16},{8,24},{16,0},{24,8},{1,17},{9,25},{17,1},{25,9},{2,18},{10... | collective-permute-start | bytes 393224 | tf_op jit(solution)/shard_map/ppermute | solution.py:116
  14.4 9.0 %collective-permute-start.4 = (bf16[4,128,128]{2,1,0:T(8,128)(2,1)S(1)}, bf16[4,128,128]{2,1,0:T(8,128)(2,1)S(1)}, u32[]{:S(2)}, u32[]{:S(2)}) collective-permute-start(bf16[4,128,128]{2,1,0:T(8,128)(2,1)S(1)} %get-tuple-element.54), channel_id=1, source_target_pairs={{0,24},{8,16},{16,8},{24,0},{1,25},{9,17},{17,9},{25,1},{2,26},{10... | collective-permute-start | bytes 393224 | tf_op jit(solution)/shard_map/ppermute | solution.py:116
  17.3 23.6 %collective-permute-start = (f32[9,32,128]{2,1,0:T(8,128)S(1)}, f32[9,32,128]{2,1,0:T(8,128)S(1)}, u32[]{:S(2)}, u32[]{:S(2)}) collective-permute-start(f32[9,32,128]{2,1,0:T(8,128)S(1)} %get-tuple-element.50), channel_id=1, source_target_pairs={{0,4},{1,5},{2,6},{3,7},{4,0},{5,1},{6,2},{7,3},{8,12},{9,13},{10,... | collective-permute-start | bytes 442376 | tf_op jit(solution)/shard_map/ppermute | solution.py:116
  21.0 20.0 %collective-permute-start.1 = (f32[9,32,128]{2,1,0:T(8,128)S(1)}, f32[9,32,128]{2,1,0:T(8,128)S(1)}, u32[]{:S(2)}, u32[]{:S(2)}) collective-permute-start(f32[9,32,128]{2,1,0:T(8,128)S(1)} %get-tuple-element.50), channel_id=1, source_target_pairs={{0,6},{1,7},{2,4},{3,5},{4,2},{5,3},{6,0},{7,1},{8,14},{9,15},{10,... | collective-permute-start | bytes 442376 | tf_op jit(solution)/shard_map/ppermute | solution.py:116
  23.4 1.0 copy-start.4
  24.5 0.7 copy-start.7
  25.9 1.5 %collective-permute-start.5 = (bf16[4,3,64,128]{3,2,1,0:T(8,128)(2,1)S(1)}, bf16[4,3,64,128]{3,2,1,0:T(8,128)(2,1)S(1)}, u32[]{:S(2)}, u32[]{:S(2)}) collective-permute-start(bf16[4,3,64,128]{3,2,1,0:T(8,128)(2,1)S(1)} %get-tuple-element.56), channel_id=1, source_target_pairs={{0,1},{1,0},{2,3},{3,2},{4,5},{5,4},{6,7},{7,6},{8,9},{9,8},{10,11... | collective-permute-start | bytes 589832 | tf_op jit(solution)/shard_map/ppermute | solution.py:116
  26.0 3.5 %collective-permute-start.8 = (f32[9,32,128]{2,1,0:T(8,128)S(1)}, f32[9,32,128]{2,1,0:T(8,128)S(1)}, u32[]{:S(2)}, u32[]{:S(2)}) collective-permute-start(f32[9,32,128]{2,1,0:T(8,128)S(1)} %collective-permute-done.7), channel_id=1, source_target_pairs={{0,1},{1,0},{2,3},{3,2},{4,5},{5,4},{6,7},{7,6},{8,9},{9,8},{10,11... | collective-permute-start | bytes 442376 | tf_op jit(solution)/shard_map/ppermute | solution.py:116
  27.5 13.5 %collective-permute-start.11 = (bf16[3,64,128]{2,1,0:T(8,128)(2,1)S(1)}, bf16[3,64,128]{2,1,0:T(8,128)(2,1)S(1)}, u32[]{:S(2)}, u32[]{:S(2)}) collective-permute-start(bf16[3,64,128]{2,1,0:T(8,128)(2,1)S(1)} %get-tuple-element.98), channel_id=1, source_target_pairs={{0,2},{1,3},{2,0},{3,1},{4,6},{5,7},{6,4},{7,5},{8,10},{9,11},{10,... | collective-permute-start | bytes 147464 | tf_op jit(solution)/shard_map/ppermute | solution.py:116
  28.2 12.8 %collective-permute-start.12 = (bf16[3,64,128]{2,1,0:T(8,128)(2,1)S(1)}, bf16[3,64,128]{2,1,0:T(8,128)(2,1)S(1)}, u32[]{:S(2)}, u32[]{:S(2)}) collective-permute-start(bf16[3,64,128]{2,1,0:T(8,128)(2,1)S(1)} %get-tuple-element.100), channel_id=1, source_target_pairs={{0,4},{1,5},{2,6},{3,7},{4,0},{5,1},{6,2},{7,3},{8,12},{9,13},{10,... | collective-permute-start | bytes 147464 | tf_op jit(solution)/shard_map/ppermute | solution.py:116
  29.5 11.6 %collective-permute-start.13 = (bf16[3,64,128]{2,1,0:T(8,128)(2,1)S(1)}, bf16[3,64,128]{2,1,0:T(8,128)(2,1)S(1)}, u32[]{:S(2)}, u32[]{:S(2)}) collective-permute-start(bf16[3,64,128]{2,1,0:T(8,128)(2,1)S(1)} %get-tuple-element.99), channel_id=1, source_target_pairs={{0,6},{1,7},{2,4},{3,5},{4,2},{5,3},{6,0},{7,1},{8,14},{9,15},{10,... | collective-permute-start | bytes 147464 | tf_op jit(solution)/shard_map/ppermute | solution.py:116
  32.0 5.8 %copy-start = (bf16[1,1024,8192]{2,1,0:T(8,128)(2,1)S(1)}, bf16[1,1024,8192]{2,1,0:T(8,128)(2,1)}, u32[]{:S(2)}) copy-start(bf16[1,1024,8192]{2,1,0:T(8,128)(2,1)} %param.5) | copy-start | bytes 50331652
  37.7 15.7 %copy-start.1 = (bf16[1,1024,8192]{2,1,0:T(8,128)(2,1)S(1)}, bf16[1,1024,8192]{2,1,0:T(8,128)(2,1)}, u32[]{:S(2)}) copy-start(bf16[1,1024,8192]{2,1,0:T(8,128)(2,1)} %param.5) | copy-start | bytes 50331652
  37.7 20.1 %copy-start.5 = (f32[1,8,128,128]{3,2,1,0:T(8,128)S(1)}, f32[1,8,128,128]{3,2,1,0:T(8,128)}, u32[]{:S(2)}) copy-start(f32[1,8,128,128]{3,2,1,0:T(8,128)} %param.6) | copy-start | bytes 1572868
  41.0 8.1 %collective-permute-start.9 = (f32[9,32,128]{2,1,0:T(8,128)S(1)}, f32[9,32,128]{2,1,0:T(8,128)S(1)}, u32[]{:S(2)}, u32[]{:S(2)}) collective-permute-start(f32[9,32,128]{2,1,0:T(8,128)S(1)} %collective-permute-done), channel_id=1, source_target_pairs={{0,1},{1,0},{2,3},{3,2},{4,5},{5,4},{6,7},{7,6},{8,9},{9,8},{10,11... | collective-permute-start | bytes 442376 | tf_op jit(solution)/shard_map/ppermute | solution.py:116
  41.1 4.5 %collective-permute-start.14 = (bf16[3,64,128]{2,1,0:T(8,128)(2,1)S(1)}, bf16[3,64,128]{2,1,0:T(8,128)(2,1)S(1)}, u32[]{:S(2)}, u32[]{:S(2)}) collective-permute-start(bf16[3,64,128]{2,1,0:T(8,128)(2,1)S(1)} %fusion.1.after_ref), channel_id=1, source_target_pairs={{0,2},{1,3},{2,0},{3,1},{4,6},{5,7},{6,4},{7,5},{8,10},{9,11},{10,... | collective-permute-start | bytes 147464 | tf_op jit(solution)/shard_map/ppermute | solution.py:116
  41.2 7.2 %collective-permute-start.15 = (bf16[3,64,128]{2,1,0:T(8,128)(2,1)S(1)}, bf16[3,64,128]{2,1,0:T(8,128)(2,1)S(1)}, u32[]{:S(2)}, u32[]{:S(2)}) collective-permute-start(bf16[3,64,128]{2,1,0:T(8,128)(2,1)S(1)} %fusion.1.after_ref), channel_id=1, source_target_pairs={{0,4},{1,5},{2,6},{3,7},{4,0},{5,1},{6,2},{7,3},{8,12},{9,13},{10,... | collective-permute-start | bytes 147464 | tf_op jit(solution)/shard_map/ppermute | solution.py:116
  43.1 5.9 %collective-permute-start.16 = (bf16[3,64,128]{2,1,0:T(8,128)(2,1)S(1)}, bf16[3,64,128]{2,1,0:T(8,128)(2,1)S(1)}, u32[]{:S(2)}, u32[]{:S(2)}) collective-permute-start(bf16[3,64,128]{2,1,0:T(8,128)(2,1)S(1)} %fusion.1.after_ref), channel_id=1, source_target_pairs={{0,6},{1,7},{2,4},{3,5},{4,2},{5,3},{6,0},{7,1},{8,14},{9,15},{10,... | collective-permute-start | bytes 147464 | tf_op jit(solution)/shard_map/ppermute | solution.py:116
  45.6 3.6 %collective-permute-start.10 = (f32[9,32,128]{2,1,0:T(8,128)S(1)}, f32[9,32,128]{2,1,0:T(8,128)S(1)}, u32[]{:S(2)}, u32[]{:S(2)}) collective-permute-start(f32[9,32,128]{2,1,0:T(8,128)S(1)} %collective-permute-done.1), channel_id=1, source_target_pairs={{0,1},{1,0},{2,3},{3,2},{4,5},{5,4},{6,7},{7,6},{8,9},{9,8},{10,11... | collective-permute-start | bytes 442376 | tf_op jit(solution)/shard_map/ppermute | solution.py:116
  49.0 8.8 %collective-permute-start.17 = (bf16[4,3,64,128]{3,2,1,0:T(8,128)(2,1)S(1)}, bf16[4,3,64,128]{3,2,1,0:T(8,128)(2,1)S(1)}, u32[]{:S(2)}, u32[]{:S(2)}) collective-permute-start(bf16[4,3,64,128]{3,2,1,0:T(8,128)(2,1)S(1)} %pad_maximum_fusion.2.s0), channel_id=1, source_target_pairs={{0,1},{1,0},{2,3},{3,2},{4,5},{5,4},{6,7},{7,6},{8,9},{9,8},{10,11... | collective-permute-start | bytes 589832 | tf_op jit(solution)/shard_map/ppermute | solution.py:116
  49.9 6.8 %collective-permute-start.18 = (f32[5,32,128]{2,1,0:T(8,128)S(1)}, f32[5,32,128]{2,1,0:T(8,128)S(1)}, u32[]{:S(2)}, u32[]{:S(2)}) collective-permute-start(f32[5,32,128]{2,1,0:T(8,128)S(1)} %get-tuple-element.61.rest_1_), channel_id=1, source_target_pairs={{0,8},{8,0},{16,24},{24,16},{1,9},{9,1},{17,25},{25,17},{2,10},{10... | collective-permute-start | bytes 245768 | tf_op jit(solution)/shard_map/ppermute | solution.py:116
  50.8 5.8 %collective-permute-start.19 = (f32[5,32,128]{2,1,0:T(8,128)S(1)}, f32[5,32,128]{2,1,0:T(8,128)S(1)}, u32[]{:S(2)}, u32[]{:S(2)}) collective-permute-start(f32[5,32,128]{2,1,0:T(8,128)S(1)} %get-tuple-element.62.rest_2_), channel_id=1, source_target_pairs={{0,16},{8,24},{16,0},{24,8},{1,17},{9,25},{17,1},{25,9},{2,18},{10... | collective-permute-start | bytes 245768 | tf_op jit(solution)/shard_map/ppermute | solution.py:116
  52.5 5.3 %collective-permute-start.20 = (f32[5,32,128]{2,1,0:T(8,128)S(1)}, f32[5,32,128]{2,1,0:T(8,128)S(1)}, u32[]{:S(2)}, u32[]{:S(2)}) collective-permute-start(f32[5,32,128]{2,1,0:T(8,128)S(1)} %get-tuple-element.63.rest_3_), channel_id=1, source_target_pairs={{0,24},{8,16},{16,8},{24,0},{1,25},{9,17},{17,9},{25,1},{2,26},{10... | collective-permute-start | bytes 245768 | tf_op jit(solution)/shard_map/ppermute | solution.py:116
  65.5 6.2 %collective-permute-start.23 = (bf16[11,32,128]{2,1,0:T(8,128)(2,1)S(1)}, bf16[11,32,128]{2,1,0:T(8,128)(2,1)S(1)}, u32[]{:S(2)}, u32[]{:S(2)}) collective-permute-start(bf16[11,32,128]{2,1,0:T(8,128)(2,1)S(1)} %get-tuple-element.64), channel_id=1, source_target_pairs={{0,1},{1,0},{2,3},{3,2},{4,5},{5,4},{6,7},{7,6},{8,9},{9,8},{10,11... | collective-permute-start | bytes 270344 | tf_op jit(solution)/shard_map/ppermute | solution.py:116
  65.6 6.1 %collective-permute-start.24 = (bf16[11,32,128]{2,1,0:T(8,128)(2,1)S(1)}, bf16[11,32,128]{2,1,0:T(8,128)(2,1)S(1)}, u32[]{:S(2)}, u32[]{:S(2)}) collective-permute-start(bf16[11,32,128]{2,1,0:T(8,128)(2,1)S(1)} %get-tuple-element.64), channel_id=1, source_target_pairs={{0,2},{1,3},{2,0},{3,1},{4,6},{5,7},{6,4},{7,5},{8,10},{9,11},{10,... | collective-permute-start | bytes 270344 | tf_op jit(solution)/shard_map/ppermute | solution.py:116
  66.4 10.2 %collective-permute-start.21 = (bf16[11,32,128]{2,1,0:T(8,128)(2,1)S(1)}, bf16[11,32,128]{2,1,0:T(8,128)(2,1)S(1)}, u32[]{:S(2)}, u32[]{:S(2)}) collective-permute-start(bf16[11,32,128]{2,1,0:T(8,128)(2,1)S(1)} %get-tuple-element.64), channel_id=1, source_target_pairs={{0,4},{1,5},{2,6},{3,7},{4,0},{5,1},{6,2},{7,3},{8,12},{9,13},{10,... | collective-permute-start | bytes 270344 | tf_op jit(solution)/shard_map/ppermute | solution.py:116
  68.4 8.2 %collective-permute-start.22 = (bf16[11,32,128]{2,1,0:T(8,128)(2,1)S(1)}, bf16[11,32,128]{2,1,0:T(8,128)(2,1)S(1)}, u32[]{:S(2)}, u32[]{:S(2)}) collective-permute-start(bf16[11,32,128]{2,1,0:T(8,128)(2,1)S(1)} %get-tuple-element.64), channel_id=1, source_target_pairs={{0,6},{1,7},{2,4},{3,5},{4,2},{5,3},{6,0},{7,1},{8,14},{9,15},{10,... | collective-permute-start | bytes 270344 | tf_op jit(solution)/shard_map/ppermute | solution.py:116
  71.7 1.3 %collective-permute-start.25 = (bf16[11,32,128]{2,1,0:T(8,128)(2,1)S(1)}, bf16[11,32,128]{2,1,0:T(8,128)(2,1)S(1)}, u32[]{:S(2)}, u32[]{:S(2)}) collective-permute-start(bf16[11,32,128]{2,1,0:T(8,128)(2,1)S(1)} %collective-permute-done.24), channel_id=1, source_target_pairs={{0,1},{1,0},{2,3},{3,2},{4,5},{5,4},{6,7},{7,6},{8,9},{9,8},{10,11... | collective-permute-start | bytes 270344 | tf_op jit(solution)/shard_map/ppermute | solution.py:116
  76.6 1.3 %collective-permute-start.26 = (bf16[11,32,128]{2,1,0:T(8,128)(2,1)S(1)}, bf16[11,32,128]{2,1,0:T(8,128)(2,1)S(1)}, u32[]{:S(2)}, u32[]{:S(2)}) collective-permute-start(bf16[11,32,128]{2,1,0:T(8,128)(2,1)S(1)} %collective-permute-done.21), channel_id=1, source_target_pairs={{0,1},{1,0},{2,3},{3,2},{4,5},{5,4},{6,7},{7,6},{8,9},{9,8},{10,11... | collective-permute-start | bytes 270344 | tf_op jit(solution)/shard_map/ppermute | solution.py:116
  76.6 1.4 %collective-permute-start.27 = (bf16[11,32,128]{2,1,0:T(8,128)(2,1)S(1)}, bf16[11,32,128]{2,1,0:T(8,128)(2,1)S(1)}, u32[]{:S(2)}, u32[]{:S(2)}) collective-permute-start(bf16[11,32,128]{2,1,0:T(8,128)(2,1)S(1)} %collective-permute-done.22), channel_id=1, source_target_pairs={{0,1},{1,0},{2,3},{3,2},{4,5},{5,4},{6,7},{7,6},{8,9},{9,8},{10,11... | collective-permute-start | bytes 270344 | tf_op jit(solution)/shard_map/ppermute | solution.py:116
  78.8 6.7 %collective-permute-start.28 = (bf16[15,32,128]{2,1,0:T(8,128)(2,1)S(1)}, bf16[15,32,128]{2,1,0:T(8,128)(2,1)S(1)}, u32[]{:S(2)}, u32[]{:S(2)}) collective-permute-start(bf16[15,32,128]{2,1,0:T(8,128)(2,1)S(1)} %get-tuple-element.71.mine_ref.s_ref), channel_id=1, source_target_pairs={{0,8},{8,0},{16,24},{24,16},{1,9},{9,1},{17,25},{25,17},{2,10},{10... | collective-permute-start | bytes 368648 | tf_op jit(solution)/shard_map/ppermute | solution.py:116
  80.2 7.9 %collective-permute-start.29 = (bf16[15,32,128]{2,1,0:T(8,128)(2,1)S(1)}, bf16[15,32,128]{2,1,0:T(8,128)(2,1)S(1)}, u32[]{:S(2)}, u32[]{:S(2)}) collective-permute-start(bf16[15,32,128]{2,1,0:T(8,128)(2,1)S(1)} %get-tuple-element.71.mine_ref.s_ref), channel_id=1, source_target_pairs={{0,16},{8,24},{16,0},{24,8},{1,17},{9,25},{17,1},{25,9},{2,18},{10... | collective-permute-start | bytes 368648 | tf_op jit(solution)/shard_map/ppermute | solution.py:116
  81.1 7.0 %collective-permute-start.30 = (bf16[15,32,128]{2,1,0:T(8,128)(2,1)S(1)}, bf16[15,32,128]{2,1,0:T(8,128)(2,1)S(1)}, u32[]{:S(2)}, u32[]{:S(2)}) collective-permute-start(bf16[15,32,128]{2,1,0:T(8,128)(2,1)S(1)} %get-tuple-element.71.mine_ref.s_ref), channel_id=1, source_target_pairs={{0,24},{8,16},{16,8},{24,0},{1,25},{9,17},{17,9},{25,1},{2,26},{10... | collective-permute-start | bytes 368648 | tf_op jit(solution)/shard_map/ppermute | solution.py:116
  92.3 10.0 %collective-permute-start.31 = (bf16[11,32,128]{2,1,0:T(8,128)(2,1)S(1)}, bf16[11,32,128]{2,1,0:T(8,128)(2,1)S(1)}, u32[]{:S(2)}, u32[]{:S(2)}) collective-permute-start(bf16[11,32,128]{2,1,0:T(8,128)(2,1)S(1)} %get-tuple-element.72), channel_id=1, source_target_pairs={{0,4},{1,5},{2,6},{3,7},{4,0},{5,1},{6,2},{7,3},{8,12},{9,13},{10,... | collective-permute-start | bytes 270344 | tf_op jit(solution)/shard_map/ppermute | solution.py:116
  94.4 7.9 %collective-permute-start.32 = (bf16[11,32,128]{2,1,0:T(8,128)(2,1)S(1)}, bf16[11,32,128]{2,1,0:T(8,128)(2,1)S(1)}, u32[]{:S(2)}, u32[]{:S(2)}) collective-permute-start(bf16[11,32,128]{2,1,0:T(8,128)(2,1)S(1)} %get-tuple-element.72), channel_id=1, source_target_pairs={{0,6},{1,7},{2,4},{3,5},{4,2},{5,3},{6,0},{7,1},{8,14},{9,15},{10,... | collective-permute-start | bytes 270344 | tf_op jit(solution)/shard_map/ppermute | solution.py:116
  96.4 6.5 %collective-permute-start.34 = (bf16[11,32,128]{2,1,0:T(8,128)(2,1)S(1)}, bf16[11,32,128]{2,1,0:T(8,128)(2,1)S(1)}, u32[]{:S(2)}, u32[]{:S(2)}) collective-permute-start(bf16[11,32,128]{2,1,0:T(8,128)(2,1)S(1)} %get-tuple-element.72), channel_id=1, source_target_pairs={{0,2},{1,3},{2,0},{3,1},{4,6},{5,7},{6,4},{7,5},{8,10},{9,11},{10,... | collective-permute-start | bytes 270344 | tf_op jit(solution)/shard_map/ppermute | solution.py:116
  102.2 1.3 %collective-permute-start.36 = (bf16[11,32,128]{2,1,0:T(8,128)(2,1)S(1)}, bf16[11,32,128]{2,1,0:T(8,128)(2,1)S(1)}, u32[]{:S(2)}, u32[]{:S(2)}) collective-permute-start(bf16[11,32,128]{2,1,0:T(8,128)(2,1)S(1)} %collective-permute-done.31), channel_id=1, source_target_pairs={{0,1},{1,0},{2,3},{3,2},{4,5},{5,4},{6,7},{7,6},{8,9},{9,8},{10,11... | collective-permute-start | bytes 270344 | tf_op jit(solution)/shard_map/ppermute | solution.py:116
  102.3 1.4 %collective-permute-start.37 = (bf16[11,32,128]{2,1,0:T(8,128)(2,1)S(1)}, bf16[11,32,128]{2,1,0:T(8,128)(2,1)S(1)}, u32[]{:S(2)}, u32[]{:S(2)}) collective-permute-start(bf16[11,32,128]{2,1,0:T(8,128)(2,1)S(1)} %collective-permute-done.32), channel_id=1, source_target_pairs={{0,1},{1,0},{2,3},{3,2},{4,5},{5,4},{6,7},{7,6},{8,9},{9,8},{10,11... | collective-permute-start | bytes 270344 | tf_op jit(solution)/shard_map/ppermute | solution.py:116
  102.8 1.3 %collective-permute-start.33 = (bf16[11,32,128]{2,1,0:T(8,128)(2,1)S(1)}, bf16[11,32,128]{2,1,0:T(8,128)(2,1)S(1)}, u32[]{:S(2)}, u32[]{:S(2)}) collective-permute-start(bf16[11,32,128]{2,1,0:T(8,128)(2,1)S(1)} %get-tuple-element.72), channel_id=1, source_target_pairs={{0,1},{1,0},{2,3},{3,2},{4,5},{5,4},{6,7},{7,6},{8,9},{9,8},{10,11... | collective-permute-start | bytes 270344 | tf_op jit(solution)/shard_map/ppermute | solution.py:116
  102.9 1.4 %collective-permute-start.35 = (bf16[11,32,128]{2,1,0:T(8,128)(2,1)S(1)}, bf16[11,32,128]{2,1,0:T(8,128)(2,1)S(1)}, u32[]{:S(2)}, u32[]{:S(2)}) collective-permute-start(bf16[11,32,128]{2,1,0:T(8,128)(2,1)S(1)} %collective-permute-done.34), channel_id=1, source_target_pairs={{0,1},{1,0},{2,3},{3,2},{4,5},{5,4},{6,7},{7,6},{8,9},{9,8},{10,11... | collective-permute-start | bytes 270344 | tf_op jit(solution)/shard_map/ppermute | solution.py:116
  105.0 6.3 %collective-permute-start.38 = (bf16[15,32,128]{2,1,0:T(8,128)(2,1)S(1)}, bf16[15,32,128]{2,1,0:T(8,128)(2,1)S(1)}, u32[]{:S(2)}, u32[]{:S(2)}) collective-permute-start(bf16[15,32,128]{2,1,0:T(8,128)(2,1)S(1)} %get-tuple-element.85.s_ref), channel_id=1, source_target_pairs={{0,8},{8,0},{16,24},{24,16},{1,9},{9,1},{17,25},{25,17},{2,10},{10... | collective-permute-start | bytes 368648 | tf_op jit(solution)/shard_map/ppermute | solution.py:116
  105.8 5.9 %collective-permute-start.39 = (bf16[15,32,128]{2,1,0:T(8,128)(2,1)S(1)}, bf16[15,32,128]{2,1,0:T(8,128)(2,1)S(1)}, u32[]{:S(2)}, u32[]{:S(2)}) collective-permute-start(bf16[15,32,128]{2,1,0:T(8,128)(2,1)S(1)} %get-tuple-element.85.s_ref), channel_id=1, source_target_pairs={{0,16},{8,24},{16,0},{24,8},{1,17},{9,25},{17,1},{25,9},{2,18},{10... | collective-permute-start | bytes 368648 | tf_op jit(solution)/shard_map/ppermute | solution.py:116
  106.8 6.9 %collective-permute-start.40 = (bf16[15,32,128]{2,1,0:T(8,128)(2,1)S(1)}, bf16[15,32,128]{2,1,0:T(8,128)(2,1)S(1)}, u32[]{:S(2)}, u32[]{:S(2)}) collective-permute-start(bf16[15,32,128]{2,1,0:T(8,128)(2,1)S(1)} %get-tuple-element.85.s_ref), channel_id=1, source_target_pairs={{0,24},{8,16},{16,8},{24,0},{1,25},{9,17},{17,9},{25,1},{2,26},{10... | collective-permute-start | bytes 368648 | tf_op jit(solution)/shard_map/ppermute | solution.py:116
